TPU v7x, 256 devices: a whole 4x4x8 slice. The times are simulated.
256 devices in a mesh: alpha: 16 (over y_hi, x, core), beta: 16 (over y_lo, z).
Axes of the slice: x: 4, y: 4 (y_hi: 2, y_lo: 2; y = y_hi * 2 + y_lo), z: 8, core: 2. Of those that a mesh axis runs over, the one named last changes fastest.
Arguments:
- coefficients: bfloat16 [8192, 16384], P('alpha', 'beta'), may hold values from -6 to 6
- couplings: bfloat16 [8, 256, 256], replicated, may hold values from -0.375 to 0.375
- exc_list: int32 [16, 16, 3], replicated, may hold values from 0 to 31, as said below
- counts: int32 [16, 16], replicated, may hold values from 0 to 1, as said below
- beta_tiles: bfloat16 [4, 1024, 16384], P(None, None, 'beta'), may hold values from -0.09375 to 0.09375
Outputs:
- sigma_vector: float32 [8192, 16384], P('alpha', 'beta')
Inputs may be any that keep to these rules, and one draw needn't show every extreme that they name: `exc_list`: entry [s, p] describes the slot from alpha device s to alpha device p: field 0 is a source block held by device s (from s * 2 to s * 2 + 1), field 1 a target block held by device p (from p * 2 to p * 2 + 1), field 2 a coupling index below 8. `counts`: 1 where a slot is live, 0 where it is empty; in every draw some device p has a live slot from every device s.
All inputs are finite; a program needn't handle non-finite values.
Results may differ from a plain program's by a relative error of at most 0.0029.
Values may be sent and summed in bfloat16 or wider, within the bound.
No kernel may reach another device: no remote copies, remote signals or barrier semaphores. Data moves between devices by JAX's collectives and lax.ppermute only.
A program may use at most 192 MiB of HBM per device.

v0:
```python
import jax
import jax.numpy as jnp
from jax import lax
from jax.sharding import PartitionSpec as P

AB = 256
ABLK = 2
STOPS = 4


def exchange_in_groups(shard, axis, split_dim, concat_dim, work, item_dim, out_dim):
    items = jax.tree.leaves(shard)[0].shape[item_dim]
    count = 2 if items % 2 == 0 else 1
    finished = []
    for k in range(count):
        group = jax.tree.map(
            lambda a: lax.slice_in_dim(
                a, k * (items // count), (k + 1) * (items // count), axis=item_dim
            ),
            shard,
        )
        finished.append(
            work(
                lax.all_to_all(
                    group, axis, split_axis=split_dim, concat_axis=concat_dim, tiled=True
                )
            )
        )
    return jax.tree.map(lambda *parts: jnp.concatenate(parts, axis=out_dim), *finished)


def shifted(block, axis, distance):
    devices = range(lax.axis_size(axis))
    route = [((i - distance) % len(devices), i) for i in devices]
    return lax.ppermute(block, axis, route)


def per_device(coefficients, couplings, exc_list, counts, beta_tiles):
    own_index = lax.axis_index("alpha")
    columns = coefficients.shape[1]
    blocks = coefficients.reshape(ABLK, AB, columns)
    incoming = exc_list[:, own_index, :]
    incoming_live = counts[:, own_index] == 1
    block_range = jnp.arange(ABLK, dtype=jnp.int32)

    def contribute(pieces, is_live, target_block, coupling_index):
        scaled = couplings[coupling_index] * is_live.astype(jnp.bfloat16)[:, None, None]
        partial_value = jnp.einsum(
            "sij,sjc->sic", scaled, pieces, preferred_element_type=jnp.float32
        )
        selector = (
            (target_block[None, :] - own_index * ABLK == block_range[:, None]) & is_live[None, :]
        ).astype(jnp.float32)
        return jnp.einsum("ts,sic->tic", selector, partial_value, precision=lax.Precision.HIGHEST)

    source_local = jnp.clip(exc_list[own_index, :, 0] - own_index * ABLK, 0, ABLK - 1)
    outgoing = blocks[source_local]

    def receive(arrived):
        return contribute(arrived, incoming_live, incoming[:, 1], incoming[:, 2])

    interm = exchange_in_groups(outgoing, "alpha", 0, 0, receive, 2, 2)
    local_rows = interm.astype(jnp.bfloat16).reshape(ABLK * AB, columns)
    summed_out = jnp.dot(local_rows, beta_tiles[0], preferred_element_type=jnp.float32)
    moving = local_rows
    for offset in range(1, STOPS):
        moving = shifted(moving, "beta", 1)
        summed_out = summed_out + jnp.dot(
            moving, beta_tiles[offset], preferred_element_type=jnp.float32
        )
    return summed_out


def solution(mesh):
    placed = (P("alpha", "beta"), P(), P(), P(), P(None, None, "beta"))
    return jax.shard_map(
        per_device, mesh=mesh, in_specs=placed, out_specs=P("alpha", "beta"), check_vma=False
    )
```

profile of v0, /device:TPU:8, one launch (start us, length us, event | category | flops | bytes accessed | tf_op | source)
XLA Modules:
  0.0 224.1 jit_solution(3679983993629709992)
XLA Ops:
  0.0 0.0 copy-start
  0.0 0.8 fusion.38
  0.8 0.4 copy-done
  1.2 4.7 %gather_fusion.1 = bf16[16,256,1024]{2,1,0:T(8,128)(2,1)} fusion(bf16[2,256,1024]{2,1,0:T(8,128)(2,1)S(1)} %bitcast.35, s32[1024]{0:T(1024)S(1)} %pad_clamp_fusion), kind=kCustom, calls=%fused_computation.1 | custom fusion | bytes 16777280 | tf_op jit(solution)/shard_map/gather | solution.py:57
  5.9 5.1 %fusion.41 = (bf16[16,256,512]{2,1,0:T(8,128)(2,1)}, bf16[16,256,512]{2,1,0:T(8,128)(2,1)S(1)}) fusion(bf16[16,256,1024]{2,1,0:T(8,128)(2,1)} %gather_fusion.1), kind=kLoop, calls=%fused_computation.48 | loop fusion | bytes 16777216 | tf_op jit(solution)/shard_map/slice | solution.py:17
  11.0 57.7 %all_to_all.10 = bf16[16,256,512]{2,1,0:T(8,128)(2,1)} all-to-all(bf16[16,256,512]{2,1,0:T(8,128)(2,1)S(1)} %get-tuple-element.6), channel_id=1, replica_groups=mesh['alpha'=16,'beta'=16] {'alpha'}, dimensions={0} | all-to-all | bytes 8388608 | tf_op jit(solution)/shard_map/all_to_all | solution.py:24
  68.7 0.0 copy-start.4
  68.7 0.0 copy-start.3
  68.7 0.0 copy-start.2
  68.7 4.7 %all-to-all-start = ((bf16[16,256,512]{2,1,0:T(8,128)(2,1)}), bf16[16,256,512]{2,1,0:T(8,128)(2,1)}, u32[]{:S(2)}, u32[]{:S(2)}) async-start(bf16[16,256,512]{2,1,0:T(8,128)(2,1)} %get-tuple-element.5), calls=%async_computation | async-start | bytes 8388608 | tf_op jit(solution)/shard_map/all_to_all | solution.py:24
  73.4 0.0 copy-done.4
  73.4 0.2 fusion.30
  73.6 0.0 copy-done.3
  73.6 0.2 dynamic-slice_reduce_fusion
  73.9 0.0 copy-done.2
  73.9 0.7 gather_fusion
  74.6 3.5 %fusion.16 = f32[16,256,512]{2,1,0:T(8,128)S(1)} fusion(bf16[16,256,512]{2,1,0:T(8,128)(2,1)} %all_to_all.10, bf16[16,256,256]{2,1,0:T(8,128)(2,1)S(1)} %gather_fusion, bf16[16]{0:T(256)(128)(2,1)S(1)} %convert_element_type.12), kind=kOutput, calls=%fused_computation.19 | convolution fusion | flops 1074790400 | bytes 14680096 | tf_op jit(solution)/shard_map/sij,sjc->sic/dot_general | solution.py:48
  78.0 6.3 %fusion.25 = bf16[2,256,512]{2,0,1:T(2,128)(2,1)S(1)} fusion(f32[16,256,512]{2,1,0:T(8,128)S(1)} %fusion.16, pred[16]{0:T(512)(128)(4,1)S(1)} %fusion.30, s32[16]{0:T(128)S(1)} %get-tuple-element.7), kind=kOutput, calls=%fused_computation.24 | convolution fusion | flops 50593856 | bytes 8912976 | tf_op jit(solution)/shard_map/ts,sic->tic/dot_general | solution.py:54
  84.4 0.1 copy.7
  84.4 45.2 %all-to-all-done = bf16[16,256,512]{2,1,0:T(8,128)(2,1)} async-done(((bf16[16,256,512]{2,1,0:T(8,128)(2,1)}), bf16[16,256,512]{2,1,0:T(8,128)(2,1)}, u32[]{:S(2)}, u32[]{:S(2)}) %all-to-all-start) | async-done | bytes 4194336 | tf_op jit(solution)/shard_map/all_to_all | solution.py:24
  129.6 3.5 %fusion.18 = f32[16,256,512]{2,1,0:T(8,128)S(1)} fusion(bf16[16,256,512]{2,1,0:T(8,128)(2,1)} %all-to-all-done, bf16[16,256,256]{2,1,0:T(8,128)(2,1)S(1)} %gather_fusion, bf16[16]{0:T(256)(128)(2,1)S(1)} %convert_element_type.12), kind=kOutput, calls=%fused_computation.21 | convolution fusion | flops 1074790400 | bytes 14680096 | tf_op jit(solution)/shard_map/sij,sjc->sic/dot_general | solution.py:48
  133.1 0.0 slice-start
  133.1 6.3 %fusion.22 = bf16[2,256,512]{2,0,1:T(2,128)(2,1)S(1)} fusion(f32[16,256,512]{2,1,0:T(8,128)S(1)} %fusion.18, pred[16]{0:T(512)(128)(4,1)S(1)} %fusion.30, s32[16]{0:T(128)S(1)} %get-tuple-element.7), kind=kOutput, calls=%fused_computation.23 | convolution fusion | flops 50593856 | bytes 8912976 | tf_op jit(solution)/shard_map/ts,sic->tic/dot_general | solution.py:54
  139.4 0.1 copy.6
  139.5 0.0 slice-start.1
  139.5 0.1 pad_maximum_fusion
  139.6 2.0 collective-permute-start
  141.6 27.9 %collective-permute-done = bf16[512,1024]{1,0:T(8,128)(2,1)S(1)} collective-permute-done((bf16[512,1024]{1,0:T(8,128)(2,1)S(1)}, bf16[512,1024]{1,0:T(8,128)(2,1)S(1)}, u32[]{:S(2)}, u32[]{:S(2)}) %collective-permute-start) | collective-permute-done | bytes 1048608 | tf_op jit(solution)/shard_map/ppermute | solution.py:35
  169.5 0.0 collective-permute-start.1
  169.5 26.4 %collective-permute-done.1 = bf16[512,1024]{1,0:T(8,128)(2,1)S(1)} collective-permute-done((bf16[512,1024]{1,0:T(8,128)(2,1)S(1)}, bf16[512,1024]{1,0:T(8,128)(2,1)S(1)}, u32[]{:S(2)}, u32[]{:S(2)}) %collective-permute-start.1) | collective-permute-done | bytes 1048608 | tf_op jit(solution)/shard_map/ppermute | solution.py:35
  195.9 0.0 collective-permute-start.2
  195.9 2.8 %fusion.10 = f32[512,1024]{1,0:T(8,128)S(1)} fusion(bf16[4,1024,1024]{2,1,0:T(8,128)(2,1)} %param.9, bf16[512,512]{1,0:T(8,128)(2,1)S(1)} %bitcast.37, bf16[512,512]{1,0:T(8,128)(2,1)S(1)} %bitcast.39), kind=kOutput, calls=%fused_computation.12 | convolution fusion | flops 1075838976 | bytes 5242880 | tf_op jit(solution)/shard_map/dot_general | solution.py:64
  198.8 0.0 slice-done
  198.8 0.0 slice-done.1
  198.8 1.3 fusion.8
  200.1 1.3 fusion.6
  201.3 20.1 %collective-permute-done.2 = bf16[512,1024]{1,0:T(8,128)(2,1)S(1)} collective-permute-done((bf16[512,1024]{1,0:T(8,128)(2,1)S(1)}, bf16[512,1024]{1,0:T(8,128)(2,1)S(1)}, u32[]{:S(2)}, u32[]{:S(2)}) %collective-permute-start.2) | collective-permute-done | bytes 1048608 | tf_op jit(solution)/shard_map/ppermute | solution.py:35
  221.4 0.0 copy-start.1
  221.4 2.7 %add_add_fusion = f32[512,1024]{1,0:T(8,128)} fusion(f32[512,1024]{1,0:T(8,128)S(1)} %fusion.6, f32[512,1024]{1,0:T(8,128)S(1)} %fusion.10, f32[512,1024]{1,0:T(8,128)S(1)} %fusion.8, bf16[512,1024]{1,0:T(8,128)(2,1)S(1)} %collective-permute-done.2, bf16[4,1024,1024]{2,1,0:T(8,128)(2,1)S(1)} %bitcast.41), kind=kOutput, calls=%fused_computation.15 | convolution fusion | flops 1075314688 | bytes 11534336 | tf_op jit(solution)/shard_map/dot_general | solution.py:68
  224.1 0.0 copy-done.1
  (5 shorter events, 0.0 us)
Async XLA Ops:
  0.0 1.2 copy-start
  68.7 4.7 %copy-start.4 = (s32[16,16]{1,0:T(8,128)S(1)}, s32[16,16]{1,0:T(8,128)}, u32[]{:S(2)}) copy-start(s32[16,16]{1,0:T(8,128)} %param.8) | copy-start | bytes 3076
  68.7 4.9 %copy-start.3 = (s32[16,16,3]{1,0,2:T(8,128)S(1)}, s32[16,16,3]{1,0,2:T(8,128)}, u32[]{:S(2)}) copy-start(s32[16,16,3]{1,0,2:T(8,128)} %param.7) | copy-start | bytes 9220
  68.7 5.2 %copy-start.2 = (bf16[8,256,256]{2,1,0:T(8,128)(2,1)S(1)}, bf16[8,256,256]{2,1,0:T(8,128)(2,1)}, u32[]{:S(2)}) copy-start(bf16[8,256,256]{2,1,0:T(8,128)(2,1)} %param.6) | copy-start | bytes 3145732
  68.7 60.9 %all-to-all-start = ((bf16[16,256,512]{2,1,0:T(8,128)(2,1)}), bf16[16,256,512]{2,1,0:T(8,128)(2,1)}, u32[]{:S(2)}, u32[]{:S(2)}) async-start(bf16[16,256,512]{2,1,0:T(8,128)(2,1)} %get-tuple-element.5), calls=%async_computation | async-start | bytes 8388608 | tf_op jit(solution)/shard_map/all_to_all | solution.py:24
  133.1 65.7 %slice-start = ((s8[8388608]{0:T(1024)(128)(4,1)}), s8[4194304]{0:T(1024)(128)(4,1)S(1)}, s32[]{:S(2)}) async-start(s8[8388608]{0:T(1024)(128)(4,1)} %bitcast.40), calls=%async_computation.2 | async-start | bytes 8388608
  139.5 59.3 %slice-start.1 = ((s8[8388608]{0:T(1024)(128)(4,1)}), s8[4194304]{0:T(1024)(128)(4,1)S(1)}, s32[]{:S(2)}) async-start(s8[8388608]{0:T(1024)(128)(4,1)} %bitcast.40), calls=%async_computation.3 | async-start | bytes 8388608
  139.6 29.9 %collective-permute-start = (bf16[512,1024]{1,0:T(8,128)(2,1)S(1)}, bf16[512,1024]{1,0:T(8,128)(2,1)S(1)}, u32[]{:S(2)}, u32[]{:S(2)}) collective-permute-start(bf16[512,1024]{1,0:T(8,128)(2,1)S(1)} %pad_maximum_fusion), channel_id=1, source_target_pairs={{15,0},{0,1},{1,2},{2,3},{3,4},{4,5},{5,6},{6,7},{7,8},{8,9},{9,10... | collective-permute-start | bytes 3145736 | tf_op jit(solution)/shard_map/ppermute | solution.py:35
  169.5 26.4 %collective-permute-start.1 = (bf16[512,1024]{1,0:T(8,128)(2,1)S(1)}, bf16[512,1024]{1,0:T(8,128)(2,1)S(1)}, u32[]{:S(2)}, u32[]{:S(2)}) collective-permute-start(bf16[512,1024]{1,0:T(8,128)(2,1)S(1)} %collective-permute-done), channel_id=1, source_target_pairs={{15,0},{0,1},{1,2},{2,3},{3,4},{4,5},{5,6},{6,7},{7,8},{8,9},{9,10... | collective-permute-start | bytes 3145736 | tf_op jit(solution)/shard_map/ppermute | solution.py:35
  195.9 25.5 %collective-permute-start.2 = (bf16[512,1024]{1,0:T(8,128)(2,1)S(1)}, bf16[512,1024]{1,0:T(8,128)(2,1)S(1)}, u32[]{:S(2)}, u32[]{:S(2)}) collective-permute-start(bf16[512,1024]{1,0:T(8,128)(2,1)S(1)} %collective-permute-done.1), channel_id=1, source_target_pairs={{15,0},{0,1},{1,2},{2,3},{3,4},{4,5},{5,6},{6,7},{7,8},{8,9},{9,10... | collective-permute-start | bytes 3145736 | tf_op jit(solution)/shard_map/ppermute | solution.py:35
  221.4 2.7 %copy-start.1 = (bf16[512,1024]{1,0:T(8,128)(2,1)S(1)}, bf16[512,1024]{1,0:T(8,128)(2,1)}, u32[]{:S(2)}) copy-start(bf16[512,1024]{1,0:T(8,128)(2,1)} %param.5) | copy-start | bytes 3145732
where the time goes:
time: 226 us; the launch traced here: 224 us
  waiting for transfers between devices  120 us (53%)
  blocking collectives  57.7 us (26%)
  matrix products  27.6 us (12%)
  local copies, waits for them, and re-layouts  11.2 us (5%)
  starting transfers between devices  6.69 us (3%)
    ppermute x3, waiting for transfers between devices, shifted(): return lax.ppermute(block, axis, route)  74.4 us
    all_to_all x1, blocking collectives, exchange_in_groups(): lax.all_to_all(group, axis, split_axis=split_dim, concat_axis=concat_dim,...  57.7 us
    all_to_all x1, waiting for transfers between devices, exchange_in_groups(): lax.all_to_all(group, axis, split_axis=split_dim, concat_axis=concat_dim,...  45.2 us
    dot_general x2, matrix products, contribute(): jnp.einsum('ts,sic->tic', selector, partial_value, precision=lax.Precisio...  12.6 us
    dot_general x2, matrix products, contribute(): jnp.einsum('sij,sjc->sic', scaled, pieces, preferred_element_type=jnp.flo...  6.96 us
    dot_general x3, matrix products, per_device(): jnp.dot(moving, beta_tiles[offset], preferred_element_type=jnp.float32)  5.18 us
    slice x1, local copies, waits for them, and re-layouts, exchange_in_groups(): lax.slice_in_dim(a, k * (items // count), (k + 1) * (items // count), axi...  5.08 us
    all_to_all x1, starting transfers between devices, exchange_in_groups(): lax.all_to_all(group, axis, split_axis=split_dim, concat_axis=concat_dim,...  4.68 us
  transfers between devices with their start and end apart: 4, of which 4 were waited for; matrix products, arithmetic and copies ran while one was open for 7% of the time, Pallas kernels for 0%

commit v1 on v0

v1 whole, which is shorter than its diff:
```python
import functools

import jax
import jax.numpy as jnp
from jax import lax
from jax.experimental import pallas as pl
from jax.experimental.pallas import tpu as pltpu
from jax.sharding import PartitionSpec as P

AB = 256
ABLK = 2
STOPS = 4
NX = 4
NZ = 8
ROWS = ABLK * AB
EARLY = 128
CHUNKS = (128, 256, 256, 256)
ROW_TILE = 128

VMEM = pl.BlockSpec(memory_space=pltpu.VMEM)
SMEM = pl.BlockSpec(memory_space=pltpu.SMEM)


def device_of(y, x, core):
    return (y * NX + x) * 2 + core


def alpha_route(move):
    route = []
    for y in range(2):
        for x in range(NX):
            for core in range(2):
                to = move(y, x, core)
                route.append((device_of(y, x, core), device_of(*to)))
    return route


def to_x(step):
    return alpha_route(lambda y, x, core: (y, (x + step) % NX, core))


SWAP_CORE = alpha_route(lambda y, x, core: (y, x, 1 - core))
SWAP_Y = alpha_route(lambda y, x, core: (1 - y, x, core))
RING = [(i, (i + 1) % (2 * NZ)) for i in range(2 * NZ)]
COLUMN = [(y * NZ + z, y * NZ + (z + 1) % NZ) for y in range(2) for z in range(NZ)]
CROSS = [(NZ - 1, 2 * NZ - 1), (2 * NZ - 1, NZ - 1)]


def after(value, *earlier):
    return lax.optimization_barrier((value, *earlier))[0]


def slot_codes(exc_list, counts):
    me = lax.axis_index("alpha")
    y = me // (2 * NX)
    mates = 2 * NX
    exc = lax.dynamic_slice_in_dim(exc_list, y * mates, mates, 0)
    live = lax.dynamic_slice_in_dim(counts, y * mates, mates, 0) == 1
    codes = []
    for target in (me, (me + mates) % (2 * mates)):
        entry = lax.dynamic_index_in_dim(exc, target, 1, keepdims=False)
        used = lax.dynamic_index_in_dim(live, target, 1, keepdims=False)
        source = entry[:, 0] - (y * mates + jnp.arange(mates, dtype=jnp.int32)) * ABLK
        goal = entry[:, 1] - target * ABLK
        codes.append(jnp.where(used, (entry[:, 2] * 2 + goal) * 2 + source, -1))
    return jnp.concatenate(codes)


def couple_kernel(which, codes, coup, mine, sib, out, *scratch):
    me = lax.axis_index("alpha")
    x, core = (me // 2) % NX, me % 2
    total = scratch[0] if scratch else out
    total[...] = jnp.zeros_like(total)
    for stack, side in ((mine, core), (sib, 1 - core)):

        @pl.loop(0, NX)
        def _(step):
            code = codes[which * 2 * NX + lax.rem(x + step, NX) * 2 + side]

            @pl.when(code >= 0)
            def _():
                kind, goal, source = code // 4, (code // 2) % 2, code % 2
                rows = pl.ds(pl.multiple_of(goal * AB, AB), AB)
                block = stack[pl.ds(pl.multiple_of(step * ROWS + source * AB, AB), AB), :]
                total[rows, :] += jnp.dot(coup[kind], block, preferred_element_type=jnp.float32)

    if scratch:
        out[...] = total[...].astype(out.dtype)


def couple(which, codes, couplings, mine, sib):
    cols = mine.shape[1]
    kind = jnp.float32 if which == 0 else jnp.bfloat16
    return pl.pallas_call(
        functools.partial(couple_kernel, which),
        in_specs=[SMEM] + [VMEM] * 3,
        out_specs=VMEM,
        scratch_shapes=[] if which == 0 else [pltpu.VMEM((ROWS, cols), jnp.float32)],
        out_shape=jax.ShapeDtypeStruct((ROWS, cols), kind),
        cost_estimate=pl.CostEstimate(
            flops=16 * AB * AB * cols, bytes_accessed=10 * ROWS * cols * 2, transcendentals=0
        ),
        compiler_params=pltpu.CompilerParams(vmem_limit_bytes=8 << 20),
    )(codes, couplings, mine, sib)


def band_kernel(places, first, *refs):
    n = len(places)
    blocks, tiles = refs[:n], refs[n]
    before, out = (None, refs[n + 1]) if first else refs[n + 1 :]

    @pl.loop(0, ROWS, step=ROW_TILE)
    def _(row):
        rows = pl.ds(pl.multiple_of(row, ROW_TILE), ROW_TILE)
        for k, (shift, start, width, lane) in enumerate(places):
            part = jnp.dot(
                blocks[k][rows, lane : lane + width],
                tiles[shift, start : start + width, :],
                preferred_element_type=jnp.float32,
            )
            if k > 0:
                out[rows, :] += part
            elif first:
                out[rows, :] = part
            else:
                out[rows, :] = before[rows, :] + part


def band(total, tiles, blocks, places):
    first = total is None
    cols = tiles.shape[2]
    flops = sum(2 * ROWS * p[2] * cols for p in places)
    arrays = list(blocks) + [tiles] + ([] if first else [total])
    return pl.pallas_call(
        functools.partial(band_kernel, tuple(places), first),
        in_specs=[VMEM] * len(arrays),
        out_specs=VMEM,
        out_shape=jax.ShapeDtypeStruct((ROWS, cols), jnp.float32),
        input_output_aliases={} if first else {len(arrays) - 1: 0},
        cost_estimate=pl.CostEstimate(flops=flops, bytes_accessed=4 << 20, transcendentals=0),
        compiler_params=pltpu.CompilerParams(vmem_limit_bytes=8 << 20),
    )(*arrays)


def per_device(coefficients, couplings, exc_list, counts, beta_tiles):
    corner = lax.axis_index("beta") % NZ == NZ - 1
    codes = slot_codes(exc_list, counts)

    def spread(own):
        return [own] + [lax.ppermute(own, "alpha", to_x(s)) for s in (-1, 2, 1)]

    def ring(block):
        crossed = lax.ppermute(block, "beta", CROSS)
        one = lax.ppermute(jnp.where(corner, crossed, block), "beta", COLUMN)
        two = lax.ppermute(one, "beta", RING)
        return [block, one, two, lax.ppermute(two, "beta", RING)]

    early = [coefficients[:, :EARLY]]
    for _ in range(STOPS - 1):
        early.append(lax.ppermute(early[-1], "beta", RING))
    starts = [EARLY + sum(CHUNKS[:k]) for k in range(len(CHUNKS))]
    owns = [coefficients[:, s : s + w] for s, w in zip(starts, CHUNKS)] + [jnp.concatenate(early, axis=1)]

    count = len(owns)
    spreads = [spread(owns[0]), spread(owns[1])] + [None] * (count - 2)
    outs = []
    total = None
    for k in range(count):
        mine = jnp.concatenate(spreads[k], axis=0)
        sib = lax.ppermute(mine, "alpha", SWAP_CORE)
        if k > 0:
            sib = after(sib, outs[k - 1][0])
        away = couple(1, codes, couplings, mine, sib)
        back = lax.ppermute(away, "alpha", SWAP_Y)
        if k + 2 < count:
            spreads[k + 2] = spread(after(owns[k + 2], away))
        near = couple(0, codes, couplings, mine, sib)
        done = (near + back.astype(jnp.float32)).astype(jnp.bfloat16)
        outs.append(ring(done) if k < count - 1 else [done])
    for k, width in enumerate(CHUNKS):
        places = [(d, starts[k], width, 0) for d in range(STOPS)]
        if k < len(CHUNKS) - 1:
            total = band(total, beta_tiles, outs[k], places)
        else:
            total = band(total, beta_tiles, outs[k][:-1], places[:-1])
            last = outs[k][-1:], places[-1:]
    total = band(total, beta_tiles, outs[-1] * STOPS, [(d, 0, EARLY, d * EARLY) for d in range(STOPS)])
    return band(total, beta_tiles, *last)


def solution(mesh):
    placed = (P("alpha", "beta"), P(), P(), P(), P(None, None, "beta"))
    return jax.shard_map(
        per_device, mesh=mesh, in_specs=placed, out_specs=P("alpha", "beta"), check_vma=False
    )
```

time: 226 us -> 202 us (0.89)
  blocking collectives: 57.7 us -> 0 us
  Pallas kernels: 0 us -> 41.9 us
  starting transfers between devices: 6.69 us -> 44.8 us
  matrix products: 27.6 us -> 0 us
  waiting for transfers between devices: 120 us -> 103 us
  local copies, waits for them, and re-layouts: 11.2 us -> 7.24 us
    all_to_all x1 -> x0, blocking collectives: 57.7 us -> none  [exchange_in_groups(): lax.all_to_all(group, axis, split_axis=split_dim, concat_axis=concat_dim,...]
    all_to_all x1 -> x0, waiting for transfers between devices: 45.2 us -> none  [exchange_in_groups(): lax.all_to_all(group, axis, split_axis=split_dim, concat_axis=concat_dim,...]
    ppermute x3 -> x44, starting transfers between devices: 2 us -> 44.8 us  [the longest x15 21.6 us: spread(): return [own] + [lax.ppermute(own, 'alpha', to_x(s)) for s in (-1, 2, 1)]]
    pallas_call x0 -> x16, Pallas kernels: none -> 41.9 us  [the longest x6 25.6 us: band(): pl.pallas_call(functools.partial(band_kernel, tuple(places), first), in_s...]
    ppermute x3 -> x44, waiting for transfers between devices: 74.4 us -> 103 us  [the longest x15 46.1 us: spread(): return [own] + [lax.ppermute(own, 'alpha', to_x(s)) for s in (-1, 2, 1)]]
    dot_general x8 -> x0, matrix products: 27.6 us -> none  [the longest x2 12.6 us: contribute(): jnp.einsum('ts,sic->tic', selector, partial_value, precision=lax.Precisio...]
    gather x2 -> x0, local copies, waits for them, and re-layouts: 5.34 us -> none  [the longest x1 4.66 us: per_device(): outgoing = blocks[source_local]]
    all_to_all x1 -> x0, starting transfers between devices: 4.68 us -> none  [exchange_in_groups(): lax.all_to_all(group, axis, split_axis=split_dim, concat_axis=concat_dim,...]
  transfers between devices with their start and end apart: 4 -> 44, of which waited for: 4 -> 23; matrix products, arithmetic and copies ran while one was open for 7% -> 3% of each run, Pallas kernels for 0% -> 19%
where the time goes in v1:
time: 202 us; the launch traced here: 200 us
  waiting for transfers between devices  103 us (51%)
  starting transfers between devices  44.8 us (22%)
  Pallas kernels  41.9 us (21%)
  local copies, waits for them, and re-layouts  7.24 us (4%)
  other arithmetic  2.72 us (1%)
    ppermute x15, waiting for transfers between devices, spread(): return [own] + [lax.ppermute(own, 'alpha', to_x(s)) for s in (-1, 2, 1)]  46.1 us
    pallas_call x6, Pallas kernels, band(): pl.pallas_call(functools.partial(band_kernel, tuple(places), first), in_s...  25.6 us
    ppermute x15, starting transfers between devices, spread(): return [own] + [lax.ppermute(own, 'alpha', to_x(s)) for s in (-1, 2, 1)]  21.6 us
    pallas_call x10, Pallas kernels, couple(): pl.pallas_call(functools.partial(couple_kernel, which), in_specs=[SMEM] +...  16.3 us
    ppermute x4, waiting for transfers between devices, ring(): two = lax.ppermute(one, 'beta', RING)  15.4 us
    ppermute x4, waiting for transfers between devices, ring(): one = lax.ppermute(jnp.where(corner, crossed, block), 'beta', COLUMN)  13.5 us
    ppermute x5, starting transfers between devices, per_device(): back = lax.ppermute(away, 'alpha', SWAP_Y)  12.5 us
    ppermute x5, waiting for transfers between devices, per_device(): back = lax.ppermute(away, 'alpha', SWAP_Y)  11.8 us
  transfers between devices with their start and end apart: 44, of which 23 were waited for; matrix products, arithmetic and copies ran while one was open for 3% of the time, Pallas kernels for 19%

profile of v1, /device:TPU:8, one launch (start us, length us, event | category | flops | bytes accessed | tf_op | source)
XLA Modules:
  0.0 199.6 jit_solution(8840779376787264405)
XLA Ops:
  0.0 1.1 fusion.4
  1.2 1.6 collective-permute-start.6
  2.7 2.7 %collective-permute-start.5 = (bf16[512,128]{1,0:T(8,128)(2,1)S(1)}, bf16[512,128]{1,0:T(8,128)(2,1)S(1)}, u32[]{:S(2)}, u32[]{:S(2)}) collective-permute-start(bf16[512,128]{1,0:T(8,128)(2,1)S(1)} %get-tuple-element.24), channel_id=1, source_target_pairs={{0,64},{16,80},{32,96},{48,112},{64,0},{80,16},{96,32},{112,48},{1... | collective-permute-start | bytes 393224 | tf_op jit(solution)/shard_map/ppermute | solution.py:150
  5.5 1.4 collective-permute-start.4
  6.9 1.0 collective-permute-done.6
  7.8 3.6 %collective-permute-done.5 = bf16[512,128]{1,0:T(8,128)(2,1)S(1)} collective-permute-done((bf16[512,128]{1,0:T(8,128)(2,1)S(1)}, bf16[512,128]{1,0:T(8,128)(2,1)S(1)}, u32[]{:S(2)}, u32[]{:S(2)}) %collective-permute-start.5) | collective-permute-done | bytes 131104 | tf_op jit(solution)/shard_map/ppermute | solution.py:150
  11.7 1.4 collective-permute-start.2
  13.1 2.4 %collective-permute-start.1 = (bf16[512,256]{1,0:T(8,128)(2,1)S(1)}, bf16[512,256]{1,0:T(8,128)(2,1)}, u32[]{:S(2)}, u32[]{:S(2)}) collective-permute-start(bf16[512,256]{1,0:T(8,128)(2,1)S(1)} %get-tuple-element.26), channel_id=1, source_target_pairs={{0,64},{16,80},{32,96},{48,112},{64,0},{80,16},{96,32},{112,48},{1... | collective-permute-start | bytes 786440 | tf_op jit(solution)/shard_map/ppermute | solution.py:150
  15.5 1.6 collective-permute-start
  17.7 1.1 shard_map.56
  19.3 2.4 %collective-permute-done.2 = bf16[512,256]{1,0:T(8,128)(2,1)S(1)} collective-permute-done((bf16[512,256]{1,0:T(8,128)(2,1)S(1)}, bf16[512,256]{1,0:T(8,128)(2,1)S(1)}, u32[]{:S(2)}, u32[]{:S(2)}) %collective-permute-start.2) | collective-permute-done | bytes 262176 | tf_op jit(solution)/shard_map/ppermute | solution.py:150
  21.7 6.2 %collective-permute-done.1 = bf16[512,256]{1,0:T(8,128)(2,1)} collective-permute-done((bf16[512,256]{1,0:T(8,128)(2,1)S(1)}, bf16[512,256]{1,0:T(8,128)(2,1)}, u32[]{:S(2)}, u32[]{:S(2)}) %collective-permute-start.1) | collective-permute-done | bytes 262176 | tf_op jit(solution)/shard_map/ppermute | solution.py:150
  27.9 0.9 collective-permute-done
  28.8 1.1 pad_maximum_fusion.mine
  30.0 2.7 %collective-permute-start.14 = (bf16[512,256]{1,0:T(8,128)(2,1)S(1)}, bf16[512,256]{1,0:T(8,128)(2,1)S(1)}, u32[]{:S(2)}, u32[]{:S(2)}) collective-permute-start(bf16[512,256]{1,0:T(8,128)(2,1)S(1)} %get-tuple-element.14), channel_id=1, source_target_pairs={{0,64},{16,80},{32,96},{48,112},{64,0},{80,16},{96,32},{112,48},{1... | collective-permute-start | bytes 786440 | tf_op jit(solution)/shard_map/ppermute | solution.py:150
  32.7 1.9 collective-permute-start.24
  34.9 5.8 %collective-permute-done.14 = bf16[512,256]{1,0:T(8,128)(2,1)S(1)} collective-permute-done((bf16[512,256]{1,0:T(8,128)(2,1)S(1)}, bf16[512,256]{1,0:T(8,128)(2,1)S(1)}, u32[]{:S(2)}, u32[]{:S(2)}) %collective-permute-start.14) | collective-permute-done | bytes 262176 | tf_op jit(solution)/shard_map/ppermute | solution.py:150
  40.7 5.1 %collective-permute-done.15 = bf16[512,256]{1,0:T(8,128)(2,1)S(1)} collective-permute-done((bf16[512,256]{1,0:T(8,128)(2,1)S(1)}, bf16[512,256]{1,0:T(8,128)(2,1)S(1)}, u32[]{:S(2)}, u32[]{:S(2)}) %collective-permute-start.15) | collective-permute-done | bytes 262176 | tf_op jit(solution)/shard_map/ppermute | solution.py:150
  45.9 2.0 collective-permute-start.25
  47.9 2.3 %collective-permute-start.8 = (bf16[512,128]{1,0:T(8,128)(2,1)S(1)}, bf16[512,128]{1,0:T(8,128)(2,1)S(1)}, u32[]{:S(2)}, u32[]{:S(2)}) collective-permute-start(bf16[512,128]{1,0:T(8,128)(2,1)S(1)} %shard_map.56), channel_id=1, source_target_pairs={{0,128},{16,144},{32,160},{48,176},{64,192},{80,208},{96,224},{112... | collective-permute-start | bytes 393224 | tf_op jit(solution)/shard_map/ppermute | solution.py:174
  50.2 5.7 %collective-permute-done.25 = bf16[512,128]{1,0:T(8,128)(2,1)S(1)} collective-permute-done((bf16[512,128]{1,0:T(8,128)(2,1)S(1)}, bf16[512,128]{1,0:T(8,128)(2,1)S(1)}, u32[]{:S(2)}, u32[]{:S(2)}) %collective-permute-start.25) | collective-permute-done | bytes 131104 | tf_op jit(solution)/shard_map/ppermute | solution.py:160
  55.9 1.0 shard_map.55
  57.0 0.8 collective-permute-done.8
  57.8 1.1 shard_map.57
  59.0 2.6 %collective-permute-start.17 = (bf16[512,256]{1,0:T(8,128)(2,1)S(1)}, bf16[512,256]{1,0:T(8,128)(2,1)S(1)}, u32[]{:S(2)}, u32[]{:S(2)}) collective-permute-start(bf16[512,256]{1,0:T(8,128)(2,1)S(1)} %shard_map.57), channel_id=1, source_target_pairs={{0,128},{16,144},{32,160},{48,176},{64,192},{80,208},{96,224},{112... | collective-permute-start | bytes 786440 | tf_op jit(solution)/shard_map/ppermute | solution.py:174
  61.5 1.7 collective-permute-done.26
  64.0 2.7 %collective-permute-start.10 = (bf16[512,256]{1,0:T(8,128)(2,1)S(1)}, bf16[512,256]{1,0:T(8,128)(2,1)S(1)}, u32[]{:S(2)}, u32[]{:S(2)}) collective-permute-start(bf16[512,256]{1,0:T(8,128)(2,1)S(1)} %get-tuple-element.13), channel_id=1, source_target_pairs={{0,64},{16,80},{32,96},{48,112},{64,0},{80,16},{96,32},{112,48},{1... | collective-permute-start | bytes 786440 | tf_op jit(solution)/shard_map/ppermute | solution.py:150
  66.6 1.1 shard_map.58
  67.7 2.9 %collective-permute-done.17 = bf16[512,256]{1,0:T(8,128)(2,1)S(1)} collective-permute-done((bf16[512,256]{1,0:T(8,128)(2,1)S(1)}, bf16[512,256]{1,0:T(8,128)(2,1)S(1)}, u32[]{:S(2)}, u32[]{:S(2)}) %collective-permute-start.17) | collective-permute-done | bytes 262176 | tf_op jit(solution)/shard_map/ppermute | solution.py:174
  70.8 1.9 shard_map.60
  72.6 1.2 collective-permute-start.27
  74.6 2.4 %collective-permute-start.28 = (bf16[512,512]{1,0:T(8,128)(2,1)S(1)}, bf16[512,512]{1,0:T(8,128)(2,1)S(1)}, u32[]{:S(2)}, u32[]{:S(2)}) collective-permute-start(bf16[512,512]{1,0:T(8,128)(2,1)S(1)} %pad_maximum_fusion.2), channel_id=1, source_target_pairs={{0,64},{16,80},{32,96},{48,112},{64,0},{80,16},{96,32},{112,48},{1... | collective-permute-start | bytes 1572872 | tf_op jit(solution)/shard_map/ppermute | solution.py:150
  79.2 9.1 %collective-permute-done.27 = bf16[512,512]{1,0:T(8,128)(2,1)S(1)} collective-permute-done((bf16[512,512]{1,0:T(8,128)(2,1)S(1)}, bf16[512,512]{1,0:T(8,128)(2,1)S(1)}, u32[]{:S(2)}, u32[]{:S(2)}) %collective-permute-start.27) | collective-permute-done | bytes 524320 | tf_op jit(solution)/shard_map/ppermute | solution.py:150
  88.4 2.6 %collective-permute-done.28 = bf16[512,512]{1,0:T(8,128)(2,1)S(1)} collective-permute-done((bf16[512,512]{1,0:T(8,128)(2,1)S(1)}, bf16[512,512]{1,0:T(8,128)(2,1)S(1)}, u32[]{:S(2)}, u32[]{:S(2)}) %collective-permute-start.28) | collective-permute-done | bytes 524320 | tf_op jit(solution)/shard_map/ppermute | solution.py:150
  91.0 9.4 %collective-permute-done.29 = bf16[512,512]{1,0:T(8,128)(2,1)S(1)} collective-permute-done((bf16[512,512]{1,0:T(8,128)(2,1)S(1)}, bf16[512,512]{1,0:T(8,128)(2,1)S(1)}, u32[]{:S(2)}, u32[]{:S(2)}) %collective-permute-start.29) | collective-permute-done | bytes 524320 | tf_op jit(solution)/shard_map/ppermute | solution.py:150
  100.6 2.7 %collective-permute-start.18 = (bf16[512,256]{1,0:T(8,128)(2,1)}, bf16[512,256]{1,0:T(8,128)(2,1)}, u32[]{:S(2)}, u32[]{:S(2)}) collective-permute-start(bf16[512,256]{1,0:T(8,128)(2,1)} %shard_map.60), channel_id=1, source_target_pairs={{0,128},{16,144},{32,160},{48,176},{64,192},{80,208},{96,224},{112... | collective-permute-start | bytes 786440 | tf_op jit(solution)/shard_map/ppermute | solution.py:174
  104.6 1.2 copy-done.2
  105.8 1.2 copy-done.4
  107.0 1.1 shard_map.59
  108.1 3.0 %collective-permute-done.18 = bf16[512,256]{1,0:T(8,128)(2,1)} collective-permute-done((bf16[512,256]{1,0:T(8,128)(2,1)}, bf16[512,256]{1,0:T(8,128)(2,1)}, u32[]{:S(2)}, u32[]{:S(2)}) %collective-permute-start.18) | collective-permute-done | bytes 262176 | tf_op jit(solution)/shard_map/ppermute | solution.py:174
  111.1 1.0 add_convert_fusion.2.refs_0_
  113.0 2.3 %shard_map.62 = bf16[512,256]{1,0:T(8,128)(2,1)S(1)} custom-call(s32[16]{0:T(128)S(1)} %pad_add_fusion.codes, bf16[8,256,256]{2,1,0:T(8,128)(2,1)S(1)} %copy-done, bf16[2048,256]{1,0:T(8,128)(2,1)} %constant_dynamic-update-slice_fusion.mine, bf16[2048,256]{1,0:T(8,128)(2,1)} %collective-permute-done.12.sib), custom_call_target="tpu_custom_call" | custom-call | flops 268435456 | bytes 2621440 | tf_op jit(solution)/shard_map/pallas_call | solution.py:94
  115.3 2.7 %collective-permute-start.19 = (bf16[512,256]{1,0:T(8,128)(2,1)S(1)}, bf16[512,256]{1,0:T(8,128)(2,1)S(1)}, u32[]{:S(2)}, u32[]{:S(2)}) collective-permute-start(bf16[512,256]{1,0:T(8,128)(2,1)S(1)} %shard_map.62), channel_id=1, source_target_pairs={{0,128},{16,144},{32,160},{48,176},{64,192},{80,208},{96,224},{112... | collective-permute-start | bytes 786440 | tf_op jit(solution)/shard_map/ppermute | solution.py:174
  118.0 1.0 collective-permute-start.33
  119.0 2.1 %shard_map.61 = f32[512,256]{1,0:T(8,128)S(1)} custom-call(s32[16]{0:T(128)S(1)} %pad_add_fusion.codes, bf16[8,256,256]{2,1,0:T(8,128)(2,1)S(1)} %copy-done, bf16[2048,256]{1,0:T(8,128)(2,1)} %constant_dynamic-update-slice_fusion.mine, bf16[2048,256]{1,0:T(8,128)(2,1)} %collective-permute-done.12.sib), custom_call_target="tpu_custom_call" | custom-call | flops 268435456 | bytes 2621440 | tf_op jit(solution)/shard_map/pallas_call | solution.py:94
  121.1 4.1 %collective-permute-done.19 = bf16[512,256]{1,0:T(8,128)(2,1)S(1)} collective-permute-done((bf16[512,256]{1,0:T(8,128)(2,1)S(1)}, bf16[512,256]{1,0:T(8,128)(2,1)S(1)}, u32[]{:S(2)}, u32[]{:S(2)}) %collective-permute-start.19) | collective-permute-done | bytes 262176 | tf_op jit(solution)/shard_map/ppermute | solution.py:174
  126.0 0.9 collective-permute-start.41
  126.9 2.1 %collective-permute-done.37.refs_1_ = bf16[512,256]{1,0:T(8,128)(2,1)S(1)} collective-permute-done((bf16[512,256]{1,0:T(8,128)(2,1)S(1)}, bf16[512,256]{1,0:T(8,128)(2,1)S(1)}, u32[]{:S(2)}, u32[]{:S(2)}) %collective-permute-start.37) | collective-permute-done | bytes 262176 | tf_op jit(solution)/shard_map/ppermute | solution.py:154
  128.9 1.5 collective-permute-start.38
  130.4 4.1 %collective-permute-done.33.refs_1_ = bf16[512,256]{1,0:T(8,128)(2,1)S(1)} collective-permute-done((bf16[512,256]{1,0:T(8,128)(2,1)S(1)}, bf16[512,256]{1,0:T(8,128)(2,1)S(1)}, u32[]{:S(2)}, u32[]{:S(2)}) %collective-permute-start.33) | collective-permute-done | bytes 262176 | tf_op jit(solution)/shard_map/ppermute | solution.py:154
  134.7 7.3 %collective-permute-done.41.refs_1_ = bf16[512,128]{1,0:T(8,128)(2,1)S(1)} collective-permute-done((bf16[512,128]{1,0:T(8,128)(2,1)S(1)}, bf16[512,128]{1,0:T(8,128)(2,1)S(1)}, u32[]{:S(2)}, u32[]{:S(2)}) %collective-permute-start.41) | collective-permute-done | bytes 131104 | tf_op jit(solution)/shard_map/ppermute | solution.py:154
  142.0 6.0 %collective-permute-done.38.refs_2_ = bf16[512,256]{1,0:T(8,128)(2,1)S(1)} collective-permute-done((bf16[512,256]{1,0:T(8,128)(2,1)S(1)}, bf16[512,256]{1,0:T(8,128)(2,1)S(1)}, u32[]{:S(2)}, u32[]{:S(2)}) %collective-permute-start.38) | collective-permute-done | bytes 262176 | tf_op jit(solution)/shard_map/ppermute | solution.py:155
  148.0 2.3 %shard_map.64 = bf16[512,512]{1,0:T(8,128)(2,1)S(1)} custom-call(s32[16]{0:T(128)S(1)} %pad_add_fusion.codes, bf16[8,256,256]{2,1,0:T(8,128)(2,1)S(1)} %copy-done, bf16[2048,512]{1,0:T(8,128)(2,1)S(1)} %constant_dynamic-update-slice_fusion.8.mine, bf16[2048,512]{1,0:T(8,128)(2,1)} %collective-permute-done.30.sib), custom_call_target="tpu_custom_call" | custom-call | flops 536870912 | bytes 5242880 | tf_op jit(solution)/shard_map/pallas_call | solution.py:94
  150.3 2.3 %collective-permute-start.31 = (bf16[512,512]{1,0:T(8,128)(2,1)S(1)}, bf16[512,512]{1,0:T(8,128)(2,1)S(1)}, u32[]{:S(2)}, u32[]{:S(2)}) collective-permute-start(bf16[512,512]{1,0:T(8,128)(2,1)S(1)} %shard_map.64), channel_id=1, source_target_pairs={{0,128},{16,144},{32,160},{48,176},{64,192},{80,208},{96,224},{112... | collective-permute-start | bytes 1572872 | tf_op jit(solution)/shard_map/ppermute | solution.py:174
  152.6 9.4 %collective-permute-done.42.refs_2_ = bf16[512,128]{1,0:T(8,128)(2,1)S(1)} collective-permute-done((bf16[512,128]{1,0:T(8,128)(2,1)S(1)}, bf16[512,128]{1,0:T(8,128)(2,1)S(1)}, u32[]{:S(2)}, u32[]{:S(2)}) %collective-permute-start.42) | collective-permute-done | bytes 131104 | tf_op jit(solution)/shard_map/ppermute | solution.py:155
  162.1 8.4 %collective-permute-done.43.refs_3_ = bf16[512,128]{1,0:T(8,128)(2,1)S(1)} collective-permute-done((bf16[512,128]{1,0:T(8,128)(2,1)S(1)}, bf16[512,128]{1,0:T(8,128)(2,1)S(1)}, u32[]{:S(2)}, u32[]{:S(2)}) %collective-permute-start.43) | collective-permute-done | bytes 131104 | tf_op jit(solution)/shard_map/ppermute | solution.py:156
  170.6 3.0 %shard_map.65.refs_5_ = f32[512,1024]{1,0:T(8,128)} custom-call(bf16[512,128]{1,0:T(8,128)(2,1)S(1)} %add_convert_fusion.4.refs_0_, bf16[512,128]{1,0:T(8,128)(2,1)S(1)} %collective-permute-done.41.refs_1_, bf16[512,128]{1,0:T(8,128)(2,1)S(1)} %collective-permute-done.42.refs_2_, bf16[512,128]{1,0:T(8,128)(2,1)S(1)} %collective-permute-done.43.refs_3_, ...), custom_call_target="tpu_custom_call" | custom-call | flops 536870912 | bytes 4194304 | tf_op jit(solution)/shard_map/pallas_call | solution.py:134
  173.6 4.8 %shard_map.66.refs_5_ = f32[512,1024]{1,0:T(8,128)} custom-call(bf16[512,256]{1,0:T(8,128)(2,1)S(1)} %add_convert_fusion.3.refs_0_, bf16[512,256]{1,0:T(8,128)(2,1)S(1)} %collective-permute-done.37.refs_1_, bf16[512,256]{1,0:T(8,128)(2,1)S(1)} %collective-permute-done.38.refs_2_, ...), custom_call_target="tpu_custom_call", output_to_operand_aliasing={{}: (5, {})} | custom-call | flops 1073741824 | bytes 4194304 | tf_op jit(solution)/shard_map/pallas_call | solution.py:134
  178.4 4.8 %shard_map.67.refs_4_ = f32[512,1024]{1,0:T(8,128)} custom-call(bf16[512,256]{1,0:T(8,128)(2,1)S(1)} %add_convert_fusion.2.refs_0_, bf16[512,256]{1,0:T(8,128)(2,1)S(1)} %collective-permute-done.33.refs_1_, bf16[512,256]{1,0:T(8,128)(2,1)S(1)} %collective-permute-done.34.refs_2_, ...), custom_call_target="tpu_custom_call", output_to_operand_aliasing={{}: (5, {})} | custom-call | flops 1073741824 | bytes 4194304 | tf_op jit(solution)/shard_map/pallas_call | solution.py:134
  183.3 4.5 %shard_map.68.refs_5_ = f32[512,1024]{1,0:T(8,128)} custom-call(bf16[512,256]{1,0:T(8,128)(2,1)S(1)} %add_convert_fusion.1.refs_0_, bf16[512,256]{1,0:T(8,128)(2,1)S(1)} %collective-permute-done.21.refs_1_, bf16[512,256]{1,0:T(8,128)(2,1)S(1)} %collective-permute-done.22.refs_2_, ...), custom_call_target="tpu_custom_call", output_to_operand_aliasing={{}: (4, {})} | custom-call | flops 805306368 | bytes 4194304 | tf_op jit(solution)/shard_map/pallas_call | solution.py:134
  187.8 2.3 %shard_map.63 = f32[512,512]{1,0:T(8,128)S(1)} custom-call(s32[16]{0:T(128)S(1)} %pad_add_fusion.codes, bf16[8,256,256]{2,1,0:T(8,128)(2,1)S(1)} %copy-done, bf16[2048,512]{1,0:T(8,128)(2,1)S(1)} %constant_dynamic-update-slice_fusion.8.mine, bf16[2048,512]{1,0:T(8,128)(2,1)} %collective-permute-done.30.sib), custom_call_target="tpu_custom_call" | custom-call | flops 536870912 | bytes 5242880 | tf_op jit(solution)/shard_map/pallas_call | solution.py:94
  190.0 1.0 collective-permute-done.31
  191.2 4.6 %shard_map.69.refs_2_ = f32[512,1024]{1,0:T(8,128)} custom-call(bf16[512,512]{1,0:T(8,128)(2,1)S(1)} %add_convert_fusion.refs_0_.refs_1_.refs_2_.refs_3_, bf16[512,512]{1,0:T(8,128)(2,1)S(1)} %add_convert_fusion.refs_0_.refs_1_.refs_2_.refs_3_, bf16[512,512]{1,0:T(8,128)(2,1)S(1)} %add_convert_fusion.refs_0_.refs_1_.refs_2_.refs_3_, ...), custom_call_target="tpu_custom_call", output_to_operand_aliasing={{}: (5, {})} | custom-call | flops 536870912 | bytes 4194304 | tf_op jit(solution)/shard_map/pallas_call | solution.py:134
  195.8 3.9 %shard_map.70 = f32[512,1024]{1,0:T(8,128)} custom-call(bf16[512,256]{1,0:T(8,128)(2,1)S(1)} %collective-permute-done.23.refs_0_, bf16[4,1024,1024]{2,1,0:T(8,128)(2,1)S(1)} %bitcast.17, f32[512,1024]{1,0:T(8,128)} %shard_map.69.refs_2_), custom_call_target="tpu_custom_call", output_to_operand_aliasing={{}: (2, {})} | custom-call | flops 268435456 | bytes 4194304 | tf_op jit(solution)/shard_map/pallas_call | solution.py:134
  (92 shorter events, 9.1 us)
Async XLA Ops:
  0.0 11.6 %copy-start.5 = (bf16[512,1024]{1,0:T(8,128)(2,1)S(1)}, bf16[512,1024]{1,0:T(8,128)(2,1)}, u32[]{:S(2)}) copy-start(bf16[512,1024]{1,0:T(8,128)(2,1)} %param.5) | copy-start | bytes 3145732
  0.0 17.1 %copy-start.7 = (s32[16,16]{1,0:T(8,128)S(1)}, s32[16,16]{1,0:T(8,128)}, u32[]{:S(2)}) copy-start(s32[16,16]{1,0:T(8,128)} %param.8) | copy-start | bytes 3076
  0.0 17.3 %copy-start.6 = (s32[16,16,3]{1,0,2:T(8,128)S(1)}, s32[16,16,3]{1,0,2:T(8,128)}, u32[]{:S(2)}) copy-start(s32[16,16,3]{1,0,2:T(8,128)} %param.7) | copy-start | bytes 9220
  0.0 17.6 %copy-start = (bf16[8,256,256]{2,1,0:T(8,128)(2,1)S(1)}, bf16[8,256,256]{2,1,0:T(8,128)(2,1)}, u32[]{:S(2)}) copy-start(bf16[8,256,256]{2,1,0:T(8,128)(2,1)} %coup.19) | copy-start | bytes 3145732
  1.2 6.7 %collective-permute-start.6 = (bf16[512,128]{1,0:T(8,128)(2,1)S(1)}, bf16[512,128]{1,0:T(8,128)(2,1)S(1)}, u32[]{:S(2)}, u32[]{:S(2)}) collective-permute-start(bf16[512,128]{1,0:T(8,128)(2,1)S(1)} %get-tuple-element.24), channel_id=1, source_target_pairs={{0,32},{16,48},{32,64},{48,80},{64,96},{80,112},{96,0},{112,16},{1... | collective-permute-start | bytes 393224 | tf_op jit(solution)/shard_map/ppermute | solution.py:150
  2.7 8.7 %collective-permute-start.5 = (bf16[512,128]{1,0:T(8,128)(2,1)S(1)}, bf16[512,128]{1,0:T(8,128)(2,1)S(1)}, u32[]{:S(2)}, u32[]{:S(2)}) collective-permute-start(bf16[512,128]{1,0:T(8,128)(2,1)S(1)} %get-tuple-element.24), channel_id=1, source_target_pairs={{0,64},{16,80},{32,96},{48,112},{64,0},{80,16},{96,32},{112,48},{1... | collective-permute-start | bytes 393224 | tf_op jit(solution)/shard_map/ppermute | solution.py:150
  5.5 6.0 %collective-permute-start.4 = (bf16[512,128]{1,0:T(8,128)(2,1)S(1)}, bf16[512,128]{1,0:T(8,128)(2,1)S(1)}, u32[]{:S(2)}, u32[]{:S(2)}) collective-permute-start(bf16[512,128]{1,0:T(8,128)(2,1)S(1)} %get-tuple-element.24), channel_id=1, source_target_pairs={{0,96},{16,112},{32,0},{48,16},{64,32},{80,48},{96,64},{112,80},{1... | collective-permute-start | bytes 393224 | tf_op jit(solution)/shard_map/ppermute | solution.py:150
  11.5 6.1 %collective-permute-start.7 = (bf16[2048,128]{1,0:T(8,128)(2,1)S(1)}, bf16[2048,128]{1,0:T(8,128)(2,1)S(1)}, u32[]{:S(2)}, u32[]{:S(2)}) collective-permute-start(bf16[2048,128]{1,0:T(8,128)(2,1)S(1)} %pad_maximum_fusion.1.mine), channel_id=1, source_target_pairs={{0,16},{16,0},{32,48},{48,32},{64,80},{80,64},{96,112},{112,96},{1... | collective-permute-start | bytes 1572872 | tf_op jit(solution)/shard_map/ppermute | solution.py:170
  11.7 10.0 %collective-permute-start.2 = (bf16[512,256]{1,0:T(8,128)(2,1)S(1)}, bf16[512,256]{1,0:T(8,128)(2,1)S(1)}, u32[]{:S(2)}, u32[]{:S(2)}) collective-permute-start(bf16[512,256]{1,0:T(8,128)(2,1)S(1)} %get-tuple-element.26), channel_id=1, source_target_pairs={{0,32},{16,48},{32,64},{48,80},{64,96},{80,112},{96,0},{112,16},{1... | collective-permute-start | bytes 786440 | tf_op jit(solution)/shard_map/ppermute | solution.py:150
  13.1 14.8 %collective-permute-start.1 = (bf16[512,256]{1,0:T(8,128)(2,1)S(1)}, bf16[512,256]{1,0:T(8,128)(2,1)}, u32[]{:S(2)}, u32[]{:S(2)}) collective-permute-start(bf16[512,256]{1,0:T(8,128)(2,1)S(1)} %get-tuple-element.26), channel_id=1, source_target_pairs={{0,64},{16,80},{32,96},{48,112},{64,0},{80,16},{96,32},{112,48},{1... | collective-permute-start | bytes 786440 | tf_op jit(solution)/shard_map/ppermute | solution.py:150
  15.5 13.2 %collective-permute-start = (bf16[512,256]{1,0:T(8,128)(2,1)S(1)}, bf16[512,256]{1,0:T(8,128)(2,1)}, u32[]{:S(2)}, u32[]{:S(2)}) collective-permute-start(bf16[512,256]{1,0:T(8,128)(2,1)S(1)} %get-tuple-element.26), channel_id=1, source_target_pairs={{0,96},{16,112},{32,0},{48,16},{64,32},{80,48},{96,64},{112,80},{1... | collective-permute-start | bytes 786440 | tf_op jit(solution)/shard_map/ppermute | solution.py:150
  18.7 16.1 %collective-permute-start.13 = (bf16[512,256]{1,0:T(8,128)(2,1)S(1)}, bf16[512,256]{1,0:T(8,128)(2,1)S(1)}, u32[]{:S(2)}, u32[]{:S(2)}) collective-permute-start(bf16[512,256]{1,0:T(8,128)(2,1)S(1)} %get-tuple-element.14), channel_id=1, source_target_pairs={{0,96},{16,112},{32,0},{48,16},{64,32},{80,48},{96,64},{112,80},{1... | collective-permute-start | bytes 786440 | tf_op jit(solution)/shard_map/ppermute | solution.py:150
  29.9 28.0 %collective-permute-start.3 = (bf16[2048,256]{1,0:T(8,128)(2,1)S(1)}, bf16[2048,256]{1,0:T(8,128)(2,1)S(1)}, u32[]{:S(2)}, u32[]{:S(2)}) collective-permute-start(bf16[2048,256]{1,0:T(8,128)(2,1)S(1)} %pad_maximum_fusion.mine), channel_id=1, source_target_pairs={{0,16},{16,0},{32,48},{48,32},{64,80},{80,64},{96,112},{112,96},{1... | collective-permute-start | bytes 3145736 | tf_op jit(solution)/shard_map/ppermute | solution.py:170
  30.0 10.7 %collective-permute-start.14 = (bf16[512,256]{1,0:T(8,128)(2,1)S(1)}, bf16[512,256]{1,0:T(8,128)(2,1)S(1)}, u32[]{:S(2)}, u32[]{:S(2)}) collective-permute-start(bf16[512,256]{1,0:T(8,128)(2,1)S(1)} %get-tuple-element.14), channel_id=1, source_target_pairs={{0,64},{16,80},{32,96},{48,112},{64,0},{80,16},{96,32},{112,48},{1... | collective-permute-start | bytes 786440 | tf_op jit(solution)/shard_map/ppermute | solution.py:150
  32.7 13.2 %collective-permute-start.24 = (bf16[512,128]{1,0:T(8,128)(2,1)S(1)}, bf16[512,128]{1,0:T(8,128)(2,1)S(1)}, u32[]{:S(2)}, u32[]{:S(2)}) collective-permute-start(bf16[512,128]{1,0:T(8,128)(2,1)S(1)} %get-tuple-element.23), channel_id=1, source_target_pairs={{0,1},{1,2},{2,3},{3,4},{4,5},{5,6},{6,7},{7,8},{8,9},{9,10},{10,1... | collective-permute-start | bytes 393224 | tf_op jit(solution)/shard_map/ppermute | solution.py:160
  34.6 11.2 %collective-permute-start.15 = (bf16[512,256]{1,0:T(8,128)(2,1)S(1)}, bf16[512,256]{1,0:T(8,128)(2,1)S(1)}, u32[]{:S(2)}, u32[]{:S(2)}) collective-permute-start(bf16[512,256]{1,0:T(8,128)(2,1)S(1)} %get-tuple-element.14), channel_id=1, source_target_pairs={{0,32},{16,48},{32,64},{48,80},{64,96},{80,112},{96,0},{112,16},{1... | collective-permute-start | bytes 786440 | tf_op jit(solution)/shard_map/ppermute | solution.py:150
  45.8 24.9 %copy-start.1 = (bf16[2048,256]{1,0:T(8,128)(2,1)}, bf16[2048,256]{1,0:T(8,128)(2,1)S(1)}, u32[]{:S(2)}) copy-start(bf16[2048,256]{1,0:T(8,128)(2,1)S(1)} %constant_dynamic-update-slice_fusion.4.mine) | copy-start | bytes 3145732
  45.8 24.9 %collective-permute-start.16 = (bf16[2048,256]{1,0:T(8,128)(2,1)S(1)}, bf16[2048,256]{1,0:T(8,128)(2,1)S(1)}, u32[]{:S(2)}, u32[]{:S(2)}) collective-permute-start(bf16[2048,256]{1,0:T(8,128)(2,1)S(1)} %constant_dynamic-update-slice_fusion.4.mine), channel_id=1, source_target_pairs={{0,16},{16,0},{32,48},{48,32},{64,80},{80,64},{96,112},{112,96},{1... | collective-permute-start | bytes 3145736 | tf_op jit(solution)/shard_map/ppermute | solution.py:170
  45.9 10.0 %collective-permute-start.25 = (bf16[512,128]{1,0:T(8,128)(2,1)S(1)}, bf16[512,128]{1,0:T(8,128)(2,1)S(1)}, u32[]{:S(2)}, u32[]{:S(2)}) collective-permute-start(bf16[512,128]{1,0:T(8,128)(2,1)S(1)} %collective-permute-done.24), channel_id=1, source_target_pairs={{0,1},{1,2},{2,3},{3,4},{4,5},{5,6},{6,7},{7,8},{8,9},{9,10},{10,1... | collective-permute-start | bytes 393224 | tf_op jit(solution)/shard_map/ppermute | solution.py:160
  47.9 9.9 %collective-permute-start.8 = (bf16[512,128]{1,0:T(8,128)(2,1)S(1)}, bf16[512,128]{1,0:T(8,128)(2,1)S(1)}, u32[]{:S(2)}, u32[]{:S(2)}) collective-permute-start(bf16[512,128]{1,0:T(8,128)(2,1)S(1)} %shard_map.56), channel_id=1, source_target_pairs={{0,128},{16,144},{32,160},{48,176},{64,192},{80,208},{96,224},{112... | collective-permute-start | bytes 393224 | tf_op jit(solution)/shard_map/ppermute | solution.py:174
  55.9 7.3 %collective-permute-start.26 = (bf16[512,128]{1,0:T(8,128)(2,1)S(1)}, bf16[512,128]{1,0:T(8,128)(2,1)S(1)}, u32[]{:S(2)}, u32[]{:S(2)}) collective-permute-start(bf16[512,128]{1,0:T(8,128)(2,1)S(1)} %collective-permute-done.25), channel_id=1, source_target_pairs={{0,1},{1,2},{2,3},{3,4},{4,5},{5,6},{6,7},{7,8},{8,9},{9,10},{10,1... | collective-permute-start | bytes 393224 | tf_op jit(solution)/shard_map/ppermute | solution.py:160
  59.0 11.7 %collective-permute-start.17 = (bf16[512,256]{1,0:T(8,128)(2,1)S(1)}, bf16[512,256]{1,0:T(8,128)(2,1)S(1)}, u32[]{:S(2)}, u32[]{:S(2)}) collective-permute-start(bf16[512,256]{1,0:T(8,128)(2,1)S(1)} %shard_map.57), channel_id=1, source_target_pairs={{0,128},{16,144},{32,160},{48,176},{64,192},{80,208},{96,224},{112... | collective-permute-start | bytes 786440 | tf_op jit(solution)/shard_map/ppermute | solution.py:174
  63.3 13.7 %collective-permute-start.9 = (bf16[512,256]{1,0:T(8,128)(2,1)S(1)}, bf16[512,256]{1,0:T(8,128)(2,1)S(1)}, u32[]{:S(2)}, u32[]{:S(2)}) collective-permute-start(bf16[512,256]{1,0:T(8,128)(2,1)S(1)} %get-tuple-element.13), channel_id=1, source_target_pairs={{0,96},{16,112},{32,0},{48,16},{64,32},{80,48},{96,64},{112,80},{1... | collective-permute-start | bytes 786440 | tf_op jit(solution)/shard_map/ppermute | solution.py:150
  64.0 13.8 %collective-permute-start.10 = (bf16[512,256]{1,0:T(8,128)(2,1)S(1)}, bf16[512,256]{1,0:T(8,128)(2,1)S(1)}, u32[]{:S(2)}, u32[]{:S(2)}) collective-permute-start(bf16[512,256]{1,0:T(8,128)(2,1)S(1)} %get-tuple-element.13), channel_id=1, source_target_pairs={{0,64},{16,80},{32,96},{48,112},{64,0},{80,16},{96,32},{112,48},{1... | collective-permute-start | bytes 786440 | tf_op jit(solution)/shard_map/ppermute | solution.py:150
  66.6 11.8 %collective-permute-start.11 = (bf16[512,256]{1,0:T(8,128)(2,1)S(1)}, bf16[512,256]{1,0:T(8,128)(2,1)S(1)}, u32[]{:S(2)}, u32[]{:S(2)}) collective-permute-start(bf16[512,256]{1,0:T(8,128)(2,1)S(1)} %get-tuple-element.13), channel_id=1, source_target_pairs={{0,32},{16,48},{32,64},{48,80},{64,96},{80,112},{96,0},{112,16},{1... | collective-permute-start | bytes 786440 | tf_op jit(solution)/shard_map/ppermute | solution.py:150
  70.8 7.0 %copy-start.3 = (bf16[2048,256]{1,0:T(8,128)(2,1)}, bf16[2048,256]{1,0:T(8,128)(2,1)S(1)}, u32[]{:S(2)}) copy-start(bf16[2048,256]{1,0:T(8,128)(2,1)S(1)} %collective-permute-done.16.sib) | copy-start | bytes 3145732
  72.6 15.7 %collective-permute-start.27 = (bf16[512,512]{1,0:T(8,128)(2,1)S(1)}, bf16[512,512]{1,0:T(8,128)(2,1)S(1)}, u32[]{:S(2)}, u32[]{:S(2)}) collective-permute-start(bf16[512,512]{1,0:T(8,128)(2,1)S(1)} %pad_maximum_fusion.2), channel_id=1, source_target_pairs={{0,96},{16,112},{32,0},{48,16},{64,32},{80,48},{96,64},{112,80},{1... | collective-permute-start | bytes 1572872 | tf_op jit(solution)/shard_map/ppermute | solution.py:150
  74.6 16.4 %collective-permute-start.28 = (bf16[512,512]{1,0:T(8,128)(2,1)S(1)}, bf16[512,512]{1,0:T(8,128)(2,1)S(1)}, u32[]{:S(2)}, u32[]{:S(2)}) collective-permute-start(bf16[512,512]{1,0:T(8,128)(2,1)S(1)} %pad_maximum_fusion.2), channel_id=1, source_target_pairs={{0,64},{16,80},{32,96},{48,112},{64,0},{80,16},{96,32},{112,48},{1... | collective-permute-start | bytes 1572872 | tf_op jit(solution)/shard_map/ppermute | solution.py:150
  77.7 22.7 %collective-permute-start.29 = (bf16[512,512]{1,0:T(8,128)(2,1)S(1)}, bf16[512,512]{1,0:T(8,128)(2,1)S(1)}, u32[]{:S(2)}, u32[]{:S(2)}) collective-permute-start(bf16[512,512]{1,0:T(8,128)(2,1)S(1)} %pad_maximum_fusion.2), channel_id=1, source_target_pairs={{0,32},{16,48},{32,64},{48,80},{64,96},{80,112},{96,0},{112,16},{1... | collective-permute-start | bytes 1572872 | tf_op jit(solution)/shard_map/ppermute | solution.py:150
  79.2 33.8 %collective-permute-start.12 = (bf16[2048,256]{1,0:T(8,128)(2,1)}, bf16[2048,256]{1,0:T(8,128)(2,1)}, u32[]{:S(2)}, u32[]{:S(2)}) collective-permute-start(bf16[2048,256]{1,0:T(8,128)(2,1)} %constant_dynamic-update-slice_fusion.mine), channel_id=1, source_target_pairs={{0,16},{16,0},{32,48},{48,32},{64,80},{80,64},{96,112},{112,96},{1... | collective-permute-start | bytes 3145736 | tf_op jit(solution)/shard_map/ppermute | solution.py:170
  100.5 47.5 %collective-permute-start.30 = (bf16[2048,512]{1,0:T(8,128)(2,1)S(1)}, bf16[2048,512]{1,0:T(8,128)(2,1)}, u32[]{:S(2)}, u32[]{:S(2)}) collective-permute-start(bf16[2048,512]{1,0:T(8,128)(2,1)S(1)} %constant_dynamic-update-slice_fusion.8.mine), channel_id=1, source_target_pairs={{0,16},{16,0},{32,48},{48,32},{64,80},{80,64},{96,112},{112,96},{1... | collective-permute-start | bytes 6291464 | tf_op jit(solution)/shard_map/ppermute | solution.py:170
  100.6 10.5 %collective-permute-start.18 = (bf16[512,256]{1,0:T(8,128)(2,1)}, bf16[512,256]{1,0:T(8,128)(2,1)}, u32[]{:S(2)}, u32[]{:S(2)}) collective-permute-start(bf16[512,256]{1,0:T(8,128)(2,1)} %shard_map.60), channel_id=1, source_target_pairs={{0,128},{16,144},{32,160},{48,176},{64,192},{80,208},{96,224},{112... | collective-permute-start | bytes 786440 | tf_op jit(solution)/shard_map/ppermute | solution.py:174
  103.2 22.7 %collective-permute-start.40 = (bf16[512,128]{1,0:T(8,128)(2,1)S(1)}, bf16[512,128]{1,0:T(8,128)(2,1)S(1)}, u32[]{:S(2)}, u32[]{:S(2)}) collective-permute-start(bf16[512,128]{1,0:T(8,128)(2,1)S(1)} %add_convert_fusion.4.refs_0_), channel_id=1, source_target_pairs={{7,15},{15,7},{23,31},{31,23},{39,47},{47,39},{55,63},{63,55},{71,... | collective-permute-start | bytes 393224 | tf_op jit(solution)/shard_map/ppermute | solution.py:153
  103.9 8.9 %collective-permute-start.36 = (bf16[512,256]{1,0:T(8,128)(2,1)S(1)}, bf16[512,256]{1,0:T(8,128)(2,1)S(1)}, u32[]{:S(2)}, u32[]{:S(2)}) collective-permute-start(bf16[512,256]{1,0:T(8,128)(2,1)S(1)} %add_convert_fusion.3.refs_0_), channel_id=1, source_target_pairs={{7,15},{15,7},{23,31},{31,23},{39,47},{47,39},{55,63},{63,55},{71,... | collective-permute-start | bytes 786440 | tf_op jit(solution)/shard_map/ppermute | solution.py:153
  104.6 1.2 copy-start.2
  105.8 1.2 copy-start.4
  112.1 5.8 %collective-permute-start.32 = (bf16[512,256]{1,0:T(8,128)(2,1)S(1)}, bf16[512,256]{1,0:T(8,128)(2,1)S(1)}, u32[]{:S(2)}, u32[]{:S(2)}) collective-permute-start(bf16[512,256]{1,0:T(8,128)(2,1)S(1)} %add_convert_fusion.2.refs_0_), channel_id=1, source_target_pairs={{7,15},{15,7},{23,31},{31,23},{39,47},{47,39},{55,63},{63,55},{71,... | collective-permute-start | bytes 786440 | tf_op jit(solution)/shard_map/ppermute | solution.py:153
  112.9 16.0 %collective-permute-start.37 = (bf16[512,256]{1,0:T(8,128)(2,1)S(1)}, bf16[512,256]{1,0:T(8,128)(2,1)S(1)}, u32[]{:S(2)}, u32[]{:S(2)}) collective-permute-start(bf16[512,256]{1,0:T(8,128)(2,1)S(1)} %broadcast_select_fusion), channel_id=1, source_target_pairs={{0,1},{1,2},{2,3},{3,4},{4,5},{5,6},{6,7},{7,0},{8,9},{9,10},{10,1... | collective-permute-start | bytes 786440 | tf_op jit(solution)/shard_map/ppermute | solution.py:154
  113.0 57.6 %slice-start = ((s8[8388608]{0:T(1024)(128)(4,1)}), s8[4194304]{0:T(1024)(128)(4,1)S(1)}, s32[]{:S(2)}) async-start(s8[8388608]{0:T(1024)(128)(4,1)} %bitcast.16), calls=%async_computation | async-start | bytes 8388608
  115.3 9.9 %collective-permute-start.19 = (bf16[512,256]{1,0:T(8,128)(2,1)S(1)}, bf16[512,256]{1,0:T(8,128)(2,1)S(1)}, u32[]{:S(2)}, u32[]{:S(2)}) collective-permute-start(bf16[512,256]{1,0:T(8,128)(2,1)S(1)} %shard_map.62), channel_id=1, source_target_pairs={{0,128},{16,144},{32,160},{48,176},{64,192},{80,208},{96,224},{112... | collective-permute-start | bytes 786440 | tf_op jit(solution)/shard_map/ppermute | solution.py:174
  118.0 16.6 %collective-permute-start.33 = (bf16[512,256]{1,0:T(8,128)(2,1)S(1)}, bf16[512,256]{1,0:T(8,128)(2,1)S(1)}, u32[]{:S(2)}, u32[]{:S(2)}) collective-permute-start(bf16[512,256]{1,0:T(8,128)(2,1)S(1)} %broadcast_select_fusion.1), channel_id=1, source_target_pairs={{0,1},{1,2},{2,3},{3,4},{4,5},{5,6},{6,7},{7,0},{8,9},{9,10},{10,1... | collective-permute-start | bytes 786440 | tf_op jit(solution)/shard_map/ppermute | solution.py:154
  121.1 49.4 %slice-start.1 = ((s8[8388608]{0:T(1024)(128)(4,1)}), s8[4194304]{0:T(1024)(128)(4,1)S(1)}, s32[]{:S(2)}) async-start(s8[8388608]{0:T(1024)(128)(4,1)} %bitcast.16), calls=%async_computation.1 | async-start | bytes 8388608
  125.2 9.3 %collective-permute-start.20 = (bf16[512,256]{1,0:T(8,128)(2,1)S(1)}, bf16[512,256]{1,0:T(8,128)(2,1)S(1)}, u32[]{:S(2)}, u32[]{:S(2)}) collective-permute-start(bf16[512,256]{1,0:T(8,128)(2,1)S(1)} %add_convert_fusion.1.refs_0_), channel_id=1, source_target_pairs={{7,15},{15,7},{23,31},{31,23},{39,47},{47,39},{55,63},{63,55},{71,... | collective-permute-start | bytes 786440 | tf_op jit(solution)/shard_map/ppermute | solution.py:153
  126.0 16.0 %collective-permute-start.41 = (bf16[512,128]{1,0:T(8,128)(2,1)S(1)}, bf16[512,128]{1,0:T(8,128)(2,1)S(1)}, u32[]{:S(2)}, u32[]{:S(2)}) collective-permute-start(bf16[512,128]{1,0:T(8,128)(2,1)S(1)} %broadcast_select_fusion.3), channel_id=1, source_target_pairs={{0,1},{1,2},{2,3},{3,4},{4,5},{5,6},{6,7},{7,0},{8,9},{9,10},{10,1... | collective-permute-start | bytes 393224 | tf_op jit(solution)/shard_map/ppermute | solution.py:154
  128.9 19.1 %collective-permute-start.38 = (bf16[512,256]{1,0:T(8,128)(2,1)S(1)}, bf16[512,256]{1,0:T(8,128)(2,1)S(1)}, u32[]{:S(2)}, u32[]{:S(2)}) collective-permute-start(bf16[512,256]{1,0:T(8,128)(2,1)S(1)} %collective-permute-done.37.refs_1_), channel_id=1, source_target_pairs={{0,1},{1,2},{2,3},{3,4},{4,5},{5,6},{6,7},{7,8},{8,9},{9,10},{10,1... | collective-permute-start | bytes 786440 | tf_op jit(solution)/shard_map/ppermute | solution.py:155
  134.5 27.5 %collective-permute-start.34 = (bf16[512,256]{1,0:T(8,128)(2,1)S(1)}, bf16[512,256]{1,0:T(8,128)(2,1)S(1)}, u32[]{:S(2)}, u32[]{:S(2)}) collective-permute-start(bf16[512,256]{1,0:T(8,128)(2,1)S(1)} %collective-permute-done.33.refs_1_), channel_id=1, source_target_pairs={{0,1},{1,2},{2,3},{3,4},{4,5},{5,6},{6,7},{7,8},{8,9},{9,10},{10,1... | collective-permute-start | bytes 786440 | tf_op jit(solution)/shard_map/ppermute | solution.py:155
  134.6 27.5 %collective-permute-start.21 = (bf16[512,256]{1,0:T(8,128)(2,1)S(1)}, bf16[512,256]{1,0:T(8,128)(2,1)S(1)}, u32[]{:S(2)}, u32[]{:S(2)}) collective-permute-start(bf16[512,256]{1,0:T(8,128)(2,1)S(1)} %broadcast_select_fusion.2), channel_id=1, source_target_pairs={{0,1},{1,2},{2,3},{3,4},{4,5},{5,6},{6,7},{7,0},{8,9},{9,10},{10,1... | collective-permute-start | bytes 786440 | tf_op jit(solution)/shard_map/ppermute | solution.py:154
  142.0 20.0 %collective-permute-start.42 = (bf16[512,128]{1,0:T(8,128)(2,1)S(1)}, bf16[512,128]{1,0:T(8,128)(2,1)S(1)}, u32[]{:S(2)}, u32[]{:S(2)}) collective-permute-start(bf16[512,128]{1,0:T(8,128)(2,1)S(1)} %collective-permute-done.41.refs_1_), channel_id=1, source_target_pairs={{0,1},{1,2},{2,3},{3,4},{4,5},{5,6},{6,7},{7,8},{8,9},{9,10},{10,1... | collective-permute-start | bytes 393224 | tf_op jit(solution)/shard_map/ppermute | solution.py:155
  148.0 25.6 %collective-permute-start.39 = (bf16[512,256]{1,0:T(8,128)(2,1)S(1)}, bf16[512,256]{1,0:T(8,128)(2,1)S(1)}, u32[]{:S(2)}, u32[]{:S(2)}) collective-permute-start(bf16[512,256]{1,0:T(8,128)(2,1)S(1)} %collective-permute-done.38.refs_2_), channel_id=1, source_target_pairs={{0,1},{1,2},{2,3},{3,4},{4,5},{5,6},{6,7},{7,8},{8,9},{9,10},{10,1... | collective-permute-start | bytes 786440 | tf_op jit(solution)/shard_map/ppermute | solution.py:156
  150.3 40.7 %collective-permute-start.31 = (bf16[512,512]{1,0:T(8,128)(2,1)S(1)}, bf16[512,512]{1,0:T(8,128)(2,1)S(1)}, u32[]{:S(2)}, u32[]{:S(2)}) collective-permute-start(bf16[512,512]{1,0:T(8,128)(2,1)S(1)} %shard_map.64), channel_id=1, source_target_pairs={{0,128},{16,144},{32,160},{48,176},{64,192},{80,208},{96,224},{112... | collective-permute-start | bytes 1572872 | tf_op jit(solution)/shard_map/ppermute | solution.py:174
  162.0 8.5 %collective-permute-start.43 = (bf16[512,128]{1,0:T(8,128)(2,1)S(1)}, bf16[512,128]{1,0:T(8,128)(2,1)S(1)}, u32[]{:S(2)}, u32[]{:S(2)}) collective-permute-start(bf16[512,128]{1,0:T(8,128)(2,1)S(1)} %collective-permute-done.42.refs_2_), channel_id=1, source_target_pairs={{0,1},{1,2},{2,3},{3,4},{4,5},{5,6},{6,7},{7,8},{8,9},{9,10},{10,1... | collective-permute-start | bytes 393224 | tf_op jit(solution)/shard_map/ppermute | solution.py:156
  162.0 16.4 %collective-permute-start.35 = (bf16[512,256]{1,0:T(8,128)(2,1)S(1)}, bf16[512,256]{1,0:T(8,128)(2,1)S(1)}, u32[]{:S(2)}, u32[]{:S(2)}) collective-permute-start(bf16[512,256]{1,0:T(8,128)(2,1)S(1)} %collective-permute-done.34.refs_2_), channel_id=1, source_target_pairs={{0,1},{1,2},{2,3},{3,4},{4,5},{5,6},{6,7},{7,8},{8,9},{9,10},{10,1... | collective-permute-start | bytes 786440 | tf_op jit(solution)/shard_map/ppermute | solution.py:156
  162.0 21.2 %collective-permute-start.22 = (bf16[512,256]{1,0:T(8,128)(2,1)S(1)}, bf16[512,256]{1,0:T(8,128)(2,1)S(1)}, u32[]{:S(2)}, u32[]{:S(2)}) collective-permute-start(bf16[512,256]{1,0:T(8,128)(2,1)S(1)} %collective-permute-done.21.refs_1_), channel_id=1, source_target_pairs={{0,1},{1,2},{2,3},{3,4},{4,5},{5,6},{6,7},{7,8},{8,9},{9,10},{10,1... | collective-permute-start | bytes 786440 | tf_op jit(solution)/shard_map/ppermute | solution.py:155
  183.3 12.5 %collective-permute-start.23 = (bf16[512,256]{1,0:T(8,128)(2,1)S(1)}, bf16[512,256]{1,0:T(8,128)(2,1)S(1)}, u32[]{:S(2)}, u32[]{:S(2)}) collective-permute-start(bf16[512,256]{1,0:T(8,128)(2,1)S(1)} %collective-permute-done.22.refs_2_), channel_id=1, source_target_pairs={{0,1},{1,2},{2,3},{3,4},{4,5},{5,6},{6,7},{7,8},{8,9},{9,10},{10,1... | collective-permute-start | bytes 786440 | tf_op jit(solution)/shard_map/ppermute | solution.py:156

commit v2 on v1

v2 whole, which is shorter than its diff:
```python
import functools

import jax
import jax.numpy as jnp
from jax import lax
from jax.experimental import pallas as pl
from jax.experimental.pallas import tpu as pltpu
from jax.sharding import PartitionSpec as P

AB = 256
ABLK = 2
STOPS = 4
NX = 4
NZ = 8
ROWS = ABLK * AB
EARLY = 384
PARTS = 2
COLUMN_TILE = 256

COST = pl.CostEstimate(flops=1 << 20, bytes_accessed=1 << 12, transcendentals=0)
VMEM = pl.BlockSpec(memory_space=pltpu.VMEM)
SMEM = pl.BlockSpec(memory_space=pltpu.SMEM)


def device_of(y, x, core):
    return (y * NX + x) * 2 + core


def alpha_route(move):
    route = []
    for y in range(2):
        for x in range(NX):
            for core in range(2):
                to = move(y, x, core)
                route.append((device_of(y, x, core), device_of(*to)))
    return route


def to_x(step):
    return alpha_route(lambda y, x, core: (y, (x + step) % NX, core))


SWAP_CORE = alpha_route(lambda y, x, core: (y, x, 1 - core))
SWAP_Y = alpha_route(lambda y, x, core: (1 - y, x, core))
RING = [(i, (i + 1) % (2 * NZ)) for i in range(2 * NZ)]


def after(value, *earlier):
    return lax.optimization_barrier((value, *earlier))[0]


def slot_codes(exc_list, counts):
    me = lax.axis_index("alpha")
    y = me // (2 * NX)
    mates = 2 * NX
    exc = lax.dynamic_slice_in_dim(exc_list, y * mates, mates, 0)
    live = lax.dynamic_slice_in_dim(counts, y * mates, mates, 0) == 1
    codes = []
    for target in (me, (me + mates) % (2 * mates)):
        entry = lax.dynamic_index_in_dim(exc, target, 1, keepdims=False)
        used = lax.dynamic_index_in_dim(live, target, 1, keepdims=False)
        source = entry[:, 0] - (y * mates + jnp.arange(mates, dtype=jnp.int32)) * ABLK
        goal = entry[:, 1] - target * ABLK
        codes.append(jnp.where(used, (entry[:, 2] * 2 + goal) * 2 + source, -1))
    return jnp.concatenate(codes)


def couple_kernel(codes, coup, mine, sib, near, away, acc):
    me = lax.axis_index("alpha")
    x, core = (me // 2) % NX, me % 2
    near[...] = jnp.zeros_like(near)
    acc[...] = jnp.zeros_like(acc)
    for which, total in enumerate((near, acc)):
        for stack, side in ((mine, core), (sib, 1 - core)):

            @pl.loop(0, NX)
            def _(step):
                code = codes[which * 2 * NX + lax.rem(x + step, NX) * 2 + side]

                @pl.when(code >= 0)
                def _():
                    kind, goal, source = code // 4, (code // 2) % 2, code % 2
                    rows = pl.ds(pl.multiple_of(goal * AB, AB), AB)
                    block = stack[pl.ds(pl.multiple_of(step * ROWS + source * AB, AB), AB), :]
                    total[rows, :] += jnp.dot(coup[kind], block, preferred_element_type=jnp.float32)

    away[...] = acc[...].astype(away.dtype)


def couple(codes, couplings, mine, sib):
    cols = mine.shape[1]
    return pl.pallas_call(
        couple_kernel,
        in_specs=[SMEM] + [VMEM] * 3,
        out_specs=[VMEM, VMEM],
        scratch_shapes=[pltpu.VMEM((ROWS, cols), jnp.float32)],
        out_shape=[
            jax.ShapeDtypeStruct((ROWS, cols), jnp.float32),
            jax.ShapeDtypeStruct((ROWS, cols), jnp.bfloat16),
        ],
        cost_estimate=COST,
        compiler_params=pltpu.CompilerParams(vmem_limit_bytes=12 << 20),
    )(codes, couplings, mine, sib)


def stack_kernel(*refs):
    out = refs[-1]
    row = 0
    for ref in refs[:-1]:
        out[row : row + ref.shape[0], :] = ref[...]
        row += ref.shape[0]


def stack(blocks):
    rows, cols = sum(b.shape[0] for b in blocks), blocks[0].shape[1]
    return pl.pallas_call(
        stack_kernel,
        in_specs=[VMEM] * len(blocks),
        out_specs=VMEM,
        out_shape=jax.ShapeDtypeStruct((rows, cols), jnp.bfloat16),
        cost_estimate=COST,
        compiler_params=pltpu.CompilerParams(vmem_limit_bytes=4 << 20),
    )(*blocks)


def band_kernel(pieces, first, *refs):
    n = len(pieces)
    blocks, tiles = refs[:n], refs[n]
    before, out = (None, refs[n + 1]) if first else refs[n + 1 :]

    @pl.loop(0, tiles.shape[2], step=COLUMN_TILE)
    def _(column):
        span = pl.ds(pl.multiple_of(column, COLUMN_TILE), COLUMN_TILE)
        left = jnp.concatenate([block[...] for block in blocks], axis=1)
        right = jnp.concatenate([tiles[d, s : s + w, span] for d, s, w in pieces], axis=0)
        part = jnp.dot(left, right, preferred_element_type=jnp.float32)
        if not first:
            part = before[:, span] + part
        out[:, span] = part.astype(out.dtype)


def band(total, tiles, blocks, pieces, kind=jnp.float32):
    first = total is None
    arrays = list(blocks) + [tiles] + ([] if first else [total])
    return pl.pallas_call(
        functools.partial(band_kernel, tuple(pieces), first),
        in_specs=[VMEM] * len(arrays),
        out_specs=VMEM,
        out_shape=jax.ShapeDtypeStruct((ROWS, tiles.shape[2]), kind),
        input_output_aliases={} if first else {len(arrays) - 1: 0},
        cost_estimate=COST,
        compiler_params=pltpu.CompilerParams(vmem_limit_bytes=12 << 20),
    )(*arrays)


def tie(*values):
    return list(lax.optimization_barrier(values))


def per_device(coefficients, couplings, exc_list, counts, beta_tiles):
    codes = slot_codes(exc_list, counts)

    def spread(own):
        left = lax.ppermute(own, "alpha", to_x(1))
        right = lax.ppermute(own, "alpha", to_x(-1))
        far = [
            lax.ppermute(left[:AB], "alpha", to_x(1)),
            lax.ppermute(right[AB:], "alpha", to_x(-1)),
        ]
        return [own, right, *far, left]

    def hop(block):
        return lax.ppermute(block, "beta", RING)

    cols = coefficients.shape[1]
    early = [coefficients[:, :EARLY]]
    for _ in range(STOPS - 1):
        early.append(hop(early[-1]))
    parts = spread(coefficients[:, EARLY:])
    *parts, early[3] = tie(*parts, early[3])
    mine = stack(parts)
    sib = lax.ppermute(mine, "alpha", SWAP_CORE)
    mixed = band(None, beta_tiles, early, [(d, 0, EARLY) for d in range(STOPS)], jnp.bfloat16)
    sib, mixed = tie(sib, mixed)
    near, away = couple(codes, couplings, mine, sib)
    back = lax.ppermute(away, "alpha", SWAP_Y)
    moved = [(near + back.astype(jnp.float32)).astype(jnp.bfloat16)]

    parts = spread(mixed)
    moved.append(hop(moved[0]))
    moved.append(hop(moved[1]))
    *parts, moved[2] = tie(*parts, moved[2])
    moved.append(hop(moved[2]))
    half = cols // PARTS
    mines = [stack([p[:, k * half : (k + 1) * half] for p in parts]) for k in range(PARTS)]
    sibs = [lax.ppermute(m, "alpha", SWAP_CORE) for m in mines]
    nears, backs = [], []
    for k in range(PARTS):
        if k:
            sibs[k], away = tie(sibs[k], away)
            backs[k - 1] = lax.ppermute(away, "alpha", SWAP_Y)
        near, away = couple(codes, couplings, mines[k], sibs[k])
        nears.append(near)
        backs.append(lax.ppermute(away, "alpha", SWAP_Y))
    width = cols - EARLY
    total = band(None, beta_tiles, moved[:3], [(d, EARLY, width) for d in range(3)])
    moved[3], total = tie(moved[3], total)
    total = total + jnp.dot(moved[3], beta_tiles[3, EARLY:], preferred_element_type=jnp.float32)
    near, back = jnp.concatenate(nears, axis=1), jnp.concatenate(backs, axis=1)
    return total + (near + back.astype(jnp.float32))


def solution(mesh):
    placed = (P("alpha", "beta"), P(), P(), P(), P(None, None, "beta"))
    return jax.shard_map(
        per_device, mesh=mesh, in_specs=placed, out_specs=P("alpha", "beta"), check_vma=False
    )
```

time: 202 us -> 158 us (0.78)
  Pallas kernels: 41.9 us -> 15.2 us
  starting transfers between devices: 44.8 us -> 22.4 us
  waiting for transfers between devices: 103 us -> 106 us
    pallas_call x16 -> x8, Pallas kernels: 41.9 us -> 15.2 us  [the longest x3 9.36 us: couple(): pl.pallas_call(couple_kernel, in_specs=[SMEM] + [VMEM] * 3, out_specs=[VM...]
    ppermute x34 -> x18, starting transfers between devices: 31.9 us -> 20.5 us  [the longest x2 5.58 us: spread(): right = lax.ppermute(own, 'alpha', to_x(-1))]
    ppermute x5 -> x1, starting transfers between devices: 12.5 us -> 1.87 us  [per_device(): back = lax.ppermute(away, 'alpha', SWAP_Y)]
    add x0 -> x1, other arithmetic: none -> 2.17 us  [per_device(): return total + (near + back.astype(jnp.float32))]
    ppermute x34 -> x18, waiting for transfers between devices: 90.8 us -> 92.7 us  [the longest x6 47.1 us: hop(): return lax.ppermute(block, 'beta', RING)]
    ppermute x5 -> x1, waiting for transfers between devices: 11.8 us -> 13 us  [per_device(): back = lax.ppermute(away, 'alpha', SWAP_Y)]
    unnamed x29 -> x20, local copies, waits for them, and re-layouts: 4.8 us -> 5.94 us
  transfers between devices with their start and end apart: 44 -> 20, of which waited for: 23 -> 14; matrix products, arithmetic and copies ran while one was open for 3% -> 2% of each run, Pallas kernels for 19% -> 7%
where the time goes in v2:
time: 158 us; the launch traced here: 156 us
  waiting for transfers between devices  106 us (67%)
  starting transfers between devices  22.4 us (14%)
  Pallas kernels  15.2 us (10%)
  local copies, waits for them, and re-layouts  9 us (6%)
  other arithmetic  2.43 us (2%)
    ppermute x6, waiting for transfers between devices, hop(): return lax.ppermute(block, 'beta', RING)  47.1 us
    ppermute x2, waiting for transfers between devices, spread(): lax.ppermute(left[:AB], 'alpha', to_x(1))  17.4 us
    ppermute x1, waiting for transfers between devices, per_device(): backs.append(lax.ppermute(away, 'alpha', SWAP_Y))  13.1 us
    ppermute x1, waiting for transfers between devices, per_device(): back = lax.ppermute(away, 'alpha', SWAP_Y)  13 us
    ppermute x1, waiting for transfers between devices, per_device(): backs[k - 1] = lax.ppermute(away, 'alpha', SWAP_Y)  11.2 us
    pallas_call x3, Pallas kernels, couple(): pl.pallas_call(couple_kernel, in_specs=[SMEM] + [VMEM] * 3, out_specs=[VM...  9.36 us
    unnamed x20, local copies, waits for them, and re-layouts  5.94 us
    ppermute x2, starting transfers between devices, spread(): right = lax.ppermute(own, 'alpha', to_x(-1))  5.58 us
  transfers between devices with their start and end apart: 20, of which 14 were waited for; matrix products, arithmetic and copies ran while one was open for 2% of the time, Pallas kernels for 7%

profile of v2, /device:TPU:8, one launch (start us, length us, event | category | flops | bytes accessed | tf_op | source)
XLA Modules:
  0.0 155.9 jit_solution(15235727093837217946)
XLA Ops:
  0.0 1.0 slice.72.refs_0_
  1.0 2.0 %collective-permute-start.4 = (bf16[512,384]{1,0:T(8,128)(2,1)S(1)}, bf16[512,384]{1,0:T(8,128)(2,1)S(1)}, u32[]{:S(2)}, u32[]{:S(2)}) collective-permute-start(bf16[512,384]{1,0:T(8,128)(2,1)S(1)} %slice.72.refs_0_), channel_id=1, source_target_pairs={{0,1},{1,2},{2,3},{3,4},{4,5},{5,6},{6,7},{7,8},{8,9},{9,10},{10,1... | collective-permute-start | bytes 1179656 | tf_op jit(solution)/shard_map/ppermute | solution.py:173
  3.0 1.1 slice.69.refs_0_
  4.2 1.6 %collective-permute-start.1 = (bf16[512,640]{1,0:T(8,128)(2,1)S(1)}, bf16[512,640]{1,0:T(8,128)(2,1)S(1)}, u32[]{:S(2)}, u32[]{:S(2)}) collective-permute-start(bf16[512,640]{1,0:T(8,128)(2,1)S(1)} %slice.69.refs_0_), channel_id=1, source_target_pairs={{0,32},{16,48},{32,64},{48,80},{64,96},{80,112},{96,0},{112,16},{1... | collective-permute-start | bytes 1966088 | tf_op jit(solution)/shard_map/ppermute | solution.py:164
  5.7 1.7 %collective-permute-start = (bf16[512,640]{1,0:T(8,128)(2,1)S(1)}, bf16[512,640]{1,0:T(8,128)(2,1)S(1)}, u32[]{:S(2)}, u32[]{:S(2)}) collective-permute-start(bf16[512,640]{1,0:T(8,128)(2,1)S(1)} %slice.69.refs_0_), channel_id=1, source_target_pairs={{0,96},{16,112},{32,0},{48,16},{64,32},{80,48},{96,64},{112,80},{1... | collective-permute-start | bytes 1966088 | tf_op jit(solution)/shard_map/ppermute | solution.py:165
  7.5 8.5 %collective-permute-done.4.refs_1_ = bf16[512,384]{1,0:T(8,128)(2,1)S(1)} collective-permute-done((bf16[512,384]{1,0:T(8,128)(2,1)S(1)}, bf16[512,384]{1,0:T(8,128)(2,1)S(1)}, u32[]{:S(2)}, u32[]{:S(2)}) %collective-permute-start.4) | collective-permute-done | bytes 393248 | tf_op jit(solution)/shard_map/ppermute | solution.py:173
  16.0 0.0 collective-permute-start.5
  16.0 12.4 %collective-permute-done.5.refs_2_ = bf16[512,384]{1,0:T(8,128)(2,1)S(1)} collective-permute-done((bf16[512,384]{1,0:T(8,128)(2,1)S(1)}, bf16[512,384]{1,0:T(8,128)(2,1)S(1)}, u32[]{:S(2)}, u32[]{:S(2)}) %collective-permute-start.5) | collective-permute-done | bytes 393248 | tf_op jit(solution)/shard_map/ppermute | solution.py:173
  28.4 0.0 collective-permute-start.6
  28.4 0.0 collective-permute-done.1.refs_4_
  28.4 1.6 %collective-permute-start.2 = (bf16[256,640]{1,0:T(8,128)(2,1)S(1)}, bf16[256,640]{1,0:T(8,128)(2,1)S(1)}, u32[]{:S(2)}, u32[]{:S(2)}) collective-permute-start(bf16[256,640]{1,0:T(8,128)(2,1)S(1)} %slice.92), channel_id=1, source_target_pairs={{0,32},{16,48},{32,64},{48,80},{64,96},{80,112},{96,0},{112,16},{1... | collective-permute-start | bytes 983048 | tf_op jit(solution)/shard_map/ppermute | solution.py:167
  30.0 0.0 collective-permute-done.refs_1_
  30.0 0.0 copy-start.7
  30.1 0.0 copy-start.6
  30.1 1.8 %collective-permute-start.3 = (bf16[256,640]{1,0:T(8,128)(2,1)S(1)}, bf16[256,640]{1,0:T(8,128)(2,1)S(1)}, u32[]{:S(2)}, u32[]{:S(2)}) collective-permute-start(bf16[256,640]{1,0:T(8,128)(2,1)S(1)} %slice.93), channel_id=1, source_target_pairs={{0,96},{16,112},{32,0},{48,16},{64,32},{80,48},{96,64},{112,80},{1... | collective-permute-start | bytes 983048 | tf_op jit(solution)/shard_map/ppermute | solution.py:168
  31.9 5.8 %collective-permute-done.2.refs_2_ = bf16[256,640]{1,0:T(8,128)(2,1)S(1)} collective-permute-done((bf16[256,640]{1,0:T(8,128)(2,1)S(1)}, bf16[256,640]{1,0:T(8,128)(2,1)S(1)}, u32[]{:S(2)}, u32[]{:S(2)}) %collective-permute-start.2) | collective-permute-done | bytes 327712 | tf_op jit(solution)/shard_map/ppermute | solution.py:167
  37.7 0.1 collective-permute-done.3.refs_3_
  37.8 2.0 %collective-permute-done.6.refs_3_ = bf16[512,384]{1,0:T(8,128)(2,1)S(1)} collective-permute-done((bf16[512,384]{1,0:T(8,128)(2,1)S(1)}, bf16[512,384]{1,0:T(8,128)(2,1)S(1)}, u32[]{:S(2)}, u32[]{:S(2)}) %collective-permute-start.6) | collective-permute-done | bytes 393248 | tf_op jit(solution)/shard_map/ppermute | solution.py:173
  39.9 0.2 shard_map.55.mine
  40.1 0.5 copy-done.4
  40.6 0.0 collective-permute-start.7
  40.6 0.2 dynamic-slice_reduce_fusion.3
  40.9 0.3 dynamic-slice_reduce_fusion.1
  41.1 0.1 pad_add_fusion.codes
  41.2 3.4 %copy-done = bf16[4,1024,1024]{2,1,0:T(8,128)(2,1)S(1)} copy-done((bf16[4,1024,1024]{2,1,0:T(8,128)(2,1)S(1)}, bf16[4,1024,1024]{2,1,0:T(8,128)(2,1)}, u32[]{:S(2)}) %copy-start) | copy-done | bytes 8388632
  44.6 1.0 copy-done.3
  45.6 1.0 copy-done.5
  46.6 2.4 %shard_map.56 = bf16[512,1024]{1,0:T(8,128)(2,1)S(1)} custom-call(bf16[512,384]{1,0:T(8,128)(2,1)S(1)} %slice.72.refs_0_, bf16[512,384]{1,0:T(8,128)(2,1)S(1)} %collective-permute-done.4.refs_1_, bf16[512,384]{1,0:T(8,128)(2,1)S(1)} %copy-done.3, bf16[512,384]{1,0:T(8,128)(2,1)S(1)} %copy-done.5, bf16[4,1024,1024]{2,1,0:T(8,128)(2,1)S(1)} %copy-done), custom_call_target="tpu_custom_call" | custom-call | flops 1048576 | bytes 4096 | tf_op jit(solution)/shard_map/pallas_call | solution.py:145
  49.0 0.0 collective-permute-done.7.sib
  49.0 4.2 %shard_map.57 = (f32[512,640]{1,0:T(8,128)S(1)}, bf16[512,640]{1,0:T(8,128)(2,1)S(1)}) custom-call(s32[16]{0:T(128)S(1)} %pad_add_fusion.codes, bf16[8,256,256]{2,1,0:T(8,128)(2,1)S(1)} %copy-done.1, bf16[2048,640]{1,0:T(8,128)(2,1)S(1)} %shard_map.55.mine, bf16[2048,640]{1,0:T(8,128)(2,1)} %collective-permute-done.7.sib), custom_call_target="tpu_custom_call" | custom-call | flops 1048576 | bytes 4096 | tf_op jit(solution)/shard_map/pallas_call | solution.py:92
  53.2 1.9 %collective-permute-start.12 = (bf16[512,640]{1,0:T(8,128)(2,1)S(1)}, bf16[512,640]{1,0:T(8,128)(2,1)S(1)}, u32[]{:S(2)}, u32[]{:S(2)}) collective-permute-start(bf16[512,640]{1,0:T(8,128)(2,1)S(1)} %get-tuple-element.38), channel_id=1, source_target_pairs={{0,128},{16,144},{32,160},{48,176},{64,192},{80,208},{96,224},{112... | collective-permute-start | bytes 1966088 | tf_op jit(solution)/shard_map/ppermute | solution.py:186
  55.0 3.8 %collective-permute-start.8 = (bf16[512,1024]{1,0:T(8,128)(2,1)S(1)}, bf16[512,1024]{1,0:T(8,128)(2,1)S(1)}, u32[]{:S(2)}, u32[]{:S(2)}) collective-permute-start(bf16[512,1024]{1,0:T(8,128)(2,1)S(1)} %shard_map.56), channel_id=1, source_target_pairs={{0,96},{16,112},{32,0},{48,16},{64,32},{80,48},{96,64},{112,80},{1... | collective-permute-start | bytes 3145736 | tf_op jit(solution)/shard_map/ppermute | solution.py:165
  58.9 0.0 collective-permute-start.9
  58.9 13.0 %collective-permute-done.12 = bf16[512,640]{1,0:T(8,128)(2,1)S(1)} collective-permute-done((bf16[512,640]{1,0:T(8,128)(2,1)S(1)}, bf16[512,640]{1,0:T(8,128)(2,1)S(1)}, u32[]{:S(2)}, u32[]{:S(2)}) %collective-permute-start.12) | collective-permute-done | bytes 655392 | tf_op jit(solution)/shard_map/ppermute | solution.py:186
  71.9 0.2 add_convert_fusion.refs_0_
  72.1 0.1 collective-permute-start.13
  72.2 18.5 %collective-permute-done.13.refs_1_ = bf16[512,640]{1,0:T(8,128)(2,1)S(1)} collective-permute-done((bf16[512,640]{1,0:T(8,128)(2,1)S(1)}, bf16[512,640]{1,0:T(8,128)(2,1)S(1)}, u32[]{:S(2)}, u32[]{:S(2)}) %collective-permute-start.13) | collective-permute-done | bytes 655392 | tf_op jit(solution)/shard_map/ppermute | solution.py:173
  90.7 0.3 collective-permute-start.10
  91.0 0.0 collective-permute-done.8
  91.0 3.3 %collective-permute-start.11 = (bf16[256,1024]{1,0:T(8,128)(2,1)S(1)}, bf16[256,1024]{1,0:T(8,128)(2,1)S(1)}, u32[]{:S(2)}, u32[]{:S(2)}) collective-permute-start(bf16[256,1024]{1,0:T(8,128)(2,1)S(1)} %slice.95), channel_id=1, source_target_pairs={{0,96},{16,112},{32,0},{48,16},{64,32},{80,48},{96,64},{112,80},{1... | collective-permute-start | bytes 1572872 | tf_op jit(solution)/shard_map/ppermute | solution.py:168
  94.3 11.6 %collective-permute-done.10 = bf16[256,1024]{1,0:T(8,128)(2,1)S(1)} collective-permute-done((bf16[256,1024]{1,0:T(8,128)(2,1)S(1)}, bf16[256,1024]{1,0:T(8,128)(2,1)S(1)}, u32[]{:S(2)}, u32[]{:S(2)}) %collective-permute-start.10) | collective-permute-done | bytes 524320 | tf_op jit(solution)/shard_map/ppermute | solution.py:167
  105.9 0.0 collective-permute-done.11
  105.9 2.3 %collective-permute-done.14.refs_2_ = bf16[512,640]{1,0:T(8,128)(2,1)S(1)} collective-permute-done((bf16[512,640]{1,0:T(8,128)(2,1)S(1)}, bf16[512,640]{1,0:T(8,128)(2,1)S(1)}, u32[]{:S(2)}, u32[]{:S(2)}) %collective-permute-start.14) | collective-permute-done | bytes 655392 | tf_op jit(solution)/shard_map/ppermute | solution.py:173
  108.2 0.1 fusion.10
  108.3 0.1 fusion.9
  108.5 0.1 fusion.8
  108.5 0.0 slice-start
  108.6 0.1 shard_map.59.mine
  108.7 0.1 collective-permute-start.16
  108.8 0.1 shard_map.61.mine
  108.9 0.0 slice-start.1
  109.0 0.6 collective-permute-start.17
  109.5 3.4 %collective-permute-done.16.sib = bf16[2048,512]{1,0:T(8,128)(2,1)S(1)} collective-permute-done((bf16[2048,512]{1,0:T(8,128)(2,1)S(1)}, bf16[2048,512]{1,0:T(8,128)(2,1)S(1)}, u32[]{:S(2)}, u32[]{:S(2)}) %collective-permute-start.16) | collective-permute-done | bytes 2097184 | tf_op jit(solution)/shard_map/ppermute | solution.py:196
  112.9 2.6 %shard_map.60 = (f32[512,512]{1,0:T(8,128)S(1)}, bf16[512,512]{1,0:T(8,128)(2,1)S(1)}) custom-call(s32[16]{0:T(128)S(1)} %pad_add_fusion.codes, bf16[8,256,256]{2,1,0:T(8,128)(2,1)S(1)} %copy-done.1, bf16[2048,512]{1,0:T(8,128)(2,1)S(1)} %shard_map.59.mine, bf16[2048,512]{1,0:T(8,128)(2,1)S(1)} %collective-permute-done.16.sib), custom_call_target="tpu_custom_call" | custom-call | flops 1048576 | bytes 4096 | tf_op jit(solution)/shard_map/pallas_call | solution.py:92
  115.6 0.4 collective-permute-done.17.sib
  115.9 2.6 %shard_map.62 = (f32[512,512]{1,0:T(8,128)S(1)}, bf16[512,512]{1,0:T(8,128)(2,1)S(1)}) custom-call(s32[16]{0:T(128)S(1)} %pad_add_fusion.codes, bf16[8,256,256]{2,1,0:T(8,128)(2,1)S(1)} %copy-done.1, bf16[2048,512]{1,0:T(8,128)(2,1)S(1)} %shard_map.61.mine, bf16[2048,512]{1,0:T(8,128)(2,1)S(1)} %collective-permute-done.17.sib), custom_call_target="tpu_custom_call" | custom-call | flops 1048576 | bytes 4096 | tf_op jit(solution)/shard_map/pallas_call | solution.py:92
  118.6 2.5 %collective-permute-start.19 = (bf16[512,512]{1,0:T(8,128)(2,1)S(1)}, bf16[512,512]{1,0:T(8,128)(2,1)S(1)}, u32[]{:S(2)}, u32[]{:S(2)}) collective-permute-start(bf16[512,512]{1,0:T(8,128)(2,1)S(1)} %get-tuple-element.52), channel_id=1, source_target_pairs={{0,128},{16,144},{32,160},{48,176},{64,192},{80,208},{96,224},{112... | collective-permute-start | bytes 1572872 | tf_op jit(solution)/shard_map/ppermute | solution.py:204
  121.0 1.1 collective-permute-start.18
  122.2 2.9 %shard_map.58 = f32[512,1024]{1,0:T(8,128)S(1)} custom-call(bf16[512,640]{1,0:T(8,128)(2,1)S(1)} %add_convert_fusion.refs_0_, bf16[512,640]{1,0:T(8,128)(2,1)S(1)} %collective-permute-done.13.refs_1_, bf16[512,640]{1,0:T(8,128)(2,1)S(1)} %collective-permute-done.14.refs_2_, bf16[4,1024,1024]{2,1,0:T(8,128)(2,1)S(1)} %bitcast.21), custom_call_target="tpu_custom_call" | custom-call | flops 1048576 | bytes 4096 | tf_op jit(solution)/shard_map/pallas_call | solution.py:145
  125.1 3.4 %collective-permute-done.15 = bf16[512,640]{1,0:T(8,128)(2,1)S(1)} collective-permute-done((bf16[512,640]{1,0:T(8,128)(2,1)S(1)}, bf16[512,640]{1,0:T(8,128)(2,1)S(1)}, u32[]{:S(2)}, u32[]{:S(2)}) %collective-permute-start.15) | collective-permute-done | bytes 655392 | tf_op jit(solution)/shard_map/ppermute | solution.py:173
  128.5 1.0 fusion.1
  129.5 13.1 %collective-permute-done.19 = bf16[512,512]{1,0:T(8,128)(2,1)S(1)} collective-permute-done((bf16[512,512]{1,0:T(8,128)(2,1)S(1)}, bf16[512,512]{1,0:T(8,128)(2,1)S(1)}, u32[]{:S(2)}, u32[]{:S(2)}) %collective-permute-start.19) | collective-permute-done | bytes 524320 | tf_op jit(solution)/shard_map/ppermute | solution.py:204
  142.5 11.2 %collective-permute-done.18 = bf16[512,512]{1,0:T(8,128)(2,1)S(1)} collective-permute-done((bf16[512,512]{1,0:T(8,128)(2,1)S(1)}, bf16[512,512]{1,0:T(8,128)(2,1)S(1)}, u32[]{:S(2)}, u32[]{:S(2)}) %collective-permute-start.18) | collective-permute-done | bytes 524320 | tf_op jit(solution)/shard_map/ppermute | solution.py:201
  153.7 2.2 %fusion = f32[512,1024]{1,0:T(8,128)} fusion(f32[512,512]{1,0:T(8,128)S(1)} %get-tuple-element.50, f32[512,512]{1,0:T(8,128)S(1)} %get-tuple-element.47, f32[512,1024]{1,0:T(8,128)S(1)} %shard_map.58, f32[512,1024]{1,0:T(8,128)S(1)} %fusion.1, bf16[512,512]{1,0:T(8,128)(2,1)S(1)} %collective-permute-done.19, bf16[512,512]{1,0:T(8,128)(2,1)S(1)} %collective-permute-done.18), kind=kLoop, calls=%fused_computation.1 | loop fusion | flops 4194304 | bytes 9437184 | tf_op jit(solution)/shard_map/add | solution.py:210
  (24 shorter events, 0.3 us)
Async XLA Ops:
  1.0 14.9 %collective-permute-start.4 = (bf16[512,384]{1,0:T(8,128)(2,1)S(1)}, bf16[512,384]{1,0:T(8,128)(2,1)S(1)}, u32[]{:S(2)}, u32[]{:S(2)}) collective-permute-start(bf16[512,384]{1,0:T(8,128)(2,1)S(1)} %slice.72.refs_0_), channel_id=1, source_target_pairs={{0,1},{1,2},{2,3},{3,4},{4,5},{5,6},{6,7},{7,8},{8,9},{9,10},{10,1... | collective-permute-start | bytes 1179656 | tf_op jit(solution)/shard_map/ppermute | solution.py:173
  4.2 24.2 %collective-permute-start.1 = (bf16[512,640]{1,0:T(8,128)(2,1)S(1)}, bf16[512,640]{1,0:T(8,128)(2,1)S(1)}, u32[]{:S(2)}, u32[]{:S(2)}) collective-permute-start(bf16[512,640]{1,0:T(8,128)(2,1)S(1)} %slice.69.refs_0_), channel_id=1, source_target_pairs={{0,32},{16,48},{32,64},{48,80},{64,96},{80,112},{96,0},{112,16},{1... | collective-permute-start | bytes 1966088 | tf_op jit(solution)/shard_map/ppermute | solution.py:164
  5.7 24.3 %collective-permute-start = (bf16[512,640]{1,0:T(8,128)(2,1)S(1)}, bf16[512,640]{1,0:T(8,128)(2,1)S(1)}, u32[]{:S(2)}, u32[]{:S(2)}) collective-permute-start(bf16[512,640]{1,0:T(8,128)(2,1)S(1)} %slice.69.refs_0_), channel_id=1, source_target_pairs={{0,96},{16,112},{32,0},{48,16},{64,32},{80,48},{96,64},{112,80},{1... | collective-permute-start | bytes 1966088 | tf_op jit(solution)/shard_map/ppermute | solution.py:165
  16.0 12.4 %collective-permute-start.5 = (bf16[512,384]{1,0:T(8,128)(2,1)S(1)}, bf16[512,384]{1,0:T(8,128)(2,1)S(1)}, u32[]{:S(2)}, u32[]{:S(2)}) collective-permute-start(bf16[512,384]{1,0:T(8,128)(2,1)S(1)} %collective-permute-done.4.refs_1_), channel_id=1, source_target_pairs={{0,1},{1,2},{2,3},{3,4},{4,5},{5,6},{6,7},{7,8},{8,9},{9,10},{10,1... | collective-permute-start | bytes 1179656 | tf_op jit(solution)/shard_map/ppermute | solution.py:173
  28.4 11.7 %copy-start.2 = (bf16[512,384]{1,0:T(8,128)(2,1)}, bf16[512,384]{1,0:T(8,128)(2,1)S(1)}, u32[]{:S(2)}) copy-start(bf16[512,384]{1,0:T(8,128)(2,1)S(1)} %collective-permute-done.5.refs_2_) | copy-start | bytes 1179652
  28.4 11.5 %collective-permute-start.6 = (bf16[512,384]{1,0:T(8,128)(2,1)S(1)}, bf16[512,384]{1,0:T(8,128)(2,1)S(1)}, u32[]{:S(2)}, u32[]{:S(2)}) collective-permute-start(bf16[512,384]{1,0:T(8,128)(2,1)S(1)} %collective-permute-done.5.refs_2_), channel_id=1, source_target_pairs={{0,1},{1,2},{2,3},{3,4},{4,5},{5,6},{6,7},{7,8},{8,9},{9,10},{10,1... | collective-permute-start | bytes 1179656 | tf_op jit(solution)/shard_map/ppermute | solution.py:173
  28.4 9.3 %collective-permute-start.2 = (bf16[256,640]{1,0:T(8,128)(2,1)S(1)}, bf16[256,640]{1,0:T(8,128)(2,1)S(1)}, u32[]{:S(2)}, u32[]{:S(2)}) collective-permute-start(bf16[256,640]{1,0:T(8,128)(2,1)S(1)} %slice.92), channel_id=1, source_target_pairs={{0,32},{16,48},{32,64},{48,80},{64,96},{80,112},{96,0},{112,16},{1... | collective-permute-start | bytes 983048 | tf_op jit(solution)/shard_map/ppermute | solution.py:167
  30.0 10.6 %copy-start.7 = (s32[16,16]{1,0:T(8,128)S(1)}, s32[16,16]{1,0:T(8,128)}, u32[]{:S(2)}) copy-start(s32[16,16]{1,0:T(8,128)} %param.8) | copy-start | bytes 3076
  30.1 10.8 %copy-start.6 = (s32[16,16,3]{1,0,2:T(8,128)S(1)}, s32[16,16,3]{1,0,2:T(8,128)}, u32[]{:S(2)}) copy-start(s32[16,16,3]{1,0,2:T(8,128)} %param.7) | copy-start | bytes 9220
  30.1 7.8 %collective-permute-start.3 = (bf16[256,640]{1,0:T(8,128)(2,1)S(1)}, bf16[256,640]{1,0:T(8,128)(2,1)S(1)}, u32[]{:S(2)}, u32[]{:S(2)}) collective-permute-start(bf16[256,640]{1,0:T(8,128)(2,1)S(1)} %slice.93), channel_id=1, source_target_pairs={{0,96},{16,112},{32,0},{48,16},{64,32},{80,48},{96,64},{112,80},{1... | collective-permute-start | bytes 983048 | tf_op jit(solution)/shard_map/ppermute | solution.py:168
  39.9 0.7 copy-start.4
  40.6 8.4 %collective-permute-start.7 = (bf16[2048,640]{1,0:T(8,128)(2,1)S(1)}, bf16[2048,640]{1,0:T(8,128)(2,1)}, u32[]{:S(2)}, u32[]{:S(2)}) collective-permute-start(bf16[2048,640]{1,0:T(8,128)(2,1)S(1)} %shard_map.55.mine), channel_id=1, source_target_pairs={{0,16},{16,0},{32,48},{48,32},{64,80},{80,64},{96,112},{112,96},{1... | collective-permute-start | bytes 7864328 | tf_op jit(solution)/shard_map/ppermute | solution.py:182
  41.2 3.4 %copy-start = (bf16[4,1024,1024]{2,1,0:T(8,128)(2,1)S(1)}, bf16[4,1024,1024]{2,1,0:T(8,128)(2,1)}, u32[]{:S(2)}) copy-start(bf16[4,1024,1024]{2,1,0:T(8,128)(2,1)} %refs_3_.1) | copy-start | bytes 25165828
  44.6 1.0 copy-start.3
  45.6 1.0 copy-start.5
  46.6 2.4 %copy-start.1 = (bf16[8,256,256]{2,1,0:T(8,128)(2,1)S(1)}, bf16[8,256,256]{2,1,0:T(8,128)(2,1)}, u32[]{:S(2)}) copy-start(bf16[8,256,256]{2,1,0:T(8,128)(2,1)} %coup.5) | copy-start | bytes 3145732
  53.2 18.7 %collective-permute-start.12 = (bf16[512,640]{1,0:T(8,128)(2,1)S(1)}, bf16[512,640]{1,0:T(8,128)(2,1)S(1)}, u32[]{:S(2)}, u32[]{:S(2)}) collective-permute-start(bf16[512,640]{1,0:T(8,128)(2,1)S(1)} %get-tuple-element.38), channel_id=1, source_target_pairs={{0,128},{16,144},{32,160},{48,176},{64,192},{80,208},{96,224},{112... | collective-permute-start | bytes 1966088 | tf_op jit(solution)/shard_map/ppermute | solution.py:186
  55.0 35.9 %collective-permute-start.8 = (bf16[512,1024]{1,0:T(8,128)(2,1)S(1)}, bf16[512,1024]{1,0:T(8,128)(2,1)S(1)}, u32[]{:S(2)}, u32[]{:S(2)}) collective-permute-start(bf16[512,1024]{1,0:T(8,128)(2,1)S(1)} %shard_map.56), channel_id=1, source_target_pairs={{0,96},{16,112},{32,0},{48,16},{64,32},{80,48},{96,64},{112,80},{1... | collective-permute-start | bytes 3145736 | tf_op jit(solution)/shard_map/ppermute | solution.py:165
  58.9 31.8 %collective-permute-start.9 = (bf16[512,1024]{1,0:T(8,128)(2,1)S(1)}, bf16[512,1024]{1,0:T(8,128)(2,1)S(1)}, u32[]{:S(2)}, u32[]{:S(2)}) collective-permute-start(bf16[512,1024]{1,0:T(8,128)(2,1)S(1)} %shard_map.56), channel_id=1, source_target_pairs={{0,32},{16,48},{32,64},{48,80},{64,96},{80,112},{96,0},{112,16},{1... | collective-permute-start | bytes 3145736 | tf_op jit(solution)/shard_map/ppermute | solution.py:164
  72.1 18.6 %collective-permute-start.13 = (bf16[512,640]{1,0:T(8,128)(2,1)S(1)}, bf16[512,640]{1,0:T(8,128)(2,1)S(1)}, u32[]{:S(2)}, u32[]{:S(2)}) collective-permute-start(bf16[512,640]{1,0:T(8,128)(2,1)S(1)} %add_convert_fusion.refs_0_), channel_id=1, source_target_pairs={{0,1},{1,2},{2,3},{3,4},{4,5},{5,6},{6,7},{7,8},{8,9},{9,10},{10,1... | collective-permute-start | bytes 1966088 | tf_op jit(solution)/shard_map/ppermute | solution.py:173
  90.6 17.6 %collective-permute-start.14 = (bf16[512,640]{1,0:T(8,128)(2,1)S(1)}, bf16[512,640]{1,0:T(8,128)(2,1)S(1)}, u32[]{:S(2)}, u32[]{:S(2)}) collective-permute-start(bf16[512,640]{1,0:T(8,128)(2,1)S(1)} %collective-permute-done.13.refs_1_), channel_id=1, source_target_pairs={{0,1},{1,2},{2,3},{3,4},{4,5},{5,6},{6,7},{7,8},{8,9},{9,10},{10,1... | collective-permute-start | bytes 1966088 | tf_op jit(solution)/shard_map/ppermute | solution.py:173
  90.7 15.2 %collective-permute-start.10 = (bf16[256,1024]{1,0:T(8,128)(2,1)S(1)}, bf16[256,1024]{1,0:T(8,128)(2,1)S(1)}, u32[]{:S(2)}, u32[]{:S(2)}) collective-permute-start(bf16[256,1024]{1,0:T(8,128)(2,1)S(1)} %slice.94), channel_id=1, source_target_pairs={{0,32},{16,48},{32,64},{48,80},{64,96},{80,112},{96,0},{112,16},{1... | collective-permute-start | bytes 1572872 | tf_op jit(solution)/shard_map/ppermute | solution.py:167
  91.0 14.9 %collective-permute-start.11 = (bf16[256,1024]{1,0:T(8,128)(2,1)S(1)}, bf16[256,1024]{1,0:T(8,128)(2,1)S(1)}, u32[]{:S(2)}, u32[]{:S(2)}) collective-permute-start(bf16[256,1024]{1,0:T(8,128)(2,1)S(1)} %slice.95), channel_id=1, source_target_pairs={{0,96},{16,112},{32,0},{48,16},{64,32},{80,48},{96,64},{112,80},{1... | collective-permute-start | bytes 1572872 | tf_op jit(solution)/shard_map/ppermute | solution.py:168
  108.5 13.6 %slice-start = ((s8[8388608]{0:T(1024)(128)(4,1)}), s8[4194304]{0:T(1024)(128)(4,1)S(1)}, s32[]{:S(2)}) async-start(s8[8388608]{0:T(1024)(128)(4,1)} %bitcast.20), calls=%async_computation | async-start | bytes 8388608
  108.7 4.2 %collective-permute-start.16 = (bf16[2048,512]{1,0:T(8,128)(2,1)S(1)}, bf16[2048,512]{1,0:T(8,128)(2,1)S(1)}, u32[]{:S(2)}, u32[]{:S(2)}) collective-permute-start(bf16[2048,512]{1,0:T(8,128)(2,1)S(1)} %shard_map.59.mine), channel_id=1, source_target_pairs={{0,16},{16,0},{32,48},{48,32},{64,80},{80,64},{96,112},{112,96},{1... | collective-permute-start | bytes 6291464 | tf_op jit(solution)/shard_map/ppermute | solution.py:196
  108.9 13.2 %slice-start.1 = ((s8[8388608]{0:T(1024)(128)(4,1)}), s8[4194304]{0:T(1024)(128)(4,1)S(1)}, s32[]{:S(2)}) async-start(s8[8388608]{0:T(1024)(128)(4,1)} %bitcast.20), calls=%async_computation.1 | async-start | bytes 8388608
  109.0 7.0 %collective-permute-start.17 = (bf16[2048,512]{1,0:T(8,128)(2,1)S(1)}, bf16[2048,512]{1,0:T(8,128)(2,1)S(1)}, u32[]{:S(2)}, u32[]{:S(2)}) collective-permute-start(bf16[2048,512]{1,0:T(8,128)(2,1)S(1)} %shard_map.61.mine), channel_id=1, source_target_pairs={{0,16},{16,0},{32,48},{48,32},{64,80},{80,64},{96,112},{112,96},{1... | collective-permute-start | bytes 6291464 | tf_op jit(solution)/shard_map/ppermute | solution.py:196
  109.5 18.9 %collective-permute-start.15 = (bf16[512,640]{1,0:T(8,128)(2,1)S(1)}, bf16[512,640]{1,0:T(8,128)(2,1)S(1)}, u32[]{:S(2)}, u32[]{:S(2)}) collective-permute-start(bf16[512,640]{1,0:T(8,128)(2,1)S(1)} %collective-permute-done.14.refs_2_), channel_id=1, source_target_pairs={{0,1},{1,2},{2,3},{3,4},{4,5},{5,6},{6,7},{7,8},{8,9},{9,10},{10,1... | collective-permute-start | bytes 1966088 | tf_op jit(solution)/shard_map/ppermute | solution.py:173
  118.6 24.0 %collective-permute-start.19 = (bf16[512,512]{1,0:T(8,128)(2,1)S(1)}, bf16[512,512]{1,0:T(8,128)(2,1)S(1)}, u32[]{:S(2)}, u32[]{:S(2)}) collective-permute-start(bf16[512,512]{1,0:T(8,128)(2,1)S(1)} %get-tuple-element.52), channel_id=1, source_target_pairs={{0,128},{16,144},{32,160},{48,176},{64,192},{80,208},{96,224},{112... | collective-permute-start | bytes 1572872 | tf_op jit(solution)/shard_map/ppermute | solution.py:204
  121.0 32.7 %collective-permute-start.18 = (bf16[512,512]{1,0:T(8,128)(2,1)S(1)}, bf16[512,512]{1,0:T(8,128)(2,1)S(1)}, u32[]{:S(2)}, u32[]{:S(2)}) collective-permute-start(bf16[512,512]{1,0:T(8,128)(2,1)S(1)} %get-tuple-element.51), channel_id=1, source_target_pairs={{0,128},{16,144},{32,160},{48,176},{64,192},{80,208},{96,224},{112... | collective-permute-start | bytes 1572872 | tf_op jit(solution)/shard_map/ppermute | solution.py:201

commit v3 on v2

--- a/solution.py
+++ b/solution.py
@@ -13,7 +13,7 @@
 NX = 4
 NZ = 8
 ROWS = ABLK * AB
-EARLY = 384
+EARLY = 512
 PARTS = 2
 COLUMN_TILE = 256
 
@@ -81,8 +81,13 @@
                 def _():
                     kind, goal, source = code // 4, (code // 2) % 2, code % 2
                     rows = pl.ds(pl.multiple_of(goal * AB, AB), AB)
-                    block = stack[pl.ds(pl.multiple_of(step * ROWS + source * AB, AB), AB), :]
-                    total[rows, :] += jnp.dot(coup[kind], block, preferred_element_type=jnp.float32)
+                    taken = pl.ds(pl.multiple_of(step * ROWS + source * AB, AB), AB)
+                    matrix = coup[kind]
+                    for column in range(0, stack.shape[1], COLUMN_TILE):
+                        span = slice(column, min(column + COLUMN_TILE, stack.shape[1]))
+                        total[rows, span] += jnp.dot(
+                            matrix, stack[taken, span], preferred_element_type=jnp.float32
+                        )
 
     away[...] = acc[...].astype(away.dtype)
 
@@ -123,34 +128,8 @@
     )(*blocks)
 
 
-def band_kernel(pieces, first, *refs):
-    n = len(pieces)
-    blocks, tiles = refs[:n], refs[n]
-    before, out = (None, refs[n + 1]) if first else refs[n + 1 :]
-
-    @pl.loop(0, tiles.shape[2], step=COLUMN_TILE)
-    def _(column):
-        span = pl.ds(pl.multiple_of(column, COLUMN_TILE), COLUMN_TILE)
-        left = jnp.concatenate([block[...] for block in blocks], axis=1)
-        right = jnp.concatenate([tiles[d, s : s + w, span] for d, s, w in pieces], axis=0)
-        part = jnp.dot(left, right, preferred_element_type=jnp.float32)
-        if not first:
-            part = before[:, span] + part
-        out[:, span] = part.astype(out.dtype)
-
-
-def band(total, tiles, blocks, pieces, kind=jnp.float32):
-    first = total is None
-    arrays = list(blocks) + [tiles] + ([] if first else [total])
-    return pl.pallas_call(
-        functools.partial(band_kernel, tuple(pieces), first),
-        in_specs=[VMEM] * len(arrays),
-        out_specs=VMEM,
-        out_shape=jax.ShapeDtypeStruct((ROWS, tiles.shape[2]), kind),
-        input_output_aliases={} if first else {len(arrays) - 1: 0},
-        cost_estimate=COST,
-        compiler_params=pltpu.CompilerParams(vmem_limit_bytes=12 << 20),
-    )(*arrays)
+def product(block, tile):
+    return jnp.dot(block, tile, preferred_element_type=jnp.float32)
 
 
 def tie(*values):
@@ -173,39 +152,47 @@
         return lax.ppermute(block, "beta", RING)
 
     cols = coefficients.shape[1]
-    early = [coefficients[:, :EARLY]]
-    for _ in range(STOPS - 1):
-        early.append(hop(early[-1]))
+    early = coefficients[:, :EARLY]
+    arrived = hop(early)
+    mixed = product(early, beta_tiles[0, :EARLY])
     parts = spread(coefficients[:, EARLY:])
-    *parts, early[3] = tie(*parts, early[3])
+    for d in range(1, STOPS - 1):
+        arrived, mixed = tie(arrived, mixed)
+        early, arrived = arrived, hop(arrived)
+        if d < STOPS - 2:
+            mixed = mixed + product(early, beta_tiles[d, :EARLY])
+    *parts, mixed, early = tie(*parts, mixed, early)
     mine = stack(parts)
     sib = lax.ppermute(mine, "alpha", SWAP_CORE)
-    mixed = band(None, beta_tiles, early, [(d, 0, EARLY) for d in range(STOPS)], jnp.bfloat16)
-    sib, mixed = tie(sib, mixed)
     near, away = couple(codes, couplings, mine, sib)
+    early, mixed, _ = tie(early, mixed, away)
+    mixed = mixed + product(early, beta_tiles[STOPS - 2, :EARLY])
+    arrived, mixed = tie(arrived, mixed)
+    mixed = (mixed + product(arrived, beta_tiles[STOPS - 1, :EARLY])).astype(jnp.bfloat16)
     back = lax.ppermute(away, "alpha", SWAP_Y)
     moved = [(near + back.astype(jnp.float32)).astype(jnp.bfloat16)]
 
     parts = spread(mixed)
     moved.append(hop(moved[0]))
+    total = product(moved[0], beta_tiles[0, EARLY:])
+    moved[1], parts[1], parts[4], total = tie(moved[1], parts[1], parts[4], total)
     moved.append(hop(moved[1]))
-    *parts, moved[2] = tie(*parts, moved[2])
-    moved.append(hop(moved[2]))
-    half = cols // PARTS
+    *parts, _ = tie(*parts, moved[2])
+    half = coefficients.shape[1] // PARTS
     mines = [stack([p[:, k * half : (k + 1) * half] for p in parts]) for k in range(PARTS)]
     sibs = [lax.ppermute(m, "alpha", SWAP_CORE) for m in mines]
     nears, backs = [], []
     for k in range(PARTS):
         if k:
-            sibs[k], away = tie(sibs[k], away)
-            backs[k - 1] = lax.ppermute(away, "alpha", SWAP_Y)
+            sibs[k] = after(sibs[k], away)
         near, away = couple(codes, couplings, mines[k], sibs[k])
         nears.append(near)
         backs.append(lax.ppermute(away, "alpha", SWAP_Y))
-    width = cols - EARLY
-    total = band(None, beta_tiles, moved[:3], [(d, EARLY, width) for d in range(3)])
+    total = total + product(moved[1], beta_tiles[1, EARLY:])
+    moved.append(hop(moved[2]))
+    total = total + product(moved[2], beta_tiles[2, EARLY:])
     moved[3], total = tie(moved[3], total)
-    total = total + jnp.dot(moved[3], beta_tiles[3, EARLY:], preferred_element_type=jnp.float32)
+    total = total + product(moved[3], beta_tiles[3, EARLY:])
     near, back = jnp.concatenate(nears, axis=1), jnp.concatenate(backs, axis=1)
     return total + (near + back.astype(jnp.float32))
 

time: 158 us -> 143 us (0.905)
  waiting for transfers between devices: 106 us -> 87.5 us
  matrix products: 0.98 us -> 9.48 us
  local copies, waits for them, and re-layouts: 9 us -> 2.91 us
  other arithmetic: 2.43 us -> 5.17 us
  Pallas kernels: 15.2 us -> 13.5 us
    ppermute x2, waiting for transfers between devices: 17.4 us -> 0.01 us  [spread(): lax.ppermute(left[:AB], 'alpha', to_x(1))]
    ppermute x1 -> x0, waiting for transfers between devices: 11.2 us -> none  [per_device(): backs[k - 1] = lax.ppermute(away, 'alpha', SWAP_Y)]
    ppermute x1 -> x2, waiting for transfers between devices: 13.1 us -> 23.3 us  [per_device(): backs.append(lax.ppermute(away, 'alpha', SWAP_Y))]
    dot_general x1 -> x8, matrix products: 0.98 us -> 9.48 us  [product(): return jnp.dot(block, tile, preferred_element_type=jnp.float32)]
    pallas_call x2 -> x0, Pallas kernels: 5.31 us -> none  [band(): pl.pallas_call(functools.partial(band_kernel, tuple(pieces), first), in_s...]
    unnamed x20 -> x18, local copies, waits for them, and re-layouts: 5.94 us -> 0.69 us
    ppermute x1, waiting for transfers between devices: 13 us -> 8.88 us  [per_device(): back = lax.ppermute(away, 'alpha', SWAP_Y)]
    pallas_call x3, Pallas kernels: 9.36 us -> 13.1 us  [couple(): pl.pallas_call(couple_kernel, in_specs=[SMEM] + [VMEM] * 3, out_specs=[VM...]
  transfers between devices with their start and end apart: 20 -> 20, of which waited for: 14 -> 11; matrix products, arithmetic and copies ran while one was open for 2% -> 9% of each run, Pallas kernels for 7% -> 9%
where the time goes in v3:
time: 143 us; the launch traced here: 140 us
  waiting for transfers between devices  87.5 us (61%)
  starting transfers between devices  21.6 us (15%)
  Pallas kernels  13.5 us (9%)
  matrix products  9.48 us (7%)
  other arithmetic  5.17 us (4%)
  local copies, waits for them, and re-layouts  2.91 us (2%)
    ppermute x6, waiting for transfers between devices, hop(): return lax.ppermute(block, 'beta', RING)  48.3 us
    ppermute x2, waiting for transfers between devices, per_device(): backs.append(lax.ppermute(away, 'alpha', SWAP_Y))  23.3 us
    pallas_call x3, Pallas kernels, couple(): pl.pallas_call(couple_kernel, in_specs=[SMEM] + [VMEM] * 3, out_specs=[VM...  13.1 us
    dot_general x8, matrix products, product(): return jnp.dot(block, tile, preferred_element_type=jnp.float32)  9.48 us
    ppermute x1, waiting for transfers between devices, per_device(): back = lax.ppermute(away, 'alpha', SWAP_Y)  8.88 us
    ppermute x2, starting transfers between devices, spread(): right = lax.ppermute(own, 'alpha', to_x(-1))  4.58 us
    ppermute x2, starting transfers between devices, spread(): lax.ppermute(right[AB:], 'alpha', to_x(-1))  4.14 us
    ppermute x1, waiting for transfers between devices, per_device(): sib = lax.ppermute(mine, 'alpha', SWAP_CORE)  3.6 us
  transfers between devices with their start and end apart: 20, of which 11 were waited for; matrix products, arithmetic and copies ran while one was open for 9% of the time, Pallas kernels for 9%

profile of v3, /device:TPU:8, one launch (start us, length us, event | category | flops | bytes accessed | tf_op | source)
XLA Modules:
  0.0 140.4 jit_solution(1717974263871705091)
XLA Ops:
  0.0 1.4 fusion.35
  1.4 2.0 %collective-permute-start.4 = (bf16[512,512]{1,0:T(8,128)(2,1)S(1)}, bf16[512,512]{1,0:T(8,128)(2,1)S(1)}, u32[]{:S(2)}, u32[]{:S(2)}) collective-permute-start(bf16[512,512]{1,0:T(8,128)(2,1)S(1)} %get-tuple-element.82), channel_id=1, source_target_pairs={{0,1},{1,2},{2,3},{3,4},{4,5},{5,6},{6,7},{7,8},{8,9},{9,10},{10,1... | collective-permute-start | bytes 1572872 | tf_op jit(solution)/shard_map/ppermute | solution.py:152
  3.4 1.5 %collective-permute-start.1 = (bf16[512,512]{1,0:T(8,128)(2,1)S(1)}, bf16[512,512]{1,0:T(8,128)(2,1)S(1)}, u32[]{:S(2)}, u32[]{:S(2)}) collective-permute-start(bf16[512,512]{1,0:T(8,128)(2,1)S(1)} %get-tuple-element.42.refs_0_), channel_id=1, source_target_pairs={{0,32},{16,48},{32,64},{48,80},{64,96},{80,112},{96,0},{112,16},{1... | collective-permute-start | bytes 1572872 | tf_op jit(solution)/shard_map/ppermute | solution.py:143
  4.8 1.7 %collective-permute-start = (bf16[512,512]{1,0:T(8,128)(2,1)S(1)}, bf16[512,512]{1,0:T(8,128)(2,1)S(1)}, u32[]{:S(2)}, u32[]{:S(2)}) collective-permute-start(bf16[512,512]{1,0:T(8,128)(2,1)S(1)} %get-tuple-element.42.refs_0_), channel_id=1, source_target_pairs={{0,96},{16,112},{32,0},{48,16},{64,32},{80,48},{96,64},{112,80},{1... | collective-permute-start | bytes 1572872 | tf_op jit(solution)/shard_map/ppermute | solution.py:144
  6.6 1.9 %fusion.17 = f32[512,1024]{1,0:T(8,128)S(1)} fusion(bf16[4,1024,1024]{2,1,0:T(8,128)(2,1)} %param.9, bf16[512,1024]{1,0:T(8,128)(2,1)S(1)} %copy-done.2), kind=kOutput, calls=%fused_computation.18 | convolution fusion | flops 536870912 | bytes 3670016 | tf_op jit(solution)/shard_map/dot_general | solution.py:132
  8.5 10.6 %collective-permute-done.4 = bf16[512,512]{1,0:T(8,128)(2,1)S(1)} collective-permute-done((bf16[512,512]{1,0:T(8,128)(2,1)S(1)}, bf16[512,512]{1,0:T(8,128)(2,1)S(1)}, u32[]{:S(2)}, u32[]{:S(2)}) %collective-permute-start.4) | collective-permute-done | bytes 524320 | tf_op jit(solution)/shard_map/ppermute | solution.py:152
  19.1 0.0 collective-permute-start.5
  19.1 0.0 collective-permute-done.1.refs_4_
  19.1 1.6 %collective-permute-start.2 = (bf16[256,512]{1,0:T(8,128)(2,1)S(1)}, bf16[256,512]{1,0:T(8,128)(2,1)S(1)}, u32[]{:S(2)}, u32[]{:S(2)}) collective-permute-start(bf16[256,512]{1,0:T(8,128)(2,1)S(1)} %slice.120), channel_id=1, source_target_pairs={{0,32},{16,48},{32,64},{48,80},{64,96},{80,112},{96,0},{112,16},{1... | collective-permute-start | bytes 786440 | tf_op jit(solution)/shard_map/ppermute | solution.py:146
  20.7 0.0 collective-permute-done.refs_1_
  20.7 1.8 %collective-permute-start.3 = (bf16[256,512]{1,0:T(8,128)(2,1)S(1)}, bf16[256,512]{1,0:T(8,128)(2,1)S(1)}, u32[]{:S(2)}, u32[]{:S(2)}) collective-permute-start(bf16[256,512]{1,0:T(8,128)(2,1)S(1)} %slice.121), channel_id=1, source_target_pairs={{0,96},{16,112},{32,0},{48,16},{64,32},{80,48},{96,64},{112,80},{1... | collective-permute-start | bytes 786440 | tf_op jit(solution)/shard_map/ppermute | solution.py:147
  22.6 1.9 %fusion.15 = f32[512,1024]{1,0:T(8,128)S(1)} fusion(bf16[512,512]{1,0:T(8,128)(2,1)S(1)} %collective-permute-done.4, bf16[4,1024,1024]{2,1,0:T(8,128)(2,1)} %param.9), kind=kOutput, calls=%fused_computation.16 | convolution fusion | flops 536870912 | bytes 3670016 | tf_op jit(solution)/shard_map/dot_general | solution.py:132
  24.5 1.7 %add.88 = f32[512,1024]{1,0:T(8,128)} add(f32[512,1024]{1,0:T(8,128)S(1)} %fusion.17, f32[512,1024]{1,0:T(8,128)S(1)} %fusion.15) | non-fusion elementwise | flops 524288 | bytes 6291456 | tf_op jit(solution)/shard_map/add | solution.py:163
  26.2 8.1 %collective-permute-done.5 = bf16[512,512]{1,0:T(8,128)(2,1)S(1)} collective-permute-done((bf16[512,512]{1,0:T(8,128)(2,1)S(1)}, bf16[512,512]{1,0:T(8,128)(2,1)S(1)}, u32[]{:S(2)}, u32[]{:S(2)}) %collective-permute-start.5) | collective-permute-done | bytes 524320 | tf_op jit(solution)/shard_map/ppermute | solution.py:152
  34.3 0.1 shard_map.55.mine
  34.5 0.7 copy-done.3
  35.2 0.2 dynamic-slice_reduce_fusion.3
  35.4 0.3 dynamic-slice_reduce_fusion.1
  35.6 0.1 collective-permute-start.9
  35.7 0.1 pad_add_fusion.codes
  35.8 3.6 %collective-permute-done.6.sib = bf16[2048,512]{1,0:T(8,128)(2,1)} collective-permute-done((bf16[2048,512]{1,0:T(8,128)(2,1)S(1)}, bf16[2048,512]{1,0:T(8,128)(2,1)}, u32[]{:S(2)}, u32[]{:S(2)}) %collective-permute-start.6) | collective-permute-done | bytes 2097184 | tf_op jit(solution)/shard_map/ppermute | solution.py:166
  39.4 5.2 %shard_map.56 = (f32[512,512]{1,0:T(8,128)S(1)}, bf16[512,512]{1,0:T(8,128)(2,1)S(1)}) custom-call(s32[16]{0:T(128)S(1)} %pad_add_fusion.codes, bf16[8,256,256]{2,1,0:T(8,128)(2,1)S(1)} %copy-done, bf16[2048,512]{1,0:T(8,128)(2,1)S(1)} %shard_map.55.mine, bf16[2048,512]{1,0:T(8,128)(2,1)} %collective-permute-done.6.sib), custom_call_target="tpu_custom_call" | custom-call | flops 1048576 | bytes 4096 | tf_op jit(solution)/shard_map/pallas_call | solution.py:97
  44.6 0.0 copy-start.1
  44.6 0.0 slice-start.1
  44.6 2.4 %collective-permute-start.7 = (bf16[512,512]{1,0:T(8,128)(2,1)S(1)}, bf16[512,512]{1,0:T(8,128)(2,1)S(1)}, u32[]{:S(2)}, u32[]{:S(2)}) collective-permute-start(bf16[512,512]{1,0:T(8,128)(2,1)S(1)} %get-tuple-element.48), channel_id=1, source_target_pairs={{0,128},{16,144},{32,160},{48,176},{64,192},{80,208},{96,224},{112... | collective-permute-start | bytes 1572872 | tf_op jit(solution)/shard_map/ppermute | solution.py:172
  47.1 2.0 %fusion.13 = f32[512,1024]{1,0:T(8,128)S(1)} fusion(bf16[512,512]{1,0:T(8,128)(2,1)S(1)} %copy-done.4, bf16[4,1024,1024]{2,1,0:T(8,128)(2,1)} %param.9), kind=kOutput, calls=%fused_computation.14 | convolution fusion | flops 536870912 | bytes 3670016 | tf_op jit(solution)/shard_map/dot_general | solution.py:132
  49.1 0.6 add.90
  49.6 2.8 %collective-permute-done.9 = bf16[512,512]{1,0:T(8,128)(2,1)S(1)} collective-permute-done((bf16[512,512]{1,0:T(8,128)(2,1)}, bf16[512,512]{1,0:T(8,128)(2,1)S(1)}, u32[]{:S(2)}, u32[]{:S(2)}) %collective-permute-start.9) | collective-permute-done | bytes 524320 | tf_op jit(solution)/shard_map/ppermute | solution.py:152
  52.5 0.7 fusion.11
  53.2 0.5 add_convert_fusion
  53.7 2.8 %collective-permute-start.10 = (bf16[512,1024]{1,0:T(8,128)(2,1)S(1)}, bf16[512,1024]{1,0:T(8,128)(2,1)S(1)}, u32[]{:S(2)}, u32[]{:S(2)}) collective-permute-start(bf16[512,1024]{1,0:T(8,128)(2,1)S(1)} %add_convert_fusion), channel_id=1, source_target_pairs={{0,96},{16,112},{32,0},{48,16},{64,32},{80,48},{96,64},{112,80},{1... | collective-permute-start | bytes 3145736 | tf_op jit(solution)/shard_map/ppermute | solution.py:144
  56.6 0.0 collective-permute-start.11
  56.6 8.9 %collective-permute-done.7 = bf16[512,512]{1,0:T(8,128)(2,1)S(1)} collective-permute-done((bf16[512,512]{1,0:T(8,128)(2,1)S(1)}, bf16[512,512]{1,0:T(8,128)(2,1)S(1)}, u32[]{:S(2)}, u32[]{:S(2)}) %collective-permute-start.7) | collective-permute-done | bytes 524320 | tf_op jit(solution)/shard_map/ppermute | solution.py:172
  65.4 0.2 add_convert_fusion.1
  65.6 0.1 collective-permute-start.8
  65.7 0.7 fusion.9
  66.4 15.2 %collective-permute-done.8 = bf16[512,512]{1,0:T(8,128)(2,1)S(1)} collective-permute-done((bf16[512,512]{1,0:T(8,128)(2,1)S(1)}, bf16[512,512]{1,0:T(8,128)(2,1)S(1)}, u32[]{:S(2)}, u32[]{:S(2)}) %collective-permute-start.8) | collective-permute-done | bytes 524320 | tf_op jit(solution)/shard_map/ppermute | solution.py:152
  81.6 0.0 collective-permute-done.10
  81.7 0.6 collective-permute-done.11
  82.3 1.1 collective-permute-start.14
  83.4 2.3 %collective-permute-start.15 = (bf16[256,1024]{1,0:T(8,128)(2,1)S(1)}, bf16[256,1024]{1,0:T(8,128)(2,1)S(1)}, u32[]{:S(2)}, u32[]{:S(2)}) collective-permute-start(bf16[256,1024]{1,0:T(8,128)(2,1)S(1)} %slice.123), channel_id=1, source_target_pairs={{0,96},{16,112},{32,0},{48,16},{64,32},{80,48},{96,64},{112,80},{1... | collective-permute-start | bytes 1572872 | tf_op jit(solution)/shard_map/ppermute | solution.py:147
  85.7 11.1 %collective-permute-done.12 = bf16[512,512]{1,0:T(8,128)(2,1)S(1)} collective-permute-done((bf16[512,512]{1,0:T(8,128)(2,1)S(1)}, bf16[512,512]{1,0:T(8,128)(2,1)S(1)}, u32[]{:S(2)}, u32[]{:S(2)}) %collective-permute-start.12) | collective-permute-done | bytes 524320 | tf_op jit(solution)/shard_map/ppermute | solution.py:152
  96.8 0.0 collective-permute-done.14
  96.8 0.0 collective-permute-done.15
  96.8 0.1 fusion.32
  96.8 0.1 fusion.33
  96.9 0.1 fusion.34
  97.1 0.1 shard_map.57.mine
  97.2 0.1 collective-permute-start.16
  97.3 0.1 shard_map.59.mine
  97.5 0.6 collective-permute-start.17
  98.1 0.0 collective-permute-start.13
  98.1 0.7 fusion.7
  98.8 2.7 %collective-permute-done.16.sib = bf16[2048,512]{1,0:T(8,128)(2,1)S(1)} collective-permute-done((bf16[2048,512]{1,0:T(8,128)(2,1)S(1)}, bf16[2048,512]{1,0:T(8,128)(2,1)S(1)}, u32[]{:S(2)}, u32[]{:S(2)}) %collective-permute-start.16) | collective-permute-done | bytes 2097184 | tf_op jit(solution)/shard_map/ppermute | solution.py:183
  101.5 4.0 %shard_map.58 = (f32[512,512]{1,0:T(8,128)S(1)}, bf16[512,512]{1,0:T(8,128)(2,1)S(1)}) custom-call(s32[16]{0:T(128)S(1)} %pad_add_fusion.codes, bf16[8,256,256]{2,1,0:T(8,128)(2,1)S(1)} %copy-done, bf16[2048,512]{1,0:T(8,128)(2,1)S(1)} %shard_map.57.mine, bf16[2048,512]{1,0:T(8,128)(2,1)S(1)} %collective-permute-done.16.sib), custom_call_target="tpu_custom_call" | custom-call | flops 1048576 | bytes 4096 | tf_op jit(solution)/shard_map/pallas_call | solution.py:97
  105.5 2.3 %collective-permute-start.18 = (bf16[512,512]{1,0:T(8,128)(2,1)S(1)}, bf16[512,512]{1,0:T(8,128)(2,1)S(1)}, u32[]{:S(2)}, u32[]{:S(2)}) collective-permute-start(bf16[512,512]{1,0:T(8,128)(2,1)S(1)} %get-tuple-element.67), channel_id=1, source_target_pairs={{0,128},{16,144},{32,160},{48,176},{64,192},{80,208},{96,224},{112... | collective-permute-start | bytes 1572872 | tf_op jit(solution)/shard_map/ppermute | solution.py:190
  107.8 0.0 collective-permute-done.17.sib
  107.8 4.0 %shard_map.60 = (f32[512,512]{1,0:T(8,128)S(1)}, bf16[512,512]{1,0:T(8,128)(2,1)S(1)}) custom-call(s32[16]{0:T(128)S(1)} %pad_add_fusion.codes, bf16[8,256,256]{2,1,0:T(8,128)(2,1)S(1)} %copy-done, bf16[2048,512]{1,0:T(8,128)(2,1)S(1)} %shard_map.59.mine, bf16[2048,512]{1,0:T(8,128)(2,1)S(1)} %collective-permute-done.17.sib), custom_call_target="tpu_custom_call" | custom-call | flops 1048576 | bytes 4096 | tf_op jit(solution)/shard_map/pallas_call | solution.py:97
  111.7 1.2 collective-permute-start.19
  112.9 0.8 add_add_fusion
  113.7 0.5 collective-permute-done.13
  114.2 0.7 fusion.1
  114.9 23.3 %collective-permute-done.19 = bf16[512,512]{1,0:T(8,128)(2,1)S(1)} collective-permute-done((bf16[512,512]{1,0:T(8,128)(2,1)S(1)}, bf16[512,512]{1,0:T(8,128)(2,1)S(1)}, u32[]{:S(2)}, u32[]{:S(2)}) %collective-permute-start.19) | collective-permute-done | bytes 524320 | tf_op jit(solution)/shard_map/ppermute | solution.py:190
  138.3 2.1 %fusion = f32[512,1024]{1,0:T(8,128)} fusion(f32[512,512]{1,0:T(8,128)S(1)} %get-tuple-element.69, f32[512,512]{1,0:T(8,128)S(1)} %get-tuple-element.66, f32[512,1024]{1,0:T(8,128)S(1)} %add_add_fusion, f32[512,1024]{1,0:T(8,128)S(1)} %fusion.1, bf16[512,512]{1,0:T(8,128)(2,1)S(1)} %collective-permute-done.19, bf16[512,512]{1,0:T(8,128)(2,1)S(1)} %collective-permute-done.18), kind=kLoop, calls=%fused_computation.1 | loop fusion | flops 4194304 | bytes 9437184 | tf_op jit(solution)/shard_map/add | solution.py:197
  (29 shorter events, 0.2 us)
Async XLA Ops:
  0.0 6.6 %copy-start.2 = (bf16[512,1024]{1,0:T(8,128)(2,1)S(1)}, bf16[512,1024]{1,0:T(8,128)(2,1)}, u32[]{:S(2)}) copy-start(bf16[512,1024]{1,0:T(8,128)(2,1)} %param.5) | copy-start | bytes 3145732
  1.4 17.7 %collective-permute-start.4 = (bf16[512,512]{1,0:T(8,128)(2,1)S(1)}, bf16[512,512]{1,0:T(8,128)(2,1)S(1)}, u32[]{:S(2)}, u32[]{:S(2)}) collective-permute-start(bf16[512,512]{1,0:T(8,128)(2,1)S(1)} %get-tuple-element.82), channel_id=1, source_target_pairs={{0,1},{1,2},{2,3},{3,4},{4,5},{5,6},{6,7},{7,8},{8,9},{9,10},{10,1... | collective-permute-start | bytes 1572872 | tf_op jit(solution)/shard_map/ppermute | solution.py:152
  3.4 15.8 %collective-permute-start.1 = (bf16[512,512]{1,0:T(8,128)(2,1)S(1)}, bf16[512,512]{1,0:T(8,128)(2,1)S(1)}, u32[]{:S(2)}, u32[]{:S(2)}) collective-permute-start(bf16[512,512]{1,0:T(8,128)(2,1)S(1)} %get-tuple-element.42.refs_0_), channel_id=1, source_target_pairs={{0,32},{16,48},{32,64},{48,80},{64,96},{80,112},{96,0},{112,16},{1... | collective-permute-start | bytes 1572872 | tf_op jit(solution)/shard_map/ppermute | solution.py:143
  4.8 15.9 %collective-permute-start = (bf16[512,512]{1,0:T(8,128)(2,1)S(1)}, bf16[512,512]{1,0:T(8,128)(2,1)S(1)}, u32[]{:S(2)}, u32[]{:S(2)}) collective-permute-start(bf16[512,512]{1,0:T(8,128)(2,1)S(1)} %get-tuple-element.42.refs_0_), channel_id=1, source_target_pairs={{0,96},{16,112},{32,0},{48,16},{64,32},{80,48},{96,64},{112,80},{1... | collective-permute-start | bytes 1572872 | tf_op jit(solution)/shard_map/ppermute | solution.py:144
  19.1 15.2 %collective-permute-start.5 = (bf16[512,512]{1,0:T(8,128)(2,1)S(1)}, bf16[512,512]{1,0:T(8,128)(2,1)S(1)}, u32[]{:S(2)}, u32[]{:S(2)}) collective-permute-start(bf16[512,512]{1,0:T(8,128)(2,1)S(1)} %collective-permute-done.4), channel_id=1, source_target_pairs={{0,1},{1,2},{2,3},{3,4},{4,5},{5,6},{6,7},{7,8},{8,9},{9,10},{10,1... | collective-permute-start | bytes 1572872 | tf_op jit(solution)/shard_map/ppermute | solution.py:152
  19.1 15.2 %collective-permute-start.2 = (bf16[256,512]{1,0:T(8,128)(2,1)S(1)}, bf16[256,512]{1,0:T(8,128)(2,1)S(1)}, u32[]{:S(2)}, u32[]{:S(2)}) collective-permute-start(bf16[256,512]{1,0:T(8,128)(2,1)S(1)} %slice.120), channel_id=1, source_target_pairs={{0,32},{16,48},{32,64},{48,80},{64,96},{80,112},{96,0},{112,16},{1... | collective-permute-start | bytes 786440 | tf_op jit(solution)/shard_map/ppermute | solution.py:146
  20.7 13.6 %collective-permute-start.3 = (bf16[256,512]{1,0:T(8,128)(2,1)S(1)}, bf16[256,512]{1,0:T(8,128)(2,1)S(1)}, u32[]{:S(2)}, u32[]{:S(2)}) collective-permute-start(bf16[256,512]{1,0:T(8,128)(2,1)S(1)} %slice.121), channel_id=1, source_target_pairs={{0,96},{16,112},{32,0},{48,16},{64,32},{80,48},{96,64},{112,80},{1... | collective-permute-start | bytes 786440 | tf_op jit(solution)/shard_map/ppermute | solution.py:147
  26.2 8.9 %copy-start.6 = (s32[16,16]{1,0:T(8,128)S(1)}, s32[16,16]{1,0:T(8,128)}, u32[]{:S(2)}) copy-start(s32[16,16]{1,0:T(8,128)} %param.8) | copy-start | bytes 3076
  26.2 9.2 %copy-start.5 = (s32[16,16,3]{1,0,2:T(8,128)S(1)}, s32[16,16,3]{1,0,2:T(8,128)}, u32[]{:S(2)}) copy-start(s32[16,16,3]{1,0,2:T(8,128)} %param.7) | copy-start | bytes 9220
  26.2 13.2 %copy-start = (bf16[8,256,256]{2,1,0:T(8,128)(2,1)S(1)}, bf16[8,256,256]{2,1,0:T(8,128)(2,1)}, u32[]{:S(2)}) copy-start(bf16[8,256,256]{2,1,0:T(8,128)(2,1)} %coup.5) | copy-start | bytes 3145732
  34.3 0.8 copy-start.3
  35.1 4.3 %collective-permute-start.6 = (bf16[2048,512]{1,0:T(8,128)(2,1)S(1)}, bf16[2048,512]{1,0:T(8,128)(2,1)}, u32[]{:S(2)}, u32[]{:S(2)}) collective-permute-start(bf16[2048,512]{1,0:T(8,128)(2,1)S(1)} %shard_map.55.mine), channel_id=1, source_target_pairs={{0,16},{16,0},{32,48},{48,32},{64,80},{80,64},{96,112},{112,96},{1... | collective-permute-start | bytes 6291464 | tf_op jit(solution)/shard_map/ppermute | solution.py:166
  35.6 16.8 %collective-permute-start.9 = (bf16[512,512]{1,0:T(8,128)(2,1)}, bf16[512,512]{1,0:T(8,128)(2,1)S(1)}, u32[]{:S(2)}, u32[]{:S(2)}) collective-permute-start(bf16[512,512]{1,0:T(8,128)(2,1)} %copy-done.3), channel_id=1, source_target_pairs={{0,1},{1,2},{2,3},{3,4},{4,5},{5,6},{6,7},{7,8},{8,9},{9,10},{10,1... | collective-permute-start | bytes 1572872 | tf_op jit(solution)/shard_map/ppermute | solution.py:152
  35.8 11.3 %copy-start.4 = (bf16[512,512]{1,0:T(8,128)(2,1)S(1)}, bf16[512,512]{1,0:T(8,128)(2,1)}, u32[]{:S(2)}) copy-start(bf16[512,512]{1,0:T(8,128)(2,1)} %copy-done.3) | copy-start | bytes 1572868
  39.4 13.0 %slice-start = ((s8[8388608]{0:T(1024)(128)(4,1)}), s8[4194304]{0:T(1024)(128)(4,1)S(1)}, s32[]{:S(2)}) async-start(s8[8388608]{0:T(1024)(128)(4,1)} %bitcast.49), calls=%async_computation | async-start | bytes 8388608
  44.6 4.4 %copy-start.1 = (f32[512,1024]{1,0:T(8,128)S(1)}, f32[512,1024]{1,0:T(8,128)}, u32[]{:S(2)}) copy-start(f32[512,1024]{1,0:T(8,128)} %add.88) | copy-start | bytes 6291460
  44.6 7.9 %slice-start.1 = ((s8[8388608]{0:T(1024)(128)(4,1)}), s8[4194304]{0:T(1024)(128)(4,1)S(1)}, s32[]{:S(2)}) async-start(s8[8388608]{0:T(1024)(128)(4,1)} %bitcast.49), calls=%async_computation.1 | async-start | bytes 8388608
  44.6 20.8 %collective-permute-start.7 = (bf16[512,512]{1,0:T(8,128)(2,1)S(1)}, bf16[512,512]{1,0:T(8,128)(2,1)S(1)}, u32[]{:S(2)}, u32[]{:S(2)}) collective-permute-start(bf16[512,512]{1,0:T(8,128)(2,1)S(1)} %get-tuple-element.48), channel_id=1, source_target_pairs={{0,128},{16,144},{32,160},{48,176},{64,192},{80,208},{96,224},{112... | collective-permute-start | bytes 1572872 | tf_op jit(solution)/shard_map/ppermute | solution.py:172
  53.7 27.9 %collective-permute-start.10 = (bf16[512,1024]{1,0:T(8,128)(2,1)S(1)}, bf16[512,1024]{1,0:T(8,128)(2,1)S(1)}, u32[]{:S(2)}, u32[]{:S(2)}) collective-permute-start(bf16[512,1024]{1,0:T(8,128)(2,1)S(1)} %add_convert_fusion), channel_id=1, source_target_pairs={{0,96},{16,112},{32,0},{48,16},{64,32},{80,48},{96,64},{112,80},{1... | collective-permute-start | bytes 3145736 | tf_op jit(solution)/shard_map/ppermute | solution.py:144
  56.6 25.7 %collective-permute-start.11 = (bf16[512,1024]{1,0:T(8,128)(2,1)S(1)}, bf16[512,1024]{1,0:T(8,128)(2,1)S(1)}, u32[]{:S(2)}, u32[]{:S(2)}) collective-permute-start(bf16[512,1024]{1,0:T(8,128)(2,1)S(1)} %add_convert_fusion), channel_id=1, source_target_pairs={{0,32},{16,48},{32,64},{48,80},{64,96},{80,112},{96,0},{112,16},{1... | collective-permute-start | bytes 3145736 | tf_op jit(solution)/shard_map/ppermute | solution.py:143
  65.6 16.0 %collective-permute-start.8 = (bf16[512,512]{1,0:T(8,128)(2,1)S(1)}, bf16[512,512]{1,0:T(8,128)(2,1)S(1)}, u32[]{:S(2)}, u32[]{:S(2)}) collective-permute-start(bf16[512,512]{1,0:T(8,128)(2,1)S(1)} %add_convert_fusion.1), channel_id=1, source_target_pairs={{0,1},{1,2},{2,3},{3,4},{4,5},{5,6},{6,7},{7,8},{8,9},{9,10},{10,1... | collective-permute-start | bytes 1572872 | tf_op jit(solution)/shard_map/ppermute | solution.py:152
  82.2 14.5 %collective-permute-start.12 = (bf16[512,512]{1,0:T(8,128)(2,1)S(1)}, bf16[512,512]{1,0:T(8,128)(2,1)S(1)}, u32[]{:S(2)}, u32[]{:S(2)}) collective-permute-start(bf16[512,512]{1,0:T(8,128)(2,1)S(1)} %collective-permute-done.8), channel_id=1, source_target_pairs={{0,1},{1,2},{2,3},{3,4},{4,5},{5,6},{6,7},{7,8},{8,9},{9,10},{10,1... | collective-permute-start | bytes 1572872 | tf_op jit(solution)/shard_map/ppermute | solution.py:152
  82.3 14.5 %collective-permute-start.14 = (bf16[256,1024]{1,0:T(8,128)(2,1)S(1)}, bf16[256,1024]{1,0:T(8,128)(2,1)S(1)}, u32[]{:S(2)}, u32[]{:S(2)}) collective-permute-start(bf16[256,1024]{1,0:T(8,128)(2,1)S(1)} %slice.122), channel_id=1, source_target_pairs={{0,32},{16,48},{32,64},{48,80},{64,96},{80,112},{96,0},{112,16},{1... | collective-permute-start | bytes 1572872 | tf_op jit(solution)/shard_map/ppermute | solution.py:146
  83.4 13.4 %collective-permute-start.15 = (bf16[256,1024]{1,0:T(8,128)(2,1)S(1)}, bf16[256,1024]{1,0:T(8,128)(2,1)S(1)}, u32[]{:S(2)}, u32[]{:S(2)}) collective-permute-start(bf16[256,1024]{1,0:T(8,128)(2,1)S(1)} %slice.123), channel_id=1, source_target_pairs={{0,96},{16,112},{32,0},{48,16},{64,32},{80,48},{96,64},{112,80},{1... | collective-permute-start | bytes 1572872 | tf_op jit(solution)/shard_map/ppermute | solution.py:147
  97.2 4.2 %collective-permute-start.16 = (bf16[2048,512]{1,0:T(8,128)(2,1)S(1)}, bf16[2048,512]{1,0:T(8,128)(2,1)S(1)}, u32[]{:S(2)}, u32[]{:S(2)}) collective-permute-start(bf16[2048,512]{1,0:T(8,128)(2,1)S(1)} %shard_map.57.mine), channel_id=1, source_target_pairs={{0,16},{16,0},{32,48},{48,32},{64,80},{80,64},{96,112},{112,96},{1... | collective-permute-start | bytes 6291464 | tf_op jit(solution)/shard_map/ppermute | solution.py:183
  97.5 10.3 %collective-permute-start.17 = (bf16[2048,512]{1,0:T(8,128)(2,1)S(1)}, bf16[2048,512]{1,0:T(8,128)(2,1)S(1)}, u32[]{:S(2)}, u32[]{:S(2)}) collective-permute-start(bf16[2048,512]{1,0:T(8,128)(2,1)S(1)} %shard_map.59.mine), channel_id=1, source_target_pairs={{0,16},{16,0},{32,48},{48,32},{64,80},{80,64},{96,112},{112,96},{1... | collective-permute-start | bytes 6291464 | tf_op jit(solution)/shard_map/ppermute | solution.py:183
  98.1 16.1 %collective-permute-start.13 = (bf16[512,512]{1,0:T(8,128)(2,1)S(1)}, bf16[512,512]{1,0:T(8,128)(2,1)S(1)}, u32[]{:S(2)}, u32[]{:S(2)}) collective-permute-start(bf16[512,512]{1,0:T(8,128)(2,1)S(1)} %collective-permute-done.12), channel_id=1, source_target_pairs={{0,1},{1,2},{2,3},{3,4},{4,5},{5,6},{6,7},{7,8},{8,9},{9,10},{10,1... | collective-permute-start | bytes 1572872 | tf_op jit(solution)/shard_map/ppermute | solution.py:152
  105.5 32.8 %collective-permute-start.18 = (bf16[512,512]{1,0:T(8,128)(2,1)S(1)}, bf16[512,512]{1,0:T(8,128)(2,1)S(1)}, u32[]{:S(2)}, u32[]{:S(2)}) collective-permute-start(bf16[512,512]{1,0:T(8,128)(2,1)S(1)} %get-tuple-element.67), channel_id=1, source_target_pairs={{0,128},{16,144},{32,160},{48,176},{64,192},{80,208},{96,224},{112... | collective-permute-start | bytes 1572872 | tf_op jit(solution)/shard_map/ppermute | solution.py:190
  111.7 26.5 %collective-permute-start.19 = (bf16[512,512]{1,0:T(8,128)(2,1)S(1)}, bf16[512,512]{1,0:T(8,128)(2,1)S(1)}, u32[]{:S(2)}, u32[]{:S(2)}) collective-permute-start(bf16[512,512]{1,0:T(8,128)(2,1)S(1)} %get-tuple-element.70), channel_id=1, source_target_pairs={{0,128},{16,144},{32,160},{48,176},{64,192},{80,208},{96,224},{112... | collective-permute-start | bytes 1572872 | tf_op jit(solution)/shard_map/ppermute | solution.py:190

commit v4 on v3

--- a/solution.py
+++ b/solution.py
@@ -153,21 +153,22 @@
 
     cols = coefficients.shape[1]
     early = coefficients[:, :EARLY]
-    arrived = hop(early)
+    arrived = [hop(early[:, : EARLY // 2]), hop(early[:, EARLY // 2 :])]
     mixed = product(early, beta_tiles[0, :EARLY])
     parts = spread(coefficients[:, EARLY:])
     for d in range(1, STOPS - 1):
-        arrived, mixed = tie(arrived, mixed)
-        early, arrived = arrived, hop(arrived)
+        arrived[0], mixed = tie(arrived[0], mixed)
+        early, arrived = arrived, [hop(block) for block in arrived]
         if d < STOPS - 2:
-            mixed = mixed + product(early, beta_tiles[d, :EARLY])
-    *parts, mixed, early = tie(*parts, mixed, early)
+            mixed = mixed + product(jnp.concatenate(early, axis=1), beta_tiles[d, :EARLY])
+    *parts, mixed, early[0], early[1] = tie(*parts, mixed, *early)
     mine = stack(parts)
     sib = lax.ppermute(mine, "alpha", SWAP_CORE)
     near, away = couple(codes, couplings, mine, sib)
-    early, mixed, _ = tie(early, mixed, away)
-    mixed = mixed + product(early, beta_tiles[STOPS - 2, :EARLY])
-    arrived, mixed = tie(arrived, mixed)
+    *early, mixed, _ = tie(*early, mixed, away)
+    mixed = mixed + product(jnp.concatenate(early, axis=1), beta_tiles[STOPS - 2, :EARLY])
+    *arrived, mixed = tie(*arrived, mixed)
+    arrived = jnp.concatenate(arrived, axis=1)
     mixed = (mixed + product(arrived, beta_tiles[STOPS - 1, :EARLY])).astype(jnp.bfloat16)
     back = lax.ppermute(away, "alpha", SWAP_Y)
     moved = [(near + back.astype(jnp.float32)).astype(jnp.bfloat16)]

time: 143 us -> 141 us (0.986)
  Pallas kernels: 13.5 us -> 8.74 us
    pallas_call x3, Pallas kernels: 13.1 us -> 8.33 us  [couple(): pl.pallas_call(couple_kernel, in_specs=[SMEM] + [VMEM] * 3, out_specs=[VM...]
    ppermute x6 -> x9, starting transfers between devices: 2.17 us -> 4.24 us  [hop(): return lax.ppermute(block, 'beta', RING)]
    ppermute x6 -> x9, waiting for transfers between devices: 48.3 us -> 50.4 us  [hop(): return lax.ppermute(block, 'beta', RING)]
    ppermute x2, starting transfers between devices: 4.14 us -> 6 us  [spread(): lax.ppermute(right[AB:], 'alpha', to_x(-1))]
    ppermute x2, starting transfers between devices: 2.65 us -> 0.78 us  [spread(): lax.ppermute(left[:AB], 'alpha', to_x(1))]
  transfers between devices with their start and end apart: 20 -> 23, of which waited for: 11 -> 11; matrix products, arithmetic and copies ran while one was open for 9% -> 10% of each run, Pallas kernels for 9% -> 6%
where the time goes in v4:
time: 141 us; the launch traced here: 139 us
  waiting for transfers between devices  88.3 us (63%)
  starting transfers between devices  23 us (16%)
  matrix products  9.51 us (7%)
  Pallas kernels  8.74 us (6%)
  other arithmetic  5.17 us (4%)
  local copies, waits for them, and re-layouts  3.69 us (3%)
    ppermute x9, waiting for transfers between devices, hop(): return lax.ppermute(block, 'beta', RING)  50.4 us
    ppermute x2, waiting for transfers between devices, per_device(): backs.append(lax.ppermute(away, 'alpha', SWAP_Y))  22.1 us
    ppermute x1, waiting for transfers between devices, per_device(): back = lax.ppermute(away, 'alpha', SWAP_Y)  9.63 us
    dot_general x8, matrix products, product(): return jnp.dot(block, tile, preferred_element_type=jnp.float32)  9.51 us
    pallas_call x3, Pallas kernels, couple(): pl.pallas_call(couple_kernel, in_specs=[SMEM] + [VMEM] * 3, out_specs=[VM...  8.33 us
    ppermute x2, starting transfers between devices, spread(): lax.ppermute(right[AB:], 'alpha', to_x(-1))  6 us
    ppermute x9, starting transfers between devices, hop(): return lax.ppermute(block, 'beta', RING)  4.24 us
    ppermute x2, starting transfers between devices, per_device(): backs.append(lax.ppermute(away, 'alpha', SWAP_Y))  3.46 us
  transfers between devices with their start and end apart: 23, of which 11 were waited for; matrix products, arithmetic and copies ran while one was open for 10% of the time, Pallas kernels for 6%

profile of v4, /device:TPU:8, one launch (start us, length us, event | category | flops | bytes accessed | tf_op | source)
XLA Modules:
  0.0 138.6 jit_solution(17729627213094576875)
XLA Ops:
  0.0 1.2 slice.104.refs_0_
  1.2 1.6 %collective-permute-start.1 = (bf16[512,512]{1,0:T(8,128)(2,1)S(1)}, bf16[512,512]{1,0:T(8,128)(2,1)S(1)}, u32[]{:S(2)}, u32[]{:S(2)}) collective-permute-start(bf16[512,512]{1,0:T(8,128)(2,1)S(1)} %slice.104.refs_0_), channel_id=1, source_target_pairs={{0,32},{16,48},{32,64},{48,80},{64,96},{80,112},{96,0},{112,16},{1... | collective-permute-start | bytes 1572872 | tf_op jit(solution)/shard_map/ppermute | solution.py:143
  2.7 1.7 %collective-permute-start = (bf16[512,512]{1,0:T(8,128)(2,1)S(1)}, bf16[512,512]{1,0:T(8,128)(2,1)S(1)}, u32[]{:S(2)}, u32[]{:S(2)}) collective-permute-start(bf16[512,512]{1,0:T(8,128)(2,1)S(1)} %slice.104.refs_0_), channel_id=1, source_target_pairs={{0,96},{16,112},{32,0},{48,16},{64,32},{80,48},{96,64},{112,80},{1... | collective-permute-start | bytes 1572872 | tf_op jit(solution)/shard_map/ppermute | solution.py:144
  4.5 1.1 fusion.47
  5.6 2.0 %collective-permute-start.4 = (bf16[512,256]{1,0:T(8,128)(2,1)S(1)}, bf16[512,256]{1,0:T(8,128)(2,1)S(1)}, u32[]{:S(2)}, u32[]{:S(2)}) collective-permute-start(bf16[512,256]{1,0:T(8,128)(2,1)S(1)} %get-tuple-element.88), channel_id=1, source_target_pairs={{0,1},{1,2},{2,3},{3,4},{4,5},{5,6},{6,7},{7,8},{8,9},{9,10},{10,1... | collective-permute-start | bytes 786440 | tf_op jit(solution)/shard_map/ppermute | solution.py:152
  7.5 1.9 %collective-permute-start.6 = (bf16[512,256]{1,0:T(8,128)(2,1)S(1)}, bf16[512,256]{1,0:T(8,128)(2,1)S(1)}, u32[]{:S(2)}, u32[]{:S(2)}) collective-permute-start(bf16[512,256]{1,0:T(8,128)(2,1)S(1)} %get-tuple-element.87), channel_id=1, source_target_pairs={{0,1},{1,2},{2,3},{3,4},{4,5},{5,6},{6,7},{7,8},{8,9},{9,10},{10,1... | collective-permute-start | bytes 786440 | tf_op jit(solution)/shard_map/ppermute | solution.py:152
  9.5 1.9 %fusion.17 = f32[512,1024]{1,0:T(8,128)S(1)} fusion(bf16[4,1024,1024]{2,1,0:T(8,128)(2,1)} %param.9, bf16[512,1024]{1,0:T(8,128)(2,1)S(1)} %copy-done.2), kind=kOutput, calls=%fused_computation.18 | convolution fusion | flops 536870912 | bytes 3670016 | tf_op jit(solution)/shard_map/dot_general | solution.py:132
  11.4 7.2 %collective-permute-done.4 = bf16[512,256]{1,0:T(8,128)(2,1)S(1)} collective-permute-done((bf16[512,256]{1,0:T(8,128)(2,1)S(1)}, bf16[512,256]{1,0:T(8,128)(2,1)S(1)}, u32[]{:S(2)}, u32[]{:S(2)}) %collective-permute-start.4) | collective-permute-done | bytes 262176 | tf_op jit(solution)/shard_map/ppermute | solution.py:152
  18.6 5.6 %collective-permute-done.6 = bf16[512,256]{1,0:T(8,128)(2,1)S(1)} collective-permute-done((bf16[512,256]{1,0:T(8,128)(2,1)S(1)}, bf16[512,256]{1,0:T(8,128)(2,1)S(1)}, u32[]{:S(2)}, u32[]{:S(2)}) %collective-permute-start.6) | collective-permute-done | bytes 262176 | tf_op jit(solution)/shard_map/ppermute | solution.py:152
  24.2 0.0 collective-permute-start.7
  24.2 0.0 collective-permute-done.1.refs_4_
  24.2 0.4 collective-permute-start.2
  24.6 0.0 collective-permute-done.refs_1_
  24.6 3.0 %collective-permute-start.3 = (bf16[256,512]{1,0:T(8,128)(2,1)S(1)}, bf16[256,512]{1,0:T(8,128)(2,1)S(1)}, u32[]{:S(2)}, u32[]{:S(2)}) collective-permute-start(bf16[256,512]{1,0:T(8,128)(2,1)S(1)} %slice.131), channel_id=1, source_target_pairs={{0,96},{16,112},{32,0},{48,16},{64,32},{80,48},{96,64},{112,80},{1... | collective-permute-start | bytes 786440 | tf_op jit(solution)/shard_map/ppermute | solution.py:147
  27.6 1.9 %fusion.15 = f32[512,1024]{1,0:T(8,128)S(1)} fusion(bf16[4,1024,1024]{2,1,0:T(8,128)(2,1)} %param.9, bf16[512,256]{1,0:T(8,128)(2,1)S(1)} %collective-permute-done.6, bf16[512,256]{1,0:T(8,128)(2,1)S(1)} %collective-permute-done.4), kind=kOutput, calls=%fused_computation.16 | convolution fusion | flops 537919488 | bytes 3670016 | tf_op jit(solution)/shard_map/dot_general | solution.py:132
  29.6 1.7 %add.88 = f32[512,1024]{1,0:T(8,128)} add(f32[512,1024]{1,0:T(8,128)S(1)} %fusion.17, f32[512,1024]{1,0:T(8,128)S(1)} %fusion.15) | non-fusion elementwise | flops 524288 | bytes 6291456 | tf_op jit(solution)/shard_map/add | solution.py:163
  31.3 0.0 collective-permute-done.5
  31.3 2.6 %collective-permute-done.7 = bf16[512,256]{1,0:T(8,128)(2,1)S(1)} collective-permute-done((bf16[512,256]{1,0:T(8,128)(2,1)S(1)}, bf16[512,256]{1,0:T(8,128)(2,1)S(1)}, u32[]{:S(2)}, u32[]{:S(2)}) %collective-permute-start.7) | collective-permute-done | bytes 262176 | tf_op jit(solution)/shard_map/ppermute | solution.py:152
  34.0 0.1 shard_map.55.mine
  34.1 0.6 copy-done.3
  34.7 0.2 dynamic-slice_reduce_fusion.3
  34.9 0.3 dynamic-slice_reduce_fusion.1
  35.2 0.1 pad_add_fusion.codes
  35.3 0.0 collective-permute-start.11
  35.3 0.2 collective-permute-start.12
  35.5 3.5 %collective-permute-done.8.sib = bf16[2048,512]{1,0:T(8,128)(2,1)} collective-permute-done((bf16[2048,512]{1,0:T(8,128)(2,1)S(1)}, bf16[2048,512]{1,0:T(8,128)(2,1)}, u32[]{:S(2)}, u32[]{:S(2)}) %collective-permute-start.8) | collective-permute-done | bytes 2097184 | tf_op jit(solution)/shard_map/ppermute | solution.py:166
  39.0 3.6 %shard_map.56 = (f32[512,512]{1,0:T(8,128)S(1)}, bf16[512,512]{1,0:T(8,128)(2,1)S(1)}) custom-call(s32[16]{0:T(128)S(1)} %pad_add_fusion.codes, bf16[8,256,256]{2,1,0:T(8,128)(2,1)S(1)} %copy-done, bf16[2048,512]{1,0:T(8,128)(2,1)S(1)} %shard_map.55.mine, bf16[2048,512]{1,0:T(8,128)(2,1)} %collective-permute-done.8.sib), custom_call_target="tpu_custom_call" | custom-call | flops 1048576 | bytes 4096 | tf_op jit(solution)/shard_map/pallas_call | solution.py:97
  42.6 0.0 copy-start.1
  42.6 0.0 slice-start.1
  42.6 2.4 %collective-permute-start.9 = (bf16[512,512]{1,0:T(8,128)(2,1)S(1)}, bf16[512,512]{1,0:T(8,128)(2,1)S(1)}, u32[]{:S(2)}, u32[]{:S(2)}) collective-permute-start(bf16[512,512]{1,0:T(8,128)(2,1)S(1)} %get-tuple-element.51), channel_id=1, source_target_pairs={{0,128},{16,144},{32,160},{48,176},{64,192},{80,208},{96,224},{112... | collective-permute-start | bytes 1572872 | tf_op jit(solution)/shard_map/ppermute | solution.py:173
  45.0 1.9 %fusion.13 = f32[512,1024]{1,0:T(8,128)S(1)} fusion(bf16[4,1024,1024]{2,1,0:T(8,128)(2,1)} %param.9, bf16[512,256]{1,0:T(8,128)(2,1)S(1)} %copy-done.4, bf16[512,256]{1,0:T(8,128)(2,1)S(1)} %collective-permute-done.5), kind=kOutput, calls=%fused_computation.14 | convolution fusion | flops 537919488 | bytes 3670016 | tf_op jit(solution)/shard_map/dot_general | solution.py:132
  46.9 0.6 add.90
  47.5 0.0 collective-permute-done.11
  47.5 4.3 %collective-permute-done.12 = bf16[512,256]{1,0:T(8,128)(2,1)S(1)} collective-permute-done((bf16[512,256]{1,0:T(8,128)(2,1)}, bf16[512,256]{1,0:T(8,128)(2,1)S(1)}, u32[]{:S(2)}, u32[]{:S(2)}) %collective-permute-start.12) | collective-permute-done | bytes 262176 | tf_op jit(solution)/shard_map/ppermute | solution.py:152
  51.9 0.7 fusion.11
  52.6 0.5 add_convert_fusion
  53.1 1.6 %collective-permute-start.13 = (bf16[512,1024]{1,0:T(8,128)(2,1)S(1)}, bf16[512,1024]{1,0:T(8,128)(2,1)S(1)}, u32[]{:S(2)}, u32[]{:S(2)}) collective-permute-start(bf16[512,1024]{1,0:T(8,128)(2,1)S(1)} %add_convert_fusion), channel_id=1, source_target_pairs={{0,96},{16,112},{32,0},{48,16},{64,32},{80,48},{96,64},{112,80},{1... | collective-permute-start | bytes 3145736 | tf_op jit(solution)/shard_map/ppermute | solution.py:144
  54.7 0.5 collective-permute-start.14
  55.2 9.6 %collective-permute-done.9 = bf16[512,512]{1,0:T(8,128)(2,1)S(1)} collective-permute-done((bf16[512,512]{1,0:T(8,128)(2,1)S(1)}, bf16[512,512]{1,0:T(8,128)(2,1)S(1)}, u32[]{:S(2)}, u32[]{:S(2)}) %collective-permute-start.9) | collective-permute-done | bytes 524320 | tf_op jit(solution)/shard_map/ppermute | solution.py:173
  64.8 0.2 add_convert_fusion.1
  65.0 0.1 collective-permute-start.10
  65.1 0.7 fusion.9
  65.8 15.2 %collective-permute-done.10 = bf16[512,512]{1,0:T(8,128)(2,1)S(1)} collective-permute-done((bf16[512,512]{1,0:T(8,128)(2,1)S(1)}, bf16[512,512]{1,0:T(8,128)(2,1)S(1)}, u32[]{:S(2)}, u32[]{:S(2)}) %collective-permute-start.10) | collective-permute-done | bytes 524320 | tf_op jit(solution)/shard_map/ppermute | solution.py:152
  81.1 0.4 collective-permute-start.17
  81.6 3.0 %collective-permute-start.18 = (bf16[256,1024]{1,0:T(8,128)(2,1)S(1)}, bf16[256,1024]{1,0:T(8,128)(2,1)S(1)}, u32[]{:S(2)}, u32[]{:S(2)}) collective-permute-start(bf16[256,1024]{1,0:T(8,128)(2,1)S(1)} %slice.133), channel_id=1, source_target_pairs={{0,96},{16,112},{32,0},{48,16},{64,32},{80,48},{96,64},{112,80},{1... | collective-permute-start | bytes 1572872 | tf_op jit(solution)/shard_map/ppermute | solution.py:147
  84.6 11.7 %collective-permute-done.15 = bf16[512,512]{1,0:T(8,128)(2,1)S(1)} collective-permute-done((bf16[512,512]{1,0:T(8,128)(2,1)S(1)}, bf16[512,512]{1,0:T(8,128)(2,1)S(1)}, u32[]{:S(2)}, u32[]{:S(2)}) %collective-permute-start.15) | collective-permute-done | bytes 524320 | tf_op jit(solution)/shard_map/ppermute | solution.py:152
  96.2 0.1 fusion.44
  96.3 0.1 fusion.45
  96.4 0.1 fusion.46
  96.5 0.1 shard_map.57.mine
  96.7 0.1 collective-permute-start.19
  96.8 0.1 shard_map.59.mine
  96.9 0.6 collective-permute-start.20
  97.5 0.7 fusion.7
  98.3 2.7 %collective-permute-done.19.sib = bf16[2048,512]{1,0:T(8,128)(2,1)S(1)} collective-permute-done((bf16[2048,512]{1,0:T(8,128)(2,1)S(1)}, bf16[2048,512]{1,0:T(8,128)(2,1)S(1)}, u32[]{:S(2)}, u32[]{:S(2)}) %collective-permute-start.19) | collective-permute-done | bytes 2097184 | tf_op jit(solution)/shard_map/ppermute | solution.py:184
  100.9 2.4 %shard_map.58 = (f32[512,512]{1,0:T(8,128)S(1)}, bf16[512,512]{1,0:T(8,128)(2,1)S(1)}) custom-call(s32[16]{0:T(128)S(1)} %pad_add_fusion.codes, bf16[8,256,256]{2,1,0:T(8,128)(2,1)S(1)} %copy-done, bf16[2048,512]{1,0:T(8,128)(2,1)S(1)} %shard_map.57.mine, bf16[2048,512]{1,0:T(8,128)(2,1)S(1)} %collective-permute-done.19.sib), custom_call_target="tpu_custom_call" | custom-call | flops 1048576 | bytes 4096 | tf_op jit(solution)/shard_map/pallas_call | solution.py:97
  103.3 1.2 collective-permute-start.21
  104.5 2.4 %shard_map.60 = (f32[512,512]{1,0:T(8,128)S(1)}, bf16[512,512]{1,0:T(8,128)(2,1)S(1)}) custom-call(s32[16]{0:T(128)S(1)} %pad_add_fusion.codes, bf16[8,256,256]{2,1,0:T(8,128)(2,1)S(1)} %copy-done, bf16[2048,512]{1,0:T(8,128)(2,1)S(1)} %shard_map.59.mine, bf16[2048,512]{1,0:T(8,128)(2,1)S(1)} %collective-permute-done.20.sib), custom_call_target="tpu_custom_call" | custom-call | flops 1048576 | bytes 4096 | tf_op jit(solution)/shard_map/pallas_call | solution.py:97
  106.9 2.2 %collective-permute-start.22 = (bf16[512,512]{1,0:T(8,128)(2,1)S(1)}, bf16[512,512]{1,0:T(8,128)(2,1)S(1)}, u32[]{:S(2)}, u32[]{:S(2)}) collective-permute-start(bf16[512,512]{1,0:T(8,128)(2,1)S(1)} %get-tuple-element.76), channel_id=1, source_target_pairs={{0,128},{16,144},{32,160},{48,176},{64,192},{80,208},{96,224},{112... | collective-permute-start | bytes 1572872 | tf_op jit(solution)/shard_map/ppermute | solution.py:191
  109.2 0.8 add_add_fusion
  109.9 3.7 %collective-permute-done.16 = bf16[512,512]{1,0:T(8,128)(2,1)S(1)} collective-permute-done((bf16[512,512]{1,0:T(8,128)(2,1)S(1)}, bf16[512,512]{1,0:T(8,128)(2,1)S(1)}, u32[]{:S(2)}, u32[]{:S(2)}) %collective-permute-start.16) | collective-permute-done | bytes 524320 | tf_op jit(solution)/shard_map/ppermute | solution.py:152
  113.6 0.7 fusion.1
  114.4 22.1 %collective-permute-done.22 = bf16[512,512]{1,0:T(8,128)(2,1)S(1)} collective-permute-done((bf16[512,512]{1,0:T(8,128)(2,1)S(1)}, bf16[512,512]{1,0:T(8,128)(2,1)S(1)}, u32[]{:S(2)}, u32[]{:S(2)}) %collective-permute-start.22) | collective-permute-done | bytes 524320 | tf_op jit(solution)/shard_map/ppermute | solution.py:191
  136.5 2.1 %fusion = f32[512,1024]{1,0:T(8,128)} fusion(f32[512,512]{1,0:T(8,128)S(1)} %get-tuple-element.75, f32[512,512]{1,0:T(8,128)S(1)} %get-tuple-element.72, f32[512,1024]{1,0:T(8,128)S(1)} %add_add_fusion, f32[512,1024]{1,0:T(8,128)S(1)} %fusion.1, bf16[512,512]{1,0:T(8,128)(2,1)S(1)} %collective-permute-done.22, bf16[512,512]{1,0:T(8,128)(2,1)S(1)} %collective-permute-done.21), kind=kLoop, calls=%fused_computation.1 | loop fusion | flops 4194304 | bytes 9437184 | tf_op jit(solution)/shard_map/add | solution.py:198
  (36 shorter events, 0.3 us)
Async XLA Ops:
  0.0 9.5 %copy-start.2 = (bf16[512,1024]{1,0:T(8,128)(2,1)S(1)}, bf16[512,1024]{1,0:T(8,128)(2,1)}, u32[]{:S(2)}) copy-start(bf16[512,1024]{1,0:T(8,128)(2,1)} %param.5) | copy-start | bytes 3145732
  1.2 23.0 %collective-permute-start.1 = (bf16[512,512]{1,0:T(8,128)(2,1)S(1)}, bf16[512,512]{1,0:T(8,128)(2,1)S(1)}, u32[]{:S(2)}, u32[]{:S(2)}) collective-permute-start(bf16[512,512]{1,0:T(8,128)(2,1)S(1)} %slice.104.refs_0_), channel_id=1, source_target_pairs={{0,32},{16,48},{32,64},{48,80},{64,96},{80,112},{96,0},{112,16},{1... | collective-permute-start | bytes 1572872 | tf_op jit(solution)/shard_map/ppermute | solution.py:143
  2.7 21.9 %collective-permute-start = (bf16[512,512]{1,0:T(8,128)(2,1)S(1)}, bf16[512,512]{1,0:T(8,128)(2,1)S(1)}, u32[]{:S(2)}, u32[]{:S(2)}) collective-permute-start(bf16[512,512]{1,0:T(8,128)(2,1)S(1)} %slice.104.refs_0_), channel_id=1, source_target_pairs={{0,96},{16,112},{32,0},{48,16},{64,32},{80,48},{96,64},{112,80},{1... | collective-permute-start | bytes 1572872 | tf_op jit(solution)/shard_map/ppermute | solution.py:144
  5.6 13.0 %collective-permute-start.4 = (bf16[512,256]{1,0:T(8,128)(2,1)S(1)}, bf16[512,256]{1,0:T(8,128)(2,1)S(1)}, u32[]{:S(2)}, u32[]{:S(2)}) collective-permute-start(bf16[512,256]{1,0:T(8,128)(2,1)S(1)} %get-tuple-element.88), channel_id=1, source_target_pairs={{0,1},{1,2},{2,3},{3,4},{4,5},{5,6},{6,7},{7,8},{8,9},{9,10},{10,1... | collective-permute-start | bytes 786440 | tf_op jit(solution)/shard_map/ppermute | solution.py:152
  7.5 16.7 %collective-permute-start.6 = (bf16[512,256]{1,0:T(8,128)(2,1)S(1)}, bf16[512,256]{1,0:T(8,128)(2,1)S(1)}, u32[]{:S(2)}, u32[]{:S(2)}) collective-permute-start(bf16[512,256]{1,0:T(8,128)(2,1)S(1)} %get-tuple-element.87), channel_id=1, source_target_pairs={{0,1},{1,2},{2,3},{3,4},{4,5},{5,6},{6,7},{7,8},{8,9},{9,10},{10,1... | collective-permute-start | bytes 786440 | tf_op jit(solution)/shard_map/ppermute | solution.py:152
  18.6 12.7 %collective-permute-start.5 = (bf16[512,256]{1,0:T(8,128)(2,1)S(1)}, bf16[512,256]{1,0:T(8,128)(2,1)S(1)}, u32[]{:S(2)}, u32[]{:S(2)}) collective-permute-start(bf16[512,256]{1,0:T(8,128)(2,1)S(1)} %collective-permute-done.4), channel_id=1, source_target_pairs={{0,1},{1,2},{2,3},{3,4},{4,5},{5,6},{6,7},{7,8},{8,9},{9,10},{10,1... | collective-permute-start | bytes 786440 | tf_op jit(solution)/shard_map/ppermute | solution.py:152
  24.2 9.8 %collective-permute-start.7 = (bf16[512,256]{1,0:T(8,128)(2,1)S(1)}, bf16[512,256]{1,0:T(8,128)(2,1)S(1)}, u32[]{:S(2)}, u32[]{:S(2)}) collective-permute-start(bf16[512,256]{1,0:T(8,128)(2,1)S(1)} %collective-permute-done.6), channel_id=1, source_target_pairs={{0,1},{1,2},{2,3},{3,4},{4,5},{5,6},{6,7},{7,8},{8,9},{9,10},{10,1... | collective-permute-start | bytes 786440 | tf_op jit(solution)/shard_map/ppermute | solution.py:152
  24.2 9.7 %collective-permute-start.2 = (bf16[256,512]{1,0:T(8,128)(2,1)S(1)}, bf16[256,512]{1,0:T(8,128)(2,1)S(1)}, u32[]{:S(2)}, u32[]{:S(2)}) collective-permute-start(bf16[256,512]{1,0:T(8,128)(2,1)S(1)} %slice.130), channel_id=1, source_target_pairs={{0,32},{16,48},{32,64},{48,80},{64,96},{80,112},{96,0},{112,16},{1... | collective-permute-start | bytes 786440 | tf_op jit(solution)/shard_map/ppermute | solution.py:146
  24.6 9.4 %collective-permute-start.3 = (bf16[256,512]{1,0:T(8,128)(2,1)S(1)}, bf16[256,512]{1,0:T(8,128)(2,1)S(1)}, u32[]{:S(2)}, u32[]{:S(2)}) collective-permute-start(bf16[256,512]{1,0:T(8,128)(2,1)S(1)} %slice.131), channel_id=1, source_target_pairs={{0,96},{16,112},{32,0},{48,16},{64,32},{80,48},{96,64},{112,80},{1... | collective-permute-start | bytes 786440 | tf_op jit(solution)/shard_map/ppermute | solution.py:147
  31.3 3.4 %copy-start.6 = (s32[16,16]{1,0:T(8,128)S(1)}, s32[16,16]{1,0:T(8,128)}, u32[]{:S(2)}) copy-start(s32[16,16]{1,0:T(8,128)} %param.8) | copy-start | bytes 3076
  31.3 3.6 %copy-start.5 = (s32[16,16,3]{1,0,2:T(8,128)S(1)}, s32[16,16,3]{1,0,2:T(8,128)}, u32[]{:S(2)}) copy-start(s32[16,16,3]{1,0,2:T(8,128)} %param.7) | copy-start | bytes 9220
  31.3 7.7 %copy-start = (bf16[8,256,256]{2,1,0:T(8,128)(2,1)S(1)}, bf16[8,256,256]{2,1,0:T(8,128)(2,1)}, u32[]{:S(2)}) copy-start(bf16[8,256,256]{2,1,0:T(8,128)(2,1)} %coup.5) | copy-start | bytes 3145732
  34.0 0.7 copy-start.3
  34.7 4.3 %collective-permute-start.8 = (bf16[2048,512]{1,0:T(8,128)(2,1)S(1)}, bf16[2048,512]{1,0:T(8,128)(2,1)}, u32[]{:S(2)}, u32[]{:S(2)}) collective-permute-start(bf16[2048,512]{1,0:T(8,128)(2,1)S(1)} %shard_map.55.mine), channel_id=1, source_target_pairs={{0,16},{16,0},{32,48},{48,32},{64,80},{80,64},{96,112},{112,96},{1... | collective-permute-start | bytes 6291464 | tf_op jit(solution)/shard_map/ppermute | solution.py:166
  35.3 9.7 %copy-start.4 = (bf16[512,256]{1,0:T(8,128)(2,1)S(1)}, bf16[512,256]{1,0:T(8,128)(2,1)}, u32[]{:S(2)}) copy-start(bf16[512,256]{1,0:T(8,128)(2,1)} %copy-done.3) | copy-start | bytes 786436
  35.3 12.2 %collective-permute-start.11 = (bf16[512,256]{1,0:T(8,128)(2,1)S(1)}, bf16[512,256]{1,0:T(8,128)(2,1)S(1)}, u32[]{:S(2)}, u32[]{:S(2)}) collective-permute-start(bf16[512,256]{1,0:T(8,128)(2,1)S(1)} %collective-permute-done.5), channel_id=1, source_target_pairs={{0,1},{1,2},{2,3},{3,4},{4,5},{5,6},{6,7},{7,8},{8,9},{9,10},{10,1... | collective-permute-start | bytes 786440 | tf_op jit(solution)/shard_map/ppermute | solution.py:152
  35.3 16.5 %collective-permute-start.12 = (bf16[512,256]{1,0:T(8,128)(2,1)}, bf16[512,256]{1,0:T(8,128)(2,1)S(1)}, u32[]{:S(2)}, u32[]{:S(2)}) collective-permute-start(bf16[512,256]{1,0:T(8,128)(2,1)} %copy-done.3), channel_id=1, source_target_pairs={{0,1},{1,2},{2,3},{3,4},{4,5},{5,6},{6,7},{7,8},{8,9},{9,10},{10,1... | collective-permute-start | bytes 786440 | tf_op jit(solution)/shard_map/ppermute | solution.py:152
  39.0 12.9 %slice-start = ((s8[8388608]{0:T(1024)(128)(4,1)}), s8[4194304]{0:T(1024)(128)(4,1)S(1)}, s32[]{:S(2)}) async-start(s8[8388608]{0:T(1024)(128)(4,1)} %bitcast.46), calls=%async_computation | async-start | bytes 8388608
  42.6 4.4 %copy-start.1 = (f32[512,1024]{1,0:T(8,128)S(1)}, f32[512,1024]{1,0:T(8,128)}, u32[]{:S(2)}) copy-start(f32[512,1024]{1,0:T(8,128)} %add.88) | copy-start | bytes 6291460
  42.6 9.3 %slice-start.1 = ((s8[8388608]{0:T(1024)(128)(4,1)}), s8[4194304]{0:T(1024)(128)(4,1)S(1)}, s32[]{:S(2)}) async-start(s8[8388608]{0:T(1024)(128)(4,1)} %bitcast.46), calls=%async_computation.1 | async-start | bytes 8388608
  42.6 22.2 %collective-permute-start.9 = (bf16[512,512]{1,0:T(8,128)(2,1)S(1)}, bf16[512,512]{1,0:T(8,128)(2,1)S(1)}, u32[]{:S(2)}, u32[]{:S(2)}) collective-permute-start(bf16[512,512]{1,0:T(8,128)(2,1)S(1)} %get-tuple-element.51), channel_id=1, source_target_pairs={{0,128},{16,144},{32,160},{48,176},{64,192},{80,208},{96,224},{112... | collective-permute-start | bytes 1572872 | tf_op jit(solution)/shard_map/ppermute | solution.py:173
  53.1 28.0 %collective-permute-start.13 = (bf16[512,1024]{1,0:T(8,128)(2,1)S(1)}, bf16[512,1024]{1,0:T(8,128)(2,1)S(1)}, u32[]{:S(2)}, u32[]{:S(2)}) collective-permute-start(bf16[512,1024]{1,0:T(8,128)(2,1)S(1)} %add_convert_fusion), channel_id=1, source_target_pairs={{0,96},{16,112},{32,0},{48,16},{64,32},{80,48},{96,64},{112,80},{1... | collective-permute-start | bytes 3145736 | tf_op jit(solution)/shard_map/ppermute | solution.py:144
  54.7 26.3 %collective-permute-start.14 = (bf16[512,1024]{1,0:T(8,128)(2,1)S(1)}, bf16[512,1024]{1,0:T(8,128)(2,1)S(1)}, u32[]{:S(2)}, u32[]{:S(2)}) collective-permute-start(bf16[512,1024]{1,0:T(8,128)(2,1)S(1)} %add_convert_fusion), channel_id=1, source_target_pairs={{0,32},{16,48},{32,64},{48,80},{64,96},{80,112},{96,0},{112,16},{1... | collective-permute-start | bytes 3145736 | tf_op jit(solution)/shard_map/ppermute | solution.py:143
  65.0 16.1 %collective-permute-start.10 = (bf16[512,512]{1,0:T(8,128)(2,1)S(1)}, bf16[512,512]{1,0:T(8,128)(2,1)S(1)}, u32[]{:S(2)}, u32[]{:S(2)}) collective-permute-start(bf16[512,512]{1,0:T(8,128)(2,1)S(1)} %add_convert_fusion.1), channel_id=1, source_target_pairs={{0,1},{1,2},{2,3},{3,4},{4,5},{5,6},{6,7},{7,8},{8,9},{9,10},{10,1... | collective-permute-start | bytes 1572872 | tf_op jit(solution)/shard_map/ppermute | solution.py:152
  81.1 15.1 %collective-permute-start.15 = (bf16[512,512]{1,0:T(8,128)(2,1)S(1)}, bf16[512,512]{1,0:T(8,128)(2,1)S(1)}, u32[]{:S(2)}, u32[]{:S(2)}) collective-permute-start(bf16[512,512]{1,0:T(8,128)(2,1)S(1)} %collective-permute-done.10), channel_id=1, source_target_pairs={{0,1},{1,2},{2,3},{3,4},{4,5},{5,6},{6,7},{7,8},{8,9},{9,10},{10,1... | collective-permute-start | bytes 1572872 | tf_op jit(solution)/shard_map/ppermute | solution.py:152
  81.1 15.1 %collective-permute-start.17 = (bf16[256,1024]{1,0:T(8,128)(2,1)S(1)}, bf16[256,1024]{1,0:T(8,128)(2,1)S(1)}, u32[]{:S(2)}, u32[]{:S(2)}) collective-permute-start(bf16[256,1024]{1,0:T(8,128)(2,1)S(1)} %slice.132), channel_id=1, source_target_pairs={{0,32},{16,48},{32,64},{48,80},{64,96},{80,112},{96,0},{112,16},{1... | collective-permute-start | bytes 1572872 | tf_op jit(solution)/shard_map/ppermute | solution.py:146
  81.6 14.6 %collective-permute-start.18 = (bf16[256,1024]{1,0:T(8,128)(2,1)S(1)}, bf16[256,1024]{1,0:T(8,128)(2,1)S(1)}, u32[]{:S(2)}, u32[]{:S(2)}) collective-permute-start(bf16[256,1024]{1,0:T(8,128)(2,1)S(1)} %slice.133), channel_id=1, source_target_pairs={{0,96},{16,112},{32,0},{48,16},{64,32},{80,48},{96,64},{112,80},{1... | collective-permute-start | bytes 1572872 | tf_op jit(solution)/shard_map/ppermute | solution.py:147
  96.7 4.2 %collective-permute-start.19 = (bf16[2048,512]{1,0:T(8,128)(2,1)S(1)}, bf16[2048,512]{1,0:T(8,128)(2,1)S(1)}, u32[]{:S(2)}, u32[]{:S(2)}) collective-permute-start(bf16[2048,512]{1,0:T(8,128)(2,1)S(1)} %shard_map.57.mine), channel_id=1, source_target_pairs={{0,16},{16,0},{32,48},{48,32},{64,80},{80,64},{96,112},{112,96},{1... | collective-permute-start | bytes 6291464 | tf_op jit(solution)/shard_map/ppermute | solution.py:184
  96.9 7.6 %collective-permute-start.20 = (bf16[2048,512]{1,0:T(8,128)(2,1)S(1)}, bf16[2048,512]{1,0:T(8,128)(2,1)S(1)}, u32[]{:S(2)}, u32[]{:S(2)}) collective-permute-start(bf16[2048,512]{1,0:T(8,128)(2,1)S(1)} %shard_map.59.mine), channel_id=1, source_target_pairs={{0,16},{16,0},{32,48},{48,32},{64,80},{80,64},{96,112},{112,96},{1... | collective-permute-start | bytes 6291464 | tf_op jit(solution)/shard_map/ppermute | solution.py:184
  97.5 16.1 %collective-permute-start.16 = (bf16[512,512]{1,0:T(8,128)(2,1)S(1)}, bf16[512,512]{1,0:T(8,128)(2,1)S(1)}, u32[]{:S(2)}, u32[]{:S(2)}) collective-permute-start(bf16[512,512]{1,0:T(8,128)(2,1)S(1)} %collective-permute-done.15), channel_id=1, source_target_pairs={{0,1},{1,2},{2,3},{3,4},{4,5},{5,6},{6,7},{7,8},{8,9},{9,10},{10,1... | collective-permute-start | bytes 1572872 | tf_op jit(solution)/shard_map/ppermute | solution.py:152
  103.3 33.2 %collective-permute-start.21 = (bf16[512,512]{1,0:T(8,128)(2,1)S(1)}, bf16[512,512]{1,0:T(8,128)(2,1)S(1)}, u32[]{:S(2)}, u32[]{:S(2)}) collective-permute-start(bf16[512,512]{1,0:T(8,128)(2,1)S(1)} %get-tuple-element.73), channel_id=1, source_target_pairs={{0,128},{16,144},{32,160},{48,176},{64,192},{80,208},{96,224},{112... | collective-permute-start | bytes 1572872 | tf_op jit(solution)/shard_map/ppermute | solution.py:191
  106.9 29.6 %collective-permute-start.22 = (bf16[512,512]{1,0:T(8,128)(2,1)S(1)}, bf16[512,512]{1,0:T(8,128)(2,1)S(1)}, u32[]{:S(2)}, u32[]{:S(2)}) collective-permute-start(bf16[512,512]{1,0:T(8,128)(2,1)S(1)} %get-tuple-element.76), channel_id=1, source_target_pairs={{0,128},{16,144},{32,160},{48,176},{64,192},{80,208},{96,224},{112... | collective-permute-start | bytes 1572872 | tf_op jit(solution)/shard_map/ppermute | solution.py:191

commit v5 on v4

--- a/solution.py
+++ b/solution.py
@@ -14,7 +14,7 @@
 NZ = 8
 ROWS = ABLK * AB
 EARLY = 512
-PARTS = 2
+PARTS = 1
 COLUMN_TILE = 256
 
 COST = pl.CostEstimate(flops=1 << 20, bytes_accessed=1 << 12, transcendentals=0)

time: 141 us -> 144 us (1.021)
  waiting for transfers between devices: 88.3 us -> 95.5 us
  starting transfers between devices: 23 us -> 20.9 us
    ppermute x2, waiting for transfers between devices: 0.01 us -> 10.3 us  [spread(): lax.ppermute(left[:AB], 'alpha', to_x(1))]
    ppermute x9, waiting for transfers between devices: 50.4 us -> 41.8 us  [hop(): return lax.ppermute(block, 'beta', RING)]
    ppermute x2 -> x1, waiting for transfers between devices: 2.68 us -> 7.05 us  [per_device(): sibs = [lax.ppermute(m, 'alpha', SWAP_CORE) for m in mines]]
    ppermute x2, starting transfers between devices: 3.37 us -> 5.87 us  [spread(): right = lax.ppermute(own, 'alpha', to_x(-1))]
    ppermute x2, starting transfers between devices: 2.05 us -> 0.01 us  [spread(): left = lax.ppermute(own, 'alpha', to_x(1))]
    ppermute x2 -> x1, starting transfers between devices: 3.46 us -> 1.67 us  [per_device(): backs.append(lax.ppermute(away, 'alpha', SWAP_Y))]
    ppermute x2 -> x1, waiting for transfers between devices: 22.1 us -> 23.4 us  [per_device(): backs.append(lax.ppermute(away, 'alpha', SWAP_Y))]
    pallas_call x3 -> x2, Pallas kernels: 8.33 us -> 7.14 us  [couple(): pl.pallas_call(couple_kernel, in_specs=[SMEM] + [VMEM] * 3, out_specs=[VM...]
  transfers between devices with their start and end apart: 23 -> 21, of which waited for: 11 -> 13; matrix products, arithmetic and copies ran while one was open for 10% -> 10% of each run, Pallas kernels for 6% -> 5%
where the time goes in v5:
time: 144 us; the launch traced here: 142 us
  waiting for transfers between devices  95.5 us (66%)
  starting transfers between devices  20.9 us (15%)
  matrix products  9.51 us (7%)
  Pallas kernels  7.54 us (5%)
  other arithmetic  5.21 us (4%)
  local copies, waits for them, and re-layouts  3.4 us (2%)
    ppermute x9, waiting for transfers between devices, hop(): return lax.ppermute(block, 'beta', RING)  41.8 us
    ppermute x1, waiting for transfers between devices, per_device(): backs.append(lax.ppermute(away, 'alpha', SWAP_Y))  23.4 us
    ppermute x2, waiting for transfers between devices, spread(): lax.ppermute(left[:AB], 'alpha', to_x(1))  10.3 us
    dot_general x8, matrix products, product(): return jnp.dot(block, tile, preferred_element_type=jnp.float32)  9.51 us
    ppermute x1, waiting for transfers between devices, per_device(): back = lax.ppermute(away, 'alpha', SWAP_Y)  8.7 us
    pallas_call x2, Pallas kernels, couple(): pl.pallas_call(couple_kernel, in_specs=[SMEM] + [VMEM] * 3, out_specs=[VM...  7.14 us
    ppermute x1, waiting for transfers between devices, per_device(): sibs = [lax.ppermute(m, 'alpha', SWAP_CORE) for m in mines]  7.05 us
    ppermute x2, starting transfers between devices, spread(): lax.ppermute(right[AB:], 'alpha', to_x(-1))  5.88 us
  transfers between devices with their start and end apart: 21, of which 13 were waited for; matrix products, arithmetic and copies ran while one was open for 10% of the time, Pallas kernels for 5%

profile of v5, /device:TPU:8, one launch (start us, length us, event | category | flops | bytes accessed | tf_op | source)
XLA Modules:
  0.0 142.2 jit_solution(1458465281105727557)
XLA Ops:
  0.0 1.2 slice.74.refs_0_
  1.2 2.8 %collective-permute-start = (bf16[512,512]{1,0:T(8,128)(2,1)S(1)}, bf16[512,512]{1,0:T(8,128)(2,1)S(1)}, u32[]{:S(2)}, u32[]{:S(2)}) collective-permute-start(bf16[512,512]{1,0:T(8,128)(2,1)S(1)} %slice.74.refs_0_), channel_id=1, source_target_pairs={{0,96},{16,112},{32,0},{48,16},{64,32},{80,48},{96,64},{112,80},{1... | collective-permute-start | bytes 1572872 | tf_op jit(solution)/shard_map/ppermute | solution.py:144
  4.0 1.1 fusion.43
  5.1 2.0 %collective-permute-start.4 = (bf16[512,256]{1,0:T(8,128)(2,1)S(1)}, bf16[512,256]{1,0:T(8,128)(2,1)S(1)}, u32[]{:S(2)}, u32[]{:S(2)}) collective-permute-start(bf16[512,256]{1,0:T(8,128)(2,1)S(1)} %get-tuple-element.76), channel_id=1, source_target_pairs={{0,1},{1,2},{2,3},{3,4},{4,5},{5,6},{6,7},{7,8},{8,9},{9,10},{10,1... | collective-permute-start | bytes 786440 | tf_op jit(solution)/shard_map/ppermute | solution.py:152
  7.1 1.9 %collective-permute-start.6 = (bf16[512,256]{1,0:T(8,128)(2,1)S(1)}, bf16[512,256]{1,0:T(8,128)(2,1)S(1)}, u32[]{:S(2)}, u32[]{:S(2)}) collective-permute-start(bf16[512,256]{1,0:T(8,128)(2,1)S(1)} %get-tuple-element.75), channel_id=1, source_target_pairs={{0,1},{1,2},{2,3},{3,4},{4,5},{5,6},{6,7},{7,8},{8,9},{9,10},{10,1... | collective-permute-start | bytes 786440 | tf_op jit(solution)/shard_map/ppermute | solution.py:152
  9.0 1.9 %fusion.16 = f32[512,1024]{1,0:T(8,128)S(1)} fusion(bf16[4,1024,1024]{2,1,0:T(8,128)(2,1)} %param.9, bf16[512,1024]{1,0:T(8,128)(2,1)S(1)} %copy-done.2), kind=kOutput, calls=%fused_computation.17 | convolution fusion | flops 536870912 | bytes 3670016 | tf_op jit(solution)/shard_map/dot_general | solution.py:132
  10.9 7.1 %collective-permute-done.4 = bf16[512,256]{1,0:T(8,128)(2,1)S(1)} collective-permute-done((bf16[512,256]{1,0:T(8,128)(2,1)S(1)}, bf16[512,256]{1,0:T(8,128)(2,1)S(1)}, u32[]{:S(2)}, u32[]{:S(2)}) %collective-permute-start.4) | collective-permute-done | bytes 262176 | tf_op jit(solution)/shard_map/ppermute | solution.py:152
  18.1 0.0 collective-permute-start.5
  18.1 5.6 %collective-permute-done.6 = bf16[512,256]{1,0:T(8,128)(2,1)S(1)} collective-permute-done((bf16[512,256]{1,0:T(8,128)(2,1)S(1)}, bf16[512,256]{1,0:T(8,128)(2,1)S(1)}, u32[]{:S(2)}, u32[]{:S(2)}) %collective-permute-start.6) | collective-permute-done | bytes 262176 | tf_op jit(solution)/shard_map/ppermute | solution.py:152
  23.7 0.0 collective-permute-start.7
  23.7 0.0 collective-permute-done.1.refs_4_
  23.7 0.9 collective-permute-start.2
  24.6 0.0 collective-permute-done.refs_1_
  24.6 2.6 %collective-permute-start.3 = (bf16[256,512]{1,0:T(8,128)(2,1)S(1)}, bf16[256,512]{1,0:T(8,128)(2,1)S(1)}, u32[]{:S(2)}, u32[]{:S(2)}) collective-permute-start(bf16[256,512]{1,0:T(8,128)(2,1)S(1)} %slice.91), channel_id=1, source_target_pairs={{0,96},{16,112},{32,0},{48,16},{64,32},{80,48},{96,64},{112,80},{1... | collective-permute-start | bytes 786440 | tf_op jit(solution)/shard_map/ppermute | solution.py:147
  27.2 1.9 %fusion.14 = f32[512,1024]{1,0:T(8,128)S(1)} fusion(bf16[4,1024,1024]{2,1,0:T(8,128)(2,1)} %param.9, bf16[512,256]{1,0:T(8,128)(2,1)S(1)} %collective-permute-done.6, bf16[512,256]{1,0:T(8,128)(2,1)S(1)} %collective-permute-done.4), kind=kOutput, calls=%fused_computation.15 | convolution fusion | flops 537919488 | bytes 3670016 | tf_op jit(solution)/shard_map/dot_general | solution.py:132
  29.1 1.7 %add.88 = f32[512,1024]{1,0:T(8,128)} add(f32[512,1024]{1,0:T(8,128)S(1)} %fusion.16, f32[512,1024]{1,0:T(8,128)S(1)} %fusion.14) | non-fusion elementwise | flops 524288 | bytes 6291456 | tf_op jit(solution)/shard_map/add | solution.py:163
  30.9 0.0 collective-permute-done.5
  30.9 2.9 %collective-permute-done.7 = bf16[512,256]{1,0:T(8,128)(2,1)S(1)} collective-permute-done((bf16[512,256]{1,0:T(8,128)(2,1)S(1)}, bf16[512,256]{1,0:T(8,128)(2,1)S(1)}, u32[]{:S(2)}, u32[]{:S(2)}) %collective-permute-start.7) | collective-permute-done | bytes 262176 | tf_op jit(solution)/shard_map/ppermute | solution.py:152
  33.8 0.0 collective-permute-done.2.refs_2_
  33.8 0.0 collective-permute-done.3.refs_3_
  33.8 0.1 shard_map.55.mine
  33.9 0.6 copy-done.3
  34.5 0.0 collective-permute-start.8
  34.5 0.2 dynamic-slice_reduce_fusion.3
  34.7 0.3 dynamic-slice_reduce_fusion.1
  35.0 0.1 pad_add_fusion.codes
  35.1 0.0 collective-permute-start.11
  35.1 0.1 collective-permute-start.12
  35.2 3.6 %collective-permute-done.8.sib = bf16[2048,512]{1,0:T(8,128)(2,1)} collective-permute-done((bf16[2048,512]{1,0:T(8,128)(2,1)S(1)}, bf16[2048,512]{1,0:T(8,128)(2,1)}, u32[]{:S(2)}, u32[]{:S(2)}) %collective-permute-start.8) | collective-permute-done | bytes 2097184 | tf_op jit(solution)/shard_map/ppermute | solution.py:166
  38.8 3.8 %shard_map.56 = (f32[512,512]{1,0:T(8,128)S(1)}, bf16[512,512]{1,0:T(8,128)(2,1)S(1)}) custom-call(s32[16]{0:T(128)S(1)} %pad_add_fusion.codes, bf16[8,256,256]{2,1,0:T(8,128)(2,1)S(1)} %copy-done, bf16[2048,512]{1,0:T(8,128)(2,1)S(1)} %shard_map.55.mine, bf16[2048,512]{1,0:T(8,128)(2,1)} %collective-permute-done.8.sib), custom_call_target="tpu_custom_call" | custom-call | flops 1048576 | bytes 4096 | tf_op jit(solution)/shard_map/pallas_call | solution.py:97
  42.6 0.0 copy-start.1
  42.6 0.0 slice-start.1
  42.6 2.2 %collective-permute-start.9 = (bf16[512,512]{1,0:T(8,128)(2,1)S(1)}, bf16[512,512]{1,0:T(8,128)(2,1)S(1)}, u32[]{:S(2)}, u32[]{:S(2)}) collective-permute-start(bf16[512,512]{1,0:T(8,128)(2,1)S(1)} %get-tuple-element.48), channel_id=1, source_target_pairs={{0,128},{16,144},{32,160},{48,176},{64,192},{80,208},{96,224},{112... | collective-permute-start | bytes 1572872 | tf_op jit(solution)/shard_map/ppermute | solution.py:173
  44.8 1.9 %fusion.12 = f32[512,1024]{1,0:T(8,128)S(1)} fusion(bf16[4,1024,1024]{2,1,0:T(8,128)(2,1)} %param.9, bf16[512,256]{1,0:T(8,128)(2,1)S(1)} %copy-done.4, bf16[512,256]{1,0:T(8,128)(2,1)S(1)} %collective-permute-done.5), kind=kOutput, calls=%fused_computation.13 | convolution fusion | flops 537919488 | bytes 3670016 | tf_op jit(solution)/shard_map/dot_general | solution.py:132
  46.8 0.6 add.90
  47.3 4.3 %collective-permute-done.12 = bf16[512,256]{1,0:T(8,128)(2,1)S(1)} collective-permute-done((bf16[512,256]{1,0:T(8,128)(2,1)}, bf16[512,256]{1,0:T(8,128)(2,1)S(1)}, u32[]{:S(2)}, u32[]{:S(2)}) %collective-permute-start.12) | collective-permute-done | bytes 262176 | tf_op jit(solution)/shard_map/ppermute | solution.py:152
  51.7 0.7 fusion.10
  52.4 0.5 add_convert_fusion.refs_0_
  52.9 3.0 %collective-permute-start.13 = (bf16[512,1024]{1,0:T(8,128)(2,1)S(1)}, bf16[512,1024]{1,0:T(8,128)(2,1)S(1)}, u32[]{:S(2)}, u32[]{:S(2)}) collective-permute-start(bf16[512,1024]{1,0:T(8,128)(2,1)S(1)} %add_convert_fusion.refs_0_), channel_id=1, source_target_pairs={{0,96},{16,112},{32,0},{48,16},{64,32},{80,48},{96,64},{112,80},{1... | collective-permute-start | bytes 3145736 | tf_op jit(solution)/shard_map/ppermute | solution.py:144
  55.9 0.0 collective-permute-start.14
  55.9 8.7 %collective-permute-done.9 = bf16[512,512]{1,0:T(8,128)(2,1)S(1)} collective-permute-done((bf16[512,512]{1,0:T(8,128)(2,1)S(1)}, bf16[512,512]{1,0:T(8,128)(2,1)S(1)}, u32[]{:S(2)}, u32[]{:S(2)}) %collective-permute-start.9) | collective-permute-done | bytes 524320 | tf_op jit(solution)/shard_map/ppermute | solution.py:173
  64.6 0.2 add_convert_fusion.1
  64.8 0.1 collective-permute-start.10
  64.9 0.7 fusion.8
  65.7 15.2 %collective-permute-done.10 = bf16[512,512]{1,0:T(8,128)(2,1)S(1)} collective-permute-done((bf16[512,512]{1,0:T(8,128)(2,1)S(1)}, bf16[512,512]{1,0:T(8,128)(2,1)S(1)}, u32[]{:S(2)}, u32[]{:S(2)}) %collective-permute-start.10) | collective-permute-done | bytes 524320 | tf_op jit(solution)/shard_map/ppermute | solution.py:152
  80.9 0.8 collective-permute-done.14.refs_4_
  81.6 0.1 collective-permute-start.17
  81.8 3.3 %collective-permute-start.18 = (bf16[256,1024]{1,0:T(8,128)(2,1)S(1)}, bf16[256,1024]{1,0:T(8,128)(2,1)S(1)}, u32[]{:S(2)}, u32[]{:S(2)}) collective-permute-start(bf16[256,1024]{1,0:T(8,128)(2,1)S(1)} %slice.93), channel_id=1, source_target_pairs={{0,96},{16,112},{32,0},{48,16},{64,32},{80,48},{96,64},{112,80},{1... | collective-permute-start | bytes 1572872 | tf_op jit(solution)/shard_map/ppermute | solution.py:147
  85.1 0.0 collective-permute-start.15
  85.1 10.2 %collective-permute-done.17.refs_2_ = bf16[256,1024]{1,0:T(8,128)(2,1)S(1)} collective-permute-done((bf16[256,1024]{1,0:T(8,128)(2,1)S(1)}, bf16[256,1024]{1,0:T(8,128)(2,1)S(1)}, u32[]{:S(2)}, u32[]{:S(2)}) %collective-permute-start.17) | collective-permute-done | bytes 524320 | tf_op jit(solution)/shard_map/ppermute | solution.py:146
  95.3 0.0 collective-permute-done.18.refs_3_
  95.3 3.7 %collective-permute-done.15 = bf16[512,512]{1,0:T(8,128)(2,1)S(1)} collective-permute-done((bf16[512,512]{1,0:T(8,128)(2,1)S(1)}, bf16[512,512]{1,0:T(8,128)(2,1)S(1)}, u32[]{:S(2)}, u32[]{:S(2)}) %collective-permute-start.15) | collective-permute-done | bytes 524320 | tf_op jit(solution)/shard_map/ppermute | solution.py:152
  99.0 0.3 shard_map.57.mine
  99.3 0.1 collective-permute-start.19
  99.4 0.1 collective-permute-start.16
  99.5 7.1 %collective-permute-done.19.sib = bf16[2048,1024]{1,0:T(8,128)(2,1)S(1)} collective-permute-done((bf16[2048,1024]{1,0:T(8,128)(2,1)S(1)}, bf16[2048,1024]{1,0:T(8,128)(2,1)S(1)}, u32[]{:S(2)}, u32[]{:S(2)}) %collective-permute-start.19) | collective-permute-done | bytes 4194336 | tf_op jit(solution)/shard_map/ppermute | solution.py:184
  106.5 3.3 %shard_map.58 = (f32[512,1024]{1,0:T(8,128)S(1)}, bf16[512,1024]{1,0:T(8,128)(2,1)S(1)}) custom-call(s32[16]{0:T(128)S(1)} %pad_add_fusion.codes, bf16[8,256,256]{2,1,0:T(8,128)(2,1)S(1)} %copy-done, bf16[2048,1024]{1,0:T(8,128)(2,1)S(1)} %shard_map.57.mine, bf16[2048,1024]{1,0:T(8,128)(2,1)S(1)} %collective-permute-done.19.sib), custom_call_target="tpu_custom_call" | custom-call | flops 1048576 | bytes 4096 | tf_op jit(solution)/shard_map/pallas_call | solution.py:97
  109.9 1.7 %collective-permute-start.20 = (bf16[512,1024]{1,0:T(8,128)(2,1)S(1)}, bf16[512,1024]{1,0:T(8,128)(2,1)S(1)}, u32[]{:S(2)}, u32[]{:S(2)}) collective-permute-start(bf16[512,1024]{1,0:T(8,128)(2,1)S(1)} %get-tuple-element.70), channel_id=1, source_target_pairs={{0,128},{16,144},{32,160},{48,176},{64,192},{80,208},{96,224},{112... | collective-permute-start | bytes 3145736 | tf_op jit(solution)/shard_map/ppermute | solution.py:191
  111.6 0.7 fusion.6
  112.3 0.8 add_add_fusion.1
  113.1 2.9 %collective-permute-done.16 = bf16[512,512]{1,0:T(8,128)(2,1)S(1)} collective-permute-done((bf16[512,512]{1,0:T(8,128)(2,1)S(1)}, bf16[512,512]{1,0:T(8,128)(2,1)S(1)}, u32[]{:S(2)}, u32[]{:S(2)}) %collective-permute-start.16) | collective-permute-done | bytes 524320 | tf_op jit(solution)/shard_map/ppermute | solution.py:152
  115.9 0.7 fusion
  116.7 23.4 %collective-permute-done.20 = bf16[512,1024]{1,0:T(8,128)(2,1)S(1)} collective-permute-done((bf16[512,1024]{1,0:T(8,128)(2,1)S(1)}, bf16[512,1024]{1,0:T(8,128)(2,1)S(1)}, u32[]{:S(2)}, u32[]{:S(2)}) %collective-permute-start.20) | collective-permute-done | bytes 1048608 | tf_op jit(solution)/shard_map/ppermute | solution.py:191
  140.1 2.2 %add_add_fusion = f32[512,1024]{1,0:T(8,128)} fusion(f32[512,1024]{1,0:T(8,128)S(1)} %get-tuple-element.69, bf16[512,1024]{1,0:T(8,128)(2,1)S(1)} %collective-permute-done.20, f32[512,1024]{1,0:T(8,128)S(1)} %add_add_fusion.1, f32[512,1024]{1,0:T(8,128)S(1)} %fusion), kind=kLoop, calls=%fused_computation | loop fusion | flops 2097152 | bytes 9437184 | tf_op jit(solution)/shard_map/add | solution.py:198
  (25 shorter events, 0.2 us)
Async XLA Ops:
  0.0 9.0 %copy-start.2 = (bf16[512,1024]{1,0:T(8,128)(2,1)S(1)}, bf16[512,1024]{1,0:T(8,128)(2,1)}, u32[]{:S(2)}) copy-start(bf16[512,1024]{1,0:T(8,128)(2,1)} %param.5) | copy-start | bytes 3145732
  1.2 23.4 %collective-permute-start = (bf16[512,512]{1,0:T(8,128)(2,1)S(1)}, bf16[512,512]{1,0:T(8,128)(2,1)S(1)}, u32[]{:S(2)}, u32[]{:S(2)}) collective-permute-start(bf16[512,512]{1,0:T(8,128)(2,1)S(1)} %slice.74.refs_0_), channel_id=1, source_target_pairs={{0,96},{16,112},{32,0},{48,16},{64,32},{80,48},{96,64},{112,80},{1... | collective-permute-start | bytes 1572872 | tf_op jit(solution)/shard_map/ppermute | solution.py:144
  4.0 19.7 %collective-permute-start.1 = (bf16[512,512]{1,0:T(8,128)(2,1)S(1)}, bf16[512,512]{1,0:T(8,128)(2,1)S(1)}, u32[]{:S(2)}, u32[]{:S(2)}) collective-permute-start(bf16[512,512]{1,0:T(8,128)(2,1)S(1)} %slice.74.refs_0_), channel_id=1, source_target_pairs={{0,32},{16,48},{32,64},{48,80},{64,96},{80,112},{96,0},{112,16},{1... | collective-permute-start | bytes 1572872 | tf_op jit(solution)/shard_map/ppermute | solution.py:143
  5.1 13.0 %collective-permute-start.4 = (bf16[512,256]{1,0:T(8,128)(2,1)S(1)}, bf16[512,256]{1,0:T(8,128)(2,1)S(1)}, u32[]{:S(2)}, u32[]{:S(2)}) collective-permute-start(bf16[512,256]{1,0:T(8,128)(2,1)S(1)} %get-tuple-element.76), channel_id=1, source_target_pairs={{0,1},{1,2},{2,3},{3,4},{4,5},{5,6},{6,7},{7,8},{8,9},{9,10},{10,1... | collective-permute-start | bytes 786440 | tf_op jit(solution)/shard_map/ppermute | solution.py:152
  7.1 16.6 %collective-permute-start.6 = (bf16[512,256]{1,0:T(8,128)(2,1)S(1)}, bf16[512,256]{1,0:T(8,128)(2,1)S(1)}, u32[]{:S(2)}, u32[]{:S(2)}) collective-permute-start(bf16[512,256]{1,0:T(8,128)(2,1)S(1)} %get-tuple-element.75), channel_id=1, source_target_pairs={{0,1},{1,2},{2,3},{3,4},{4,5},{5,6},{6,7},{7,8},{8,9},{9,10},{10,1... | collective-permute-start | bytes 786440 | tf_op jit(solution)/shard_map/ppermute | solution.py:152
  18.1 12.8 %collective-permute-start.5 = (bf16[512,256]{1,0:T(8,128)(2,1)S(1)}, bf16[512,256]{1,0:T(8,128)(2,1)S(1)}, u32[]{:S(2)}, u32[]{:S(2)}) collective-permute-start(bf16[512,256]{1,0:T(8,128)(2,1)S(1)} %collective-permute-done.4), channel_id=1, source_target_pairs={{0,1},{1,2},{2,3},{3,4},{4,5},{5,6},{6,7},{7,8},{8,9},{9,10},{10,1... | collective-permute-start | bytes 786440 | tf_op jit(solution)/shard_map/ppermute | solution.py:152
  23.7 10.1 %collective-permute-start.7 = (bf16[512,256]{1,0:T(8,128)(2,1)S(1)}, bf16[512,256]{1,0:T(8,128)(2,1)S(1)}, u32[]{:S(2)}, u32[]{:S(2)}) collective-permute-start(bf16[512,256]{1,0:T(8,128)(2,1)S(1)} %collective-permute-done.6), channel_id=1, source_target_pairs={{0,1},{1,2},{2,3},{3,4},{4,5},{5,6},{6,7},{7,8},{8,9},{9,10},{10,1... | collective-permute-start | bytes 786440 | tf_op jit(solution)/shard_map/ppermute | solution.py:152
  23.7 10.1 %collective-permute-start.2 = (bf16[256,512]{1,0:T(8,128)(2,1)S(1)}, bf16[256,512]{1,0:T(8,128)(2,1)S(1)}, u32[]{:S(2)}, u32[]{:S(2)}) collective-permute-start(bf16[256,512]{1,0:T(8,128)(2,1)S(1)} %slice.90), channel_id=1, source_target_pairs={{0,32},{16,48},{32,64},{48,80},{64,96},{80,112},{96,0},{112,16},{1... | collective-permute-start | bytes 786440 | tf_op jit(solution)/shard_map/ppermute | solution.py:146
  24.6 9.2 %collective-permute-start.3 = (bf16[256,512]{1,0:T(8,128)(2,1)S(1)}, bf16[256,512]{1,0:T(8,128)(2,1)S(1)}, u32[]{:S(2)}, u32[]{:S(2)}) collective-permute-start(bf16[256,512]{1,0:T(8,128)(2,1)S(1)} %slice.91), channel_id=1, source_target_pairs={{0,96},{16,112},{32,0},{48,16},{64,32},{80,48},{96,64},{112,80},{1... | collective-permute-start | bytes 786440 | tf_op jit(solution)/shard_map/ppermute | solution.py:147
  30.9 3.6 %copy-start.6 = (s32[16,16]{1,0:T(8,128)S(1)}, s32[16,16]{1,0:T(8,128)}, u32[]{:S(2)}) copy-start(s32[16,16]{1,0:T(8,128)} %param.8) | copy-start | bytes 3076
  30.9 3.9 %copy-start.5 = (s32[16,16,3]{1,0,2:T(8,128)S(1)}, s32[16,16,3]{1,0,2:T(8,128)}, u32[]{:S(2)}) copy-start(s32[16,16,3]{1,0,2:T(8,128)} %param.7) | copy-start | bytes 9220
  30.9 7.9 %copy-start = (bf16[8,256,256]{2,1,0:T(8,128)(2,1)S(1)}, bf16[8,256,256]{2,1,0:T(8,128)(2,1)}, u32[]{:S(2)}) copy-start(bf16[8,256,256]{2,1,0:T(8,128)(2,1)} %coup.3) | copy-start | bytes 3145732
  33.8 0.7 copy-start.3
  34.5 4.3 %collective-permute-start.8 = (bf16[2048,512]{1,0:T(8,128)(2,1)S(1)}, bf16[2048,512]{1,0:T(8,128)(2,1)}, u32[]{:S(2)}, u32[]{:S(2)}) collective-permute-start(bf16[2048,512]{1,0:T(8,128)(2,1)S(1)} %shard_map.55.mine), channel_id=1, source_target_pairs={{0,16},{16,0},{32,48},{48,32},{64,80},{80,64},{96,112},{112,96},{1... | collective-permute-start | bytes 6291464 | tf_op jit(solution)/shard_map/ppermute | solution.py:166
  35.1 9.7 %copy-start.4 = (bf16[512,256]{1,0:T(8,128)(2,1)S(1)}, bf16[512,256]{1,0:T(8,128)(2,1)}, u32[]{:S(2)}) copy-start(bf16[512,256]{1,0:T(8,128)(2,1)} %copy-done.3) | copy-start | bytes 786436
  35.1 12.2 %collective-permute-start.11 = (bf16[512,256]{1,0:T(8,128)(2,1)S(1)}, bf16[512,256]{1,0:T(8,128)(2,1)S(1)}, u32[]{:S(2)}, u32[]{:S(2)}) collective-permute-start(bf16[512,256]{1,0:T(8,128)(2,1)S(1)} %collective-permute-done.5), channel_id=1, source_target_pairs={{0,1},{1,2},{2,3},{3,4},{4,5},{5,6},{6,7},{7,8},{8,9},{9,10},{10,1... | collective-permute-start | bytes 786440 | tf_op jit(solution)/shard_map/ppermute | solution.py:152
  35.1 16.5 %collective-permute-start.12 = (bf16[512,256]{1,0:T(8,128)(2,1)}, bf16[512,256]{1,0:T(8,128)(2,1)S(1)}, u32[]{:S(2)}, u32[]{:S(2)}) collective-permute-start(bf16[512,256]{1,0:T(8,128)(2,1)} %copy-done.3), channel_id=1, source_target_pairs={{0,1},{1,2},{2,3},{3,4},{4,5},{5,6},{6,7},{7,8},{8,9},{9,10},{10,1... | collective-permute-start | bytes 786440 | tf_op jit(solution)/shard_map/ppermute | solution.py:152
  38.8 12.9 %slice-start = ((s8[8388608]{0:T(1024)(128)(4,1)}), s8[4194304]{0:T(1024)(128)(4,1)S(1)}, s32[]{:S(2)}) async-start(s8[8388608]{0:T(1024)(128)(4,1)} %bitcast.46), calls=%async_computation | async-start | bytes 8388608
  42.6 4.2 %copy-start.1 = (f32[512,1024]{1,0:T(8,128)S(1)}, f32[512,1024]{1,0:T(8,128)}, u32[]{:S(2)}) copy-start(f32[512,1024]{1,0:T(8,128)} %add.88) | copy-start | bytes 6291460
  42.6 9.1 %slice-start.1 = ((s8[8388608]{0:T(1024)(128)(4,1)}), s8[4194304]{0:T(1024)(128)(4,1)S(1)}, s32[]{:S(2)}) async-start(s8[8388608]{0:T(1024)(128)(4,1)} %bitcast.46), calls=%async_computation.1 | async-start | bytes 8388608
  42.6 22.0 %collective-permute-start.9 = (bf16[512,512]{1,0:T(8,128)(2,1)S(1)}, bf16[512,512]{1,0:T(8,128)(2,1)S(1)}, u32[]{:S(2)}, u32[]{:S(2)}) collective-permute-start(bf16[512,512]{1,0:T(8,128)(2,1)S(1)} %get-tuple-element.48), channel_id=1, source_target_pairs={{0,128},{16,144},{32,160},{48,176},{64,192},{80,208},{96,224},{112... | collective-permute-start | bytes 1572872 | tf_op jit(solution)/shard_map/ppermute | solution.py:173
  52.9 27.9 %collective-permute-start.13 = (bf16[512,1024]{1,0:T(8,128)(2,1)S(1)}, bf16[512,1024]{1,0:T(8,128)(2,1)S(1)}, u32[]{:S(2)}, u32[]{:S(2)}) collective-permute-start(bf16[512,1024]{1,0:T(8,128)(2,1)S(1)} %add_convert_fusion.refs_0_), channel_id=1, source_target_pairs={{0,96},{16,112},{32,0},{48,16},{64,32},{80,48},{96,64},{112,80},{1... | collective-permute-start | bytes 3145736 | tf_op jit(solution)/shard_map/ppermute | solution.py:144
  55.9 25.7 %collective-permute-start.14 = (bf16[512,1024]{1,0:T(8,128)(2,1)S(1)}, bf16[512,1024]{1,0:T(8,128)(2,1)S(1)}, u32[]{:S(2)}, u32[]{:S(2)}) collective-permute-start(bf16[512,1024]{1,0:T(8,128)(2,1)S(1)} %add_convert_fusion.refs_0_), channel_id=1, source_target_pairs={{0,32},{16,48},{32,64},{48,80},{64,96},{80,112},{96,0},{112,16},{1... | collective-permute-start | bytes 3145736 | tf_op jit(solution)/shard_map/ppermute | solution.py:143
  64.8 16.0 %collective-permute-start.10 = (bf16[512,512]{1,0:T(8,128)(2,1)S(1)}, bf16[512,512]{1,0:T(8,128)(2,1)S(1)}, u32[]{:S(2)}, u32[]{:S(2)}) collective-permute-start(bf16[512,512]{1,0:T(8,128)(2,1)S(1)} %add_convert_fusion.1), channel_id=1, source_target_pairs={{0,1},{1,2},{2,3},{3,4},{4,5},{5,6},{6,7},{7,8},{8,9},{9,10},{10,1... | collective-permute-start | bytes 1572872 | tf_op jit(solution)/shard_map/ppermute | solution.py:152
  81.6 13.7 %collective-permute-start.17 = (bf16[256,1024]{1,0:T(8,128)(2,1)S(1)}, bf16[256,1024]{1,0:T(8,128)(2,1)S(1)}, u32[]{:S(2)}, u32[]{:S(2)}) collective-permute-start(bf16[256,1024]{1,0:T(8,128)(2,1)S(1)} %slice.92), channel_id=1, source_target_pairs={{0,32},{16,48},{32,64},{48,80},{64,96},{80,112},{96,0},{112,16},{1... | collective-permute-start | bytes 1572872 | tf_op jit(solution)/shard_map/ppermute | solution.py:146
  81.8 13.5 %collective-permute-start.18 = (bf16[256,1024]{1,0:T(8,128)(2,1)S(1)}, bf16[256,1024]{1,0:T(8,128)(2,1)S(1)}, u32[]{:S(2)}, u32[]{:S(2)}) collective-permute-start(bf16[256,1024]{1,0:T(8,128)(2,1)S(1)} %slice.93), channel_id=1, source_target_pairs={{0,96},{16,112},{32,0},{48,16},{64,32},{80,48},{96,64},{112,80},{1... | collective-permute-start | bytes 1572872 | tf_op jit(solution)/shard_map/ppermute | solution.py:147
  85.1 14.0 %collective-permute-start.15 = (bf16[512,512]{1,0:T(8,128)(2,1)S(1)}, bf16[512,512]{1,0:T(8,128)(2,1)S(1)}, u32[]{:S(2)}, u32[]{:S(2)}) collective-permute-start(bf16[512,512]{1,0:T(8,128)(2,1)S(1)} %collective-permute-done.10), channel_id=1, source_target_pairs={{0,1},{1,2},{2,3},{3,4},{4,5},{5,6},{6,7},{7,8},{8,9},{9,10},{10,1... | collective-permute-start | bytes 1572872 | tf_op jit(solution)/shard_map/ppermute | solution.py:152
  99.3 7.2 %collective-permute-start.19 = (bf16[2048,1024]{1,0:T(8,128)(2,1)S(1)}, bf16[2048,1024]{1,0:T(8,128)(2,1)S(1)}, u32[]{:S(2)}, u32[]{:S(2)}) collective-permute-start(bf16[2048,1024]{1,0:T(8,128)(2,1)S(1)} %shard_map.57.mine), channel_id=1, source_target_pairs={{0,16},{16,0},{32,48},{48,32},{64,80},{80,64},{96,112},{112,96},{1... | collective-permute-start | bytes 12582920 | tf_op jit(solution)/shard_map/ppermute | solution.py:184
  99.4 16.5 %collective-permute-start.16 = (bf16[512,512]{1,0:T(8,128)(2,1)S(1)}, bf16[512,512]{1,0:T(8,128)(2,1)S(1)}, u32[]{:S(2)}, u32[]{:S(2)}) collective-permute-start(bf16[512,512]{1,0:T(8,128)(2,1)S(1)} %collective-permute-done.15), channel_id=1, source_target_pairs={{0,1},{1,2},{2,3},{3,4},{4,5},{5,6},{6,7},{7,8},{8,9},{9,10},{10,1... | collective-permute-start | bytes 1572872 | tf_op jit(solution)/shard_map/ppermute | solution.py:152
  109.9 30.2 %collective-permute-start.20 = (bf16[512,1024]{1,0:T(8,128)(2,1)S(1)}, bf16[512,1024]{1,0:T(8,128)(2,1)S(1)}, u32[]{:S(2)}, u32[]{:S(2)}) collective-permute-start(bf16[512,1024]{1,0:T(8,128)(2,1)S(1)} %get-tuple-element.70), channel_id=1, source_target_pairs={{0,128},{16,144},{32,160},{48,176},{64,192},{80,208},{96,224},{112... | collective-permute-start | bytes 3145736 | tf_op jit(solution)/shard_map/ppermute | solution.py:191
